TPU v7x, 32 devices: a whole 2x2x4 slice. The times are simulated.
32 devices in a mesh: batch: 2 (over x), rows: 16 (over z, y, core).
Axes of the slice: x: 2, y: 2, z: 4, core: 2. Of those that a mesh axis runs over, the one named last changes fastest.
Arguments:
- layer_input: bfloat16 [2, 64, 64, 2048], P('batch', 'rows'), may hold values from -6 to 6
- pre_activation: bfloat16 [2, 64, 64, 2048], P('batch', 'rows'), may hold values from -6 to 6
- cotangent: bfloat16 [2, 64, 64, 2048], P('batch', 'rows'), may hold values from -6 to 6
- weight: bfloat16 [64, 64], replicated, may hold values from -0.75 to 0.75
- spectral: bfloat16 [2304, 64, 128], P('rows'), may hold values from -6 to 6
- slab_ids: int32 [2, 32], P('batch'), may hold values from 0 to 2047, as said below
- extents: int32 [2, 32], P('batch'), may hold values from 1 to 2048, as said below
Outputs:
- grad_input: bfloat16 [2, 64, 64, 2048], P('batch', 'rows')
- grad_spectral: float32 [2304, 64, 128], P('rows')
- grad_weight: float32 [64, 64], replicated
Inputs may be any that keep to these rules, and one draw needn't show every extreme that they name: `slab_ids`: within a sample the 32 slab numbers are distinct and include 0 and 2047; slots 2 k to 2 k + 1 are stored on index k of rows. `extents`: A slot's extent counts its slab's live columns from column 0.
All inputs are finite; a program needn't handle non-finite values.
Results may differ from a plain program's by a relative error of at most 0.0085.
Values may be sent and summed in bfloat16 or wider, within the bound.
No kernel may reach another device: no remote copies, remote signals or barrier semaphores. Data moves between devices by JAX's collectives and lax.ppermute only.
A program may use at most 128 MiB of HBM per device.

v0:
```python
import math

import jax
import jax.numpy as jnp
from jax import lax
from jax.sharding import PartitionSpec as P

PA = 48
SLAB = 2
NR = 4096
MODES = 96


def column_table(column_count, freq_count):
    column_index = jnp.arange(column_count, dtype=jnp.int32)
    freq_index = jnp.arange(freq_count, dtype=jnp.int32)
    phase = column_index[:, None] * freq_index[None, :] % column_count
    angle = phase.astype(jnp.float32) * (2.0 * math.pi / column_count)
    return jnp.concatenate([jnp.cos(angle), -jnp.sin(angle)], axis=1).astype(jnp.bfloat16)


def row_table(positions, row_total, freq_count):
    freq_index = jnp.arange(freq_count, dtype=jnp.int32) - freq_count // 2
    phase = jnp.mod(freq_index[:, None] * positions[None, :], row_total)
    angle = phase.astype(jnp.float32) * (2.0 * math.pi / row_total)
    return jnp.concatenate([jnp.cos(angle), jnp.sin(angle)], axis=0).astype(jnp.bfloat16)


def stored_positions(slab_list, slab_rows):
    offsets = jnp.tile(jnp.arange(slab_rows, dtype=jnp.int32), slab_list.shape[0])
    return jnp.repeat(slab_list, slab_rows) * slab_rows + offsets


def gelu_slope(values):
    return (
        0.5 * (1.0 + lax.erf(values * 0.7071067811865476))
        + values * jnp.exp(-0.5 * values * values) * 0.3989422804014327
    )


def row_combine(row_sums, scale):
    upper = row_sums[0]
    lower = row_sums[1]
    real_part = upper[:, :, 0] + lower[:, :, 1]
    imag_part = upper[:, :, 1] - lower[:, :, 0]
    return (jnp.stack([real_part, imag_part], axis=2) * scale).astype(jnp.bfloat16)


def to_blocks(spectra, half_modes):
    chans = spectra.shape[1]
    shaped = spectra.reshape(half_modes, 2, chans, 2, half_modes, 2)
    return shaped.transpose(2, 3, 1, 5, 0, 4).reshape(chans, 2, 2, 2, half_modes * half_modes)


def from_blocks(blocked, half_modes):
    chans = blocked.shape[0]
    shaped = blocked.reshape(chans, 2, 2, 2, half_modes, half_modes)
    return shaped.transpose(4, 2, 0, 1, 5, 3).reshape(2 * half_modes, chans, 2, 2 * half_modes)


def factor_pair(owned, chans):
    input_modes = owned[:chans]
    grad_out = owned[chans:]
    factor_left = input_modes.transpose(4, 0, 1, 2, 3).reshape(owned.shape[4], chans, 8)
    real_out = grad_out[:, 0]
    imag_out = grad_out[:, 1]
    first_half = jnp.stack([real_out, imag_out], axis=1)
    second_half = jnp.stack([imag_out, -real_out], axis=1)
    stacked = jnp.concatenate([first_half, second_half], axis=0)
    factor_right = stacked.transpose(4, 0, 1, 2, 3).reshape(owned.shape[4], 2 * chans, 8)
    return (factor_left, factor_right)


def modes_to_channels(grad_modes):
    blocks = grad_modes.shape[0]
    chans = grad_modes.shape[1]
    return grad_modes.reshape(blocks, chans, 2, 2, 2).transpose(1, 2, 3, 4, 0)


def row_adjoint(rowtab, grad_grid, scale):
    real_part = grad_grid[:, :, 0]
    imag_part = grad_grid[:, :, 1]
    upper = jnp.stack([real_part, imag_part], axis=2)
    lower = jnp.stack([-imag_part, real_part], axis=2)
    joined = jnp.concatenate([upper, lower], axis=0)
    summed = jnp.dot(
        rowtab.T, joined.reshape(joined.shape[0], -1), preferred_element_type=jnp.float32
    )
    return (summed * scale).astype(jnp.bfloat16)


def shards(layer_input, pre_activation, cotangent, weight, spectral, slab_ids, extents):
    batch_devices = lax.axis_size("batch")
    local_rows = layer_input.shape[1]
    channels = layer_input.shape[2]
    column_count = layer_input.shape[3]
    slab_list = slab_ids[0]
    active = slab_list.shape[0]
    slots = local_rows // SLAB
    scale = 1.0 / math.sqrt(NR * column_count)
    position = lax.axis_index("rows")
    own_extents = lax.dynamic_slice_in_dim(extents[0], position * slots, slots)
    column_index = jnp.arange(column_count, dtype=jnp.int32)
    alive = column_index[None, :] < jnp.repeat(own_extents, SLAB)[:, None]
    mask_half = alive.astype(jnp.bfloat16)
    mask_full = alive.astype(jnp.float32)
    masked_in = layer_input[0] * mask_half[:, None, :]
    grad_pre = (
        cotangent[0].astype(jnp.float32)
        * mask_full[:, None, :]
        * gelu_slope(pre_activation[0].astype(jnp.float32))
    ).astype(jnp.bfloat16)
    coltab = column_table(column_count, MODES)
    stacked = jnp.concatenate([masked_in, grad_pre], axis=1)
    colspec = jnp.dot(stacked.reshape(-1, column_count), coltab, preferred_element_type=jnp.float32)
    colspec = colspec.reshape(local_rows, 2 * channels, 2 * MODES).astype(jnp.bfloat16)
    gathered_rows = lax.all_to_all(colspec, "rows", split_axis=1, concat_axis=0, tiled=True)
    all_rows = gathered_rows.shape[0]
    owned_channels = gathered_rows.shape[1]
    rowtab = row_table(stored_positions(slab_list, SLAB), NR, MODES)
    row_sums = jnp.dot(
        rowtab, gathered_rows.reshape(all_rows, -1), preferred_element_type=jnp.float32
    )
    spectra = row_combine(row_sums.reshape(2, MODES, owned_channels, 2, MODES), scale)
    owned = lax.all_to_all(to_blocks(spectra, PA), "rows", split_axis=4, concat_axis=0, tiled=True)
    factor_left, factor_right = factor_pair(owned, channels)
    grad_modes = jnp.einsum(
        "bix,bxk->bik", spectral, factor_right, preferred_element_type=jnp.float32
    ).astype(jnp.bfloat16)
    own_grad = jnp.einsum(
        "bik,bxk->bix", factor_left, factor_right, preferred_element_type=jnp.float32
    )
    grad_spectral = lax.psum(own_grad, "batch")
    returned = lax.all_to_all(
        modes_to_channels(grad_modes), "rows", split_axis=0, concat_axis=4, tiled=True
    )
    rowback = row_adjoint(rowtab, from_blocks(returned, PA), scale)
    rowback = rowback.reshape(all_rows, -1, 2 * MODES)
    local_back = lax.all_to_all(rowback, "rows", split_axis=0, concat_axis=1, tiled=True)
    spatial = jnp.dot(
        local_back.reshape(-1, 2 * MODES), coltab.T, preferred_element_type=jnp.float32
    )
    spatial = spatial.reshape(local_rows, channels, column_count)
    row_weight = jnp.broadcast_to(weight, (local_rows, channels, channels))
    direct = jnp.einsum("rio,roc->ric", row_weight, grad_pre, preferred_element_type=jnp.float32)
    grad_input = ((spatial + direct) * mask_full[:, None, :]).astype(jnp.bfloat16)[None]
    row_partial = jnp.einsum(
        "ric,roc->rio", masked_in, grad_pre, preferred_element_type=jnp.float32
    )
    local_weight = jnp.sum(row_partial, axis=0)
    grad_weight = lax.psum(local_weight, ("batch", "rows"))
    grad_weight = grad_weight * (1.0 / math.sqrt(batch_devices * active * SLAB * column_count))
    return (grad_input, grad_spectral, grad_weight)


def solution(mesh):
    return jax.shard_map(
        shards,
        mesh=mesh,
        in_specs=(
            P("batch", "rows", None, None),
            P("batch", "rows", None, None),
            P("batch", "rows", None, None),
            P(),
            P("rows", None, None),
            P("batch", None),
            P("batch", None),
        ),
        out_specs=(P("batch", "rows", None, None), P("rows", None, None), P()),
        check_vma=False,
    )
```

profile of v0, /device:TPU:0, one launch (start us, length us, event | category | flops | bytes accessed | tf_op | source)
XLA Modules:
  0.0 304.3 jit_solution(13098841507869636662)
XLA Ops:
  7.2 3.9 %negate_convert_fusion = (bf16[2048,96]{0,1:T(8,128)(2,1)}, bf16[2048,96]{0,1:T(8,128)(2,1)}) fusion(), kind=kLoop, calls=%fused_computation.40 | loop fusion | flops 3342336 | bytes 786432 | tf_op jit(solution)/shard_map/convert.3
  15.1 1.6 fusion.17
  16.6 1.8 copy.52
  18.4 7.5 %all-to-all-start = ((bf16[4,128,192]{2,0,1:T(4,128)(2,1)}), bf16[4,128,192]{2,0,1:T(4,128)(2,1)}, u32[]{:S(2)}, u32[]{:S(2)}) async-start(bf16[4,128,192]{2,0,1:T(4,128)(2,1)} %copy.52), calls=%async_computation | async-start | bytes 524288 | tf_op jit(solution)/shard_map/all_to_all | solution.py:117
  26.6 9.3 %all-to-all-done = bf16[4,128,192]{2,0,1:T(4,128)(2,1)} async-done(((bf16[4,128,192]{2,0,1:T(4,128)(2,1)}), bf16[4,128,192]{2,0,1:T(4,128)(2,1)}, u32[]{:S(2)}, u32[]{:S(2)}) %all-to-all-start) | async-done | bytes 196640 | tf_op jit(solution)/shard_map/all_to_all | solution.py:117
  37.7 1.9 reshape.119
  41.9 3.0 squeeze.7
  44.8 3.1 %fusion.45 = (f32[96,8,1,96]{3,2,1,0:T(1,128)}, f32[96,8,1,96]{3,2,1,0:T(1,128)}) fusion(f32[96,8,2,96]{3,2,1,0:T(2,128)} %squeeze.7), kind=kLoop, calls=%fused_computation.82 | loop fusion | bytes 1179648 | tf_op jit(solution)/shard_map/slice | solution.py:44
  47.9 4.2 %copy.79 = f32[96,8,1,96]{1,3,0,2:T(8,128)} copy(f32[96,8,1,96]{3,2,1,0:T(1,128)} %get-tuple-element.10) | data formatting | bytes 589824
  52.1 3.0 squeeze.8
  55.1 2.9 fusion.44
  58.0 4.2 %copy.80 = f32[96,8,1,96]{1,3,0,2:T(8,128)} copy(f32[96,8,1,96]{3,2,1,0:T(1,128)} %get-tuple-element.8) | data formatting | bytes 589824
  62.2 6.9 %sub.9 = f32[96,8,1,96]{1,3,0,2:T(8,128)} subtract(f32[96,8,1,96]{1,3,0,2:T(8,128)} %copy.79, f32[96,8,1,96]{1,3,0,2:T(8,128)} %copy.80) | non-fusion elementwise | flops 73728 | bytes 884736 | tf_op jit(solution)/shard_map/sub | solution.py:45
  69.1 6.2 %copy.60 = f32[48,2,8,1,48,2]{4,2,5,3,1,0:T(8,128)} copy(f32[48,2,8,1,48,2]{2,5,4,1,0,3:T(2,128)} %bitcast.84) | data formatting | bytes 589824 | tf_op jit(solution)/shard_map/stack | solution.py:46
  75.3 4.2 %copy.77 = f32[96,8,1,96]{1,3,0,2:T(8,128)} copy(f32[96,8,1,96]{3,2,1,0:T(1,128)} %get-tuple-element.9) | data formatting | bytes 589824
  79.5 4.2 %copy.78 = f32[96,8,1,96]{1,3,0,2:T(8,128)} copy(f32[96,8,1,96]{3,2,1,0:T(1,128)} %get-tuple-element.7) | data formatting | bytes 589824
  83.7 6.9 %add.60 = f32[96,8,1,96]{1,3,0,2:T(8,128)} add(f32[96,8,1,96]{1,3,0,2:T(8,128)} %copy.77, f32[96,8,1,96]{1,3,0,2:T(8,128)} %copy.78) | non-fusion elementwise | flops 73728 | bytes 884736 | tf_op jit(solution)/shard_map/add | solution.py:44
  90.6 6.2 %copy.59 = f32[48,2,8,1,48,2]{4,2,5,3,1,0:T(8,128)} copy(f32[48,2,8,1,48,2]{2,5,4,1,0,3:T(2,128)} %bitcast.85) | data formatting | bytes 589824 | tf_op jit(solution)/shard_map/stack | solution.py:46
  96.8 2.5 fusion.24
  99.3 9.3 %copy.74 = bf16[8,2,2,2,48,48]{0,3,2,1,5,4:T(2,128)(2,1)} copy(bf16[8,2,2,2,48,48]{5,0,3,1,2,4:T(8,128)(2,1)} %fusion.24) | data formatting | bytes 589824 | tf_op jit(solution)/shard_map/reshape | solution.py:52
  108.6 7.0 %reshape.131 = bf16[16,2,4608]{2,1,0:T(2,128)(2,1)} reshape(bf16[2304,2,2,2,8]{4,3,2,1,0:T(2,128)(2,1)} %bitcast.87) | data formatting | bytes 589824
  115.6 14.7 %all_to_all.60 = bf16[16,2,4608]{2,1,0:T(2,128)(2,1)} all-to-all(bf16[16,2,4608]{2,1,0:T(2,128)(2,1)} %reshape.131), channel_id=1, replica_groups=mesh['batch'=2,'rows'=16] {'rows'}, dimensions={0} | all-to-all | bytes 589824 | tf_op jit(solution)/shard_map/all_to_all | solution.py:125
  130.3 7.4 %reshape.132 = bf16[2304,2,2,2,8]{4,3,2,1,0:T(2,128)(2,1)} reshape(bf16[16,2,4608]{2,1,0:T(2,128)(2,1)} %all_to_all.60) | data formatting | bytes 589824
  137.7 12.1 %copy.75 = bf16[8,2,2,2,16,144]{5,4,0,3,2,1:T(8,128)(2,1)} copy(bf16[8,2,2,2,16,144]{0,3,2,1,5,4:T(2,128)(2,1)} %bitcast.88) | data formatting | bytes 589824 | tf_op jit(solution)/shard_map/all_to_all | solution.py:125
  149.8 1.8 fusion.46
  152.5 1.9 copy.65
  154.5 1.7 copy.85
  156.2 1.9 copy.73
  158.1 4.0 %fusion.48 = f32[144,64,128]{2,1,0:T(8,128)} fusion(bf16[144,64,8]{1,2,0:T(8,128)(2,1)} %bitcast.97, bf16[144,128,8]{1,2,0:T(8,128)(2,1)} %bitcast.91), kind=kOutput, calls=%fused_computation.85 | convolution fusion | flops 18874368 | bytes 5160960 | tf_op jit(solution)/shard_map/bik,bxk->bix/dot_general | solution.py:130
  162.1 3.0 convolution_convert_fusion
  165.1 2.0 copy.66
  167.1 4.2 %all-to-all-start.2 = ((bf16[64,2,2,2,144]{4,3,2,1,0:T(2,128)(2,1)}), bf16[64,2,2,2,144]{4,3,2,1,0:T(2,128)(2,1)}, u32[]{:S(2)}, u32[]{:S(2)}) async-start(bf16[64,2,2,2,144]{4,3,2,1,0:T(2,128)(2,1)} %bitcast.98), calls=%async_computation.2 | async-start | bytes 524288 | tf_op jit(solution)/shard_map/all_to_all | solution.py:134
  171.3 1.6 convolution_bitcast_fusion.1
  173.0 42.4 %psum.15 = f32[64,64]{1,0:T(8,128)} all-reduce(f32[64,64]{1,0:T(8,128)S(1)} %convolution_bitcast_fusion.1), channel_id=1, replica_groups=mesh['batch'=2,'rows'=16] {'batch','rows'}, use_global_device_ids=true, to_apply=%region_1.2 | all-reduce | flops 4096 | bytes 32768 | tf_op jit(solution)/shard_map/psum | solution.py:151
  215.4 1.8 copy.67
  217.2 2.1 reshape.123
  219.3 13.9 %copy.69 = bf16[48,2,4,2,48,2]{2,5,4,3,1,0:T(2,128)(2,1)} copy(bf16[48,2,4,2,48,2]{4,0,5,1,3,2:T(8,128)(2,1)} %bitcast.89) | data formatting | bytes 294912 | tf_op jit(solution)/shard_map/transpose | solution.py:58
  233.2 8.4 %copy.68 = bf16[48,2,4,2,48,2]{5,4,3,2,1,0:T(8,128)(2,1)} copy(bf16[48,2,4,2,48,2]{4,0,5,1,3,2:T(8,128)(2,1)} %bitcast.90) | data formatting | bytes 294912 | tf_op jit(solution)/shard_map/transpose | solution.py:58
  241.7 2.9 slice_negate_fusion
  244.5 3.1 %pad_maximum_fusion = bf16[96,4,2,96]{1,3,2,0:T(8,128)(2,1)} fusion(bf16[96,4,1,96]{1,3,2,0:T(8,128)(2,1)S(1)} %get-tuple-element.4, bf16[96,4,1,96]{1,3,2,0:T(8,128)(2,1)S(1)} %get-tuple-element.3), kind=kLoop, calls=%fused_computation | loop fusion | flops 73728 | bytes 294912 | tf_op jit(solution)/shard_map/stack | solution.py:84
  247.6 4.9 %copy.70 = bf16[96,4,2,96]{3,2,1,0:T(2,128)(2,1)} copy(bf16[96,4,2,96]{1,3,2,0:T(8,128)(2,1)} %pad_maximum_fusion) | data formatting | bytes 294912 | tf_op jit(solution)/shard_map/stack | solution.py:84
  253.7 17.1 %concatenate.27 = bf16[96,768]{1,0:T(8,128)(2,1)} reshape(bf16[48,2,4,2,48,2]{5,4,3,2,1,0:T(8,128)(2,1)} %copy.68) | data formatting | bytes 294912 | tf_op jit(solution)/shard_map/concatenate | solution.py:85
  270.7 1.8 fusion.20
  272.5 1.7 reshape.125
  274.2 5.3 %all-to-all-start.3 = ((bf16[64,4,192]{2,1,0:T(4,128)(2,1)}), bf16[64,4,192]{2,1,0:T(4,128)(2,1)S(1)}, u32[]{:S(2)}, u32[]{:S(2)}) async-start(bf16[64,4,192]{2,1,0:T(4,128)(2,1)} %reshape.125), calls=%async_computation.3 | async-start | bytes 262144 | tf_op jit(solution)/shard_map/all_to_all | solution.py:139
  281.0 6.5 %all-to-all-done.3 = bf16[64,4,192]{2,1,0:T(4,128)(2,1)S(1)} async-done(((bf16[64,4,192]{2,1,0:T(4,128)(2,1)}), bf16[64,4,192]{2,1,0:T(4,128)(2,1)S(1)}, u32[]{:S(2)}, u32[]{:S(2)}) %all-to-all-start.3) | async-done | bytes 98336 | tf_op jit(solution)/shard_map/all_to_all | solution.py:139
  289.2 1.5 fusion.28
  292.2 5.2 %copy.90 = f32[144,64,128]{2,1,0:T(8,128)} copy(f32[144,64,128]{2,1,0:T(8,128)} %all-reduce.2.cloned.1.call-done) | data formatting | bytes 9437184
  (51 shorter events, 15.2 us)
Async XLA Ops:
  7.2 154.9 %copy-start = (bf16[144,64,128]{2,1,0:T(8,128)(2,1)S(1)}, bf16[144,64,128]{2,1,0:T(8,128)(2,1)}, u32[]{:S(2)}) copy-start(bf16[144,64,128]{2,1,0:T(8,128)(2,1)} %param.11) | copy-start | bytes 7077892
  11.9 1.6 copy-start.4
  11.9 1.9 copy-start.5
  12.0 2.9 copy-start.6
  13.5 1.4 copy-start.1
  13.5 1.4 copy-start.2
  13.5 1.6 copy-start.3
  15.1 11.1 %copy-start.11 = (s32[1,32]{1,0:T(1,128)S(1)}, s32[1,32]{1,0:T(1,128)}, u32[]{:S(2)}) copy-start(s32[1,32]{1,0:T(1,128)} %param.12) | copy-start | bytes 388
  18.4 17.5 %all-to-all-start = ((bf16[4,128,192]{2,0,1:T(4,128)(2,1)}), bf16[4,128,192]{2,0,1:T(4,128)(2,1)}, u32[]{:S(2)}, u32[]{:S(2)}) async-start(bf16[4,128,192]{2,0,1:T(4,128)(2,1)} %copy.52), calls=%async_computation | async-start | bytes 524288 | tf_op jit(solution)/shard_map/all_to_all | solution.py:117
  25.9 266.3 %all-reduce.2.cloned.1.call-start = ((), (), s32[]{:S(2)}) async-start(), calls=%async_computation.4 | async-start | bytes 9437184 | tf_op jit(solution)/shard_map/psum | solution.py:133
  26.6 15.2 %copy-start.8 = (bf16[96,64]{1,0:T(8,128)(2,1)}, bf16[96,64]{1,0:T(8,128)(2,1)S(1)}, u32[]{:S(2)}) copy-start(bf16[96,64]{1,0:T(8,128)(2,1)S(1)} %get-tuple-element.15) | copy-start | bytes 36868
  26.6 15.2 %copy-start.9 = (bf16[96,64]{1,0:T(8,128)(2,1)}, bf16[96,64]{1,0:T(8,128)(2,1)S(1)}, u32[]{:S(2)}) copy-start(bf16[96,64]{1,0:T(8,128)(2,1)S(1)} %get-tuple-element.16) | copy-start | bytes 36868
  167.1 48.3 %all-to-all-start.2 = ((bf16[64,2,2,2,144]{4,3,2,1,0:T(2,128)(2,1)}), bf16[64,2,2,2,144]{4,3,2,1,0:T(2,128)(2,1)}, u32[]{:S(2)}, u32[]{:S(2)}) async-start(bf16[64,2,2,2,144]{4,3,2,1,0:T(2,128)(2,1)} %bitcast.98), calls=%async_computation.2 | async-start | bytes 524288 | tf_op jit(solution)/shard_map/all_to_all | solution.py:134
  272.5 18.2 %copy-start.10 = (bf16[64,64]{1,0:T(8,128)(2,1)S(1)}, bf16[64,64]{1,0:T(8,128)(2,1)}, u32[]{:S(2)}) copy-start(bf16[64,64]{1,0:T(8,128)(2,1)} %param.10) | copy-start | bytes 24580
  274.2 13.2 %all-to-all-start.3 = ((bf16[64,4,192]{2,1,0:T(4,128)(2,1)}), bf16[64,4,192]{2,1,0:T(4,128)(2,1)S(1)}, u32[]{:S(2)}, u32[]{:S(2)}) async-start(bf16[64,4,192]{2,1,0:T(4,128)(2,1)} %reshape.125), calls=%async_computation.3 | async-start | bytes 262144 | tf_op jit(solution)/shard_map/all_to_all | solution.py:139
  289.2 1.6 copy-start.7
Sparse Core Ops, SparseCore 0:
  162.2 119.0 all-reduce.1
where the time goes:
time: 309 us; the launch traced here: 304 us
  local copies, waits for them, and re-layouts  152 us (49%)
  blocking collectives  57.2 us (19%)
  other arithmetic  31.5 us (10%)
  starting transfers between devices  17.2 us (6%)
  matrix products  16.2 us (5%)
  waiting for transfers between devices  15.9 us (5%)
  between operations  14.3 us (5%)
    psum x1, blocking collectives, shards(): grad_weight = lax.psum(local_weight, ('batch', 'rows'))  42.4 us
    unnamed x31, local copies, waits for them, and re-layouts  36.7 us
    transpose x2, local copies, waits for them, and re-layouts, from_blocks(): shaped.transpose(4, 2, 0, 1, 5, 3)  22.3 us
    concatenate x2, local copies, waits for them, and re-layouts, row_adjoint(): joined = jnp.concatenate([upper, lower], axis=0)  18.2 us
    all_to_all x1, blocking collectives, shards(): lax.all_to_all(to_blocks(spectra, PA), 'rows', split_axis=4, concat_axis=...  14.7 us
    another operation x2, local copies, waits for them, and re-layouts, row_combine(): jnp.stack([real_part, imag_part], axis=2) * scale  12.3 us
    all_to_all x1, local copies, waits for them, and re-layouts, shards(): lax.all_to_all(to_blocks(spectra, PA), 'rows', split_axis=4, concat_axis=...  12.1 us
    all_to_all x1, waiting for transfers between devices, shards(): lax.all_to_all(colspec, 'rows', split_axis=1, concat_axis=0, tiled=True)  9.32 us
  transfers between devices with their start and end apart: 4, of which 2 were waited for; matrix products, arithmetic and copies ran while one was open for 24% of the time, Pallas kernels for 0%

commit v1 on v0

v1 whole, which is shorter than its diff:
```python
import functools
import math

import jax
import jax.numpy as jnp
import numpy as np
from jax import lax
from jax.experimental import pallas as pl
from jax.experimental.pallas import tpu as pltpu
from jax.sharding import PartitionSpec as P

PA = 48
SLAB = 2
NR = 4096
MODES = 96
F32 = jnp.float32
BF16 = jnp.bfloat16
VMEM_LIMIT = 56 * 1024 * 1024


class Plan:
    def __init__(self, ranks, local_rows, channels, columns, held):
        self.ranks = ranks
        self.local_rows = local_rows
        self.channels = channels
        self.columns = columns
        self.held = held
        self.pairs = -(-PA // ranks)
        first = [(held * k) // PA for k in range(ranks)]
        last = [(held * (k + 1) - 1) // PA for k in range(ranks)]
        self.first = np.array(first, np.int32)
        self.steps = max(b - a for a, b in zip(first, last)) + 1
        self.exact = held == self.steps * PA and self.pairs * ranks == PA
        self.both = 2 * channels
        self.half = self.pairs * self.both
        self.group = 2 * local_rows
        self.share = channels // ranks
        self.scale = 1.0 / math.sqrt(NR * columns)

    def column_table(self):
        pair, part, odd, owner = np.meshgrid(
            np.arange(self.pairs),
            np.arange(2),
            np.arange(2),
            np.arange(self.ranks),
            indexing="ij",
        )
        freq = 2 * (self.pairs * owner + pair) + odd
        freq, part = freq.reshape(-1, 1), part.reshape(-1, 1)
        phase = (freq * np.arange(self.columns)[None, :]) % self.columns
        angle = 2.0 * math.pi * phase / self.columns
        table = np.where(part == 0, np.cos(angle), -np.sin(angle))
        return np.where(freq < MODES, table, 0.0).astype(np.float32).astype(jnp.bfloat16)

    def spread(self):
        out = np.zeros((self.ranks * self.group, self.group * self.ranks), np.float32)
        for owner in range(self.ranks):
            for e in range(self.group):
                out[owner * self.group + e, e * self.ranks + owner] = 1.0
        return out.astype(jnp.bfloat16)

    def gather_back(self):
        return self.spread().T

    def share_out(self):
        out = np.zeros((self.ranks * self.group, self.channels), np.float32)
        for i in range(self.channels):
            out[(i // self.share) * self.group + i % self.share, i] = 1.0
        return out.astype(jnp.bfloat16)

    def share_in(self):
        out = np.zeros((self.channels, self.ranks * 8), np.float32)
        for i in range(self.channels):
            base = (i // self.share) * 8 + i % self.share
            out[i, base] = 1.0
            out[i, base + self.share] = 1.0
        return out.astype(jnp.bfloat16)


def turn_table(freq, mode_part, mode_odd, positions, row_part, row_odd, mode_major):
    turn = lambda a, b: (a[:, None], b[None, :]) if mode_major else (a[None, :], b[:, None])
    f, pos = turn(jnp.asarray(freq), positions)
    mp, rp = turn(jnp.asarray(mode_part), jnp.asarray(row_part))
    mo, ro = turn(jnp.asarray(mode_odd), jnp.asarray(row_odd))
    phase = jnp.mod(f * pos + (mp - rp) * (NR // 4), NR)
    value = jnp.cos(phase.astype(F32) * (2.0 * math.pi / NR))
    return jnp.where(mo == ro, value, 0.0).astype(BF16)


def turn_tables(plan, slab_list):
    rows = plan.ranks * plan.local_rows
    row_index = np.arange(rows)
    positions = jnp.repeat(slab_list, SLAB) * SLAB + jnp.asarray(row_index % SLAB, jnp.int32)

    def modes(order):
        k, step, part, odd, low = np.meshgrid(
            *(np.arange(n) for n in (plan.ranks, plan.steps, 2, 2, 2)), indexing="ij"
        )
        freq = 2 * (plan.first[k] + step) + low - MODES // 2
        return [x.transpose(order).reshape(-1).astype(np.int32) for x in (freq, part, odd)]

    def rows_side(shape_order):
        odd, row, part = np.meshgrid(np.arange(2), row_index, np.arange(2), indexing="ij")
        odd, part = (x.transpose(shape_order).reshape(-1).astype(np.int32) for x in (odd, part))
        spread = jnp.broadcast_to(positions[None, :, None], (2, rows, 2))
        return spread.transpose(shape_order).reshape(-1), part, odd

    forward = turn_table(*modes((0, 1, 2, 3, 4)), *rows_side((0, 1, 2)), True)
    backward = turn_table(*modes((1, 0, 2, 3, 4)), *rows_side((2, 1, 0)), False)
    return forward, backward


def gelu_slope(values):
    return (
        0.5 * (1.0 + lax.erf(values * 0.7071067811865476))
        + values * jnp.exp(-0.5 * values * values) * 0.3989422804014327
    )


NT = (((1,), (1,)), ((), ()))
TN = (((0,), (0,)), ((), ()))


def column_kernel(
    plan, ext_ref, x_ref, pre_ref, cot_ref, tab_ref, spread_ref, share_ref,
    gp_ref, out_ref, v_ref, stage_ref, gw_ref,
):
    row = pl.program_id(0)
    chans, ranks = plan.channels, plan.ranks
    slots = plan.local_rows // SLAB
    extent = ext_ref[0, lax.axis_index("rows") * slots + row // SLAB]
    step = 256
    for start in range(0, plan.columns, step):
        cols = slice(start, start + step)
        live = lax.broadcasted_iota(jnp.int32, (chans, step), 1) + start < extent
        kept = jnp.where(live, x_ref[0, 0, :, cols].astype(F32), 0.0).astype(BF16)
        slope = gelu_slope(pre_ref[0, 0, :, cols].astype(F32))
        grad = jnp.where(live, cot_ref[0, 0, :, cols].astype(F32) * slope, 0.0).astype(BF16)
        v_ref[:chans, cols] = kept
        v_ref[chans:, cols] = grad
        gp_ref[0, :, cols] = grad
    spec = lax.dot_general(tab_ref[...], v_ref[...], NT, preferred_element_type=F32).astype(BF16)
    weight = lax.dot_general(v_ref[:chans], v_ref[chans:], NT, preferred_element_type=F32)
    for pair in range(plan.pairs):
        for part in range(2):
            for odd in range(2):
                base = ((pair * 2 + part) * 2 + odd) * ranks
                lane = (odd * plan.pairs + pair) * plan.both
                stage_ref[row, part, :, lane : lane + plan.both] = spec[base : base + ranks]

    @pl.when(row == 0)
    def _():
        gw_ref[...] = weight

    @pl.when(row > 0)
    def _():
        gw_ref[...] += weight

    @pl.when(row == plan.local_rows - 1)
    def _():
        wide = 2 * plan.half
        staged = stage_ref[...].reshape(plan.group * ranks, wide)
        out_ref[:, :wide] = jnp.dot(
            spread_ref[...], staged, preferred_element_type=F32
        ).astype(BF16)
        total = gw_ref[...]
        high = total.astype(BF16)
        low = (total - high.astype(F32)).astype(BF16)
        split = jnp.concatenate([high, low], axis=1)
        out_ref[:, wide:] = jnp.dot(
            share_ref[...], split, preferred_element_type=F32
        ).astype(BF16)


def row_kernel(plan, turn_ref, in_ref, out_ref, share_ref):
    half = plan.half
    stacked = jnp.concatenate([in_ref[:, :half], in_ref[:, half : 2 * half]], axis=0)
    sums = jnp.dot(turn_ref[...], stacked, preferred_element_type=F32)
    out_ref[...] = (sums * plan.scale).astype(BF16)
    pieces = in_ref[:, 2 * half :].astype(F32).reshape(plan.ranks, plan.group, plan.both)
    summed = jnp.sum(pieces, axis=0)
    share_ref[...] = summed + pltpu.roll(summed, plan.channels, axis=1)


def out_pair(tile, chans):
    lane = lax.broadcasted_iota(jnp.int32, tile.shape, 1)
    row = lax.broadcasted_iota(jnp.int32, tile.shape, 0)
    across = pltpu.roll(tile, chans, axis=1)
    other = pltpu.roll(tile, 4, axis=0)
    return jnp.where(lane < chans, across, jnp.where(row < 4, other, -other))


def where_held(plan, owner, step, pair, offset):
    place = step * PA + plan.pairs * owner + pair - offset
    ok = (place >= 0) & (place < plan.held) & (plan.pairs * owner + pair < PA)
    return jnp.clip(place, 0, plan.held - 1), ok


def mode_offset(plan):
    k = lax.axis_index("rows")
    return lax.rem(k * plan.held, PA)


def mix_kernel(plan, owners, samples, *refs):
    share_refs, (in_ref, spec_ref, out_ref) = refs[:samples], refs[samples:]
    chans = plan.channels
    total = share_refs[0][...]
    for ref in share_refs[1:]:
        total = total + ref[...]
    total = total[:8, :chans]
    high = total.astype(BF16).astype(F32)
    low = pltpu.roll(total - high, plan.share, axis=0)
    row = lax.broadcasted_iota(jnp.int32, total.shape, 0)
    zero = jnp.zeros_like(total)
    shared = jnp.where(row < plan.share, high, jnp.where(row < 2 * plan.share, low, zero))

    def body(local, carry):
        owner = pl.program_id(0) * owners + local
        pieces = []
        for step in range(plan.steps):
            for pair in range(plan.pairs):
                start = pl.multiple_of(local * (8 * plan.steps) + 8 * step, 8)
                tile = in_ref[pl.ds(start, 8), pair * plan.both : (pair + 1) * plan.both]
                left = out_pair(tile.astype(F32), chans).astype(BF16)
                if plan.exact:
                    right = spec_ref[step, local * plan.pairs + pair]
                else:
                    place, ok = where_held(plan, owner, step, pair, mode_offset(plan))
                    right = spec_ref[0, place]
                piece = lax.dot_general(left, right, NT, preferred_element_type=F32)
                if not plan.exact:
                    piece = jnp.where(ok, piece, 0.0)
                pieces.append(piece)
        if len(pieces) % 2 == 0:
            pieces.append(jnp.zeros_like(shared))
        pieces.append(shared)
        joined = jnp.concatenate(pieces[:-2] + [pieces[-2], pieces[-1]], axis=1)
        out_ref[pl.ds(pl.multiple_of(local * 8, 8), 8), :] = joined.astype(BF16)
        return carry

    lax.fori_loop(0, owners, body, 0)


def outer_kernel(plan, owners, samples, *refs):
    in_refs, out_ref = refs[:samples], refs[samples]
    chans = plan.channels
    swap = lax.axis_index("batch") != 0

    def body(local, carry):
        owner = pl.program_id(0) * owners + local
        for step in range(plan.steps):
            for pair in range(plan.pairs):
                start = pl.multiple_of(local * (8 * plan.steps) + 8 * step, 8)
                cols = slice(pair * plan.both, (pair + 1) * plan.both)
                tiles = [ref[pl.ds(start, 8), cols].astype(F32) for ref in in_refs]
                if samples == 2:
                    tiles = [
                        jnp.where(swap, tiles[1], tiles[0]),
                        jnp.where(swap, tiles[0], tiles[1]),
                    ]
                left = jnp.concatenate([t[:, :chans] for t in tiles], axis=0).astype(BF16)
                right = jnp.concatenate([out_pair(t, chans) for t in tiles], axis=0).astype(BF16)
                value = lax.dot_general(left, right, TN, preferred_element_type=F32)
                if plan.exact:
                    out_ref[step, local * plan.pairs + pair] = value
                else:
                    place, ok = where_held(plan, owner, step, pair, mode_offset(plan))

                    @pl.when(ok)
                    def _():
                        out_ref[0, place] = value
        return carry

    lax.fori_loop(0, owners, body, 0)


def adjoint_kernel(plan, weight_scale, turn_ref, in_ref, share_ref, out_ref, gw_ref):
    chans = plan.channels
    span = plan.pairs * chans
    parts = [in_ref[:, s * span : (s + 1) * span] for s in range(plan.steps)]
    sums = jnp.dot(turn_ref[...], jnp.concatenate(parts, axis=0), preferred_element_type=F32)
    sums = sums * plan.scale
    real, imag = sums[: sums.shape[0] // 2], sums[sums.shape[0] // 2 :]
    pieces = []
    for pair in range(plan.pairs):
        cols = slice(pair * chans, (pair + 1) * chans)
        pieces += [real[:, cols], imag[:, cols]]
    out_ref[...] = jnp.concatenate(pieces, axis=1).astype(BF16)
    shared = in_ref[:, in_ref.shape[1] - chans :]
    total = jnp.dot(share_ref[...], shared, preferred_element_type=F32)
    gw_ref[...] = total * weight_scale


def spatial_kernel(plan, step, ext_ref, in_ref, back_ref, w_ref, tab_ref, gp_ref, out_ref, left_ref):
    chans, rows = plan.channels, plan.local_rows
    block = 2 * plan.ranks
    slots = rows // SLAB
    first = lax.axis_index("rows") * slots

    @pl.when(pl.program_id(0) == 0)
    def _():
        ordered = jnp.dot(back_ref[...], in_ref[...], preferred_element_type=F32)
        for row in range(rows):
            lines = ordered[row * block : (row + 1) * block]
            pieces = [
                lines[:, b * chans : (b + 1) * chans] for b in range(2 * plan.pairs)
            ]
            stacked = jnp.concatenate(pieces, axis=0)
            left_ref[row * chans : (row + 1) * chans] = stacked.T.astype(BF16)

    spatial = jnp.dot(left_ref[...], tab_ref[...], preferred_element_type=F32)
    column = lax.broadcasted_iota(jnp.int32, (chans, step), 1) + pl.program_id(0) * step
    for row in range(rows):
        direct = jnp.dot(w_ref[...], gp_ref[row], preferred_element_type=F32)
        value = spatial[row * chans : (row + 1) * chans] + direct
        live = column < ext_ref[0, first + row // SLAB]
        out_ref[0, row] = jnp.where(live, value, 0.0).astype(BF16)


def whole(array):
    return pl.BlockSpec(array.shape, lambda *_: (0,) * array.ndim)


def call(body, args, outs, name, flops, **kw):
    size = sum(a.size * a.dtype.itemsize for a in (*args, *outs))
    return pl.pallas_call(
        body,
        out_shape=outs,
        name=name,
        cost_estimate=pl.CostEstimate(flops=flops, bytes_accessed=size, transcendentals=0),
        compiler_params=pltpu.CompilerParams(vmem_limit_bytes=VMEM_LIMIT),
        **kw,
    )(*args)


def exchange(value):
    return lax.all_to_all(value, "rows", split_axis=0, concat_axis=0, tiled=True)


def every_sample(value, count):
    if count == 1:
        return [value]
    if count == 2:
        return [value, lax.ppermute(value, "batch", [(0, 1), (1, 0)])]
    gathered = lax.all_gather(value, "batch")
    return [gathered[i] for i in range(count)]


def shards(layer_input, pre_activation, cotangent, weight, spectral, slab_ids, extents):
    samples = lax.axis_size("batch")
    _, local_rows, chans, columns = layer_input.shape
    plan = Plan(lax.axis_size("rows"), local_rows, chans, columns, spectral.shape[0])
    ranks, active = plan.ranks, slab_ids.shape[1]
    sds = jax.ShapeDtypeStruct
    smem = pl.BlockSpec(memory_space=pltpu.SMEM)
    table = jnp.asarray(plan.column_table())
    forward_turn, backward_turn = turn_tables(plan, slab_ids[0])

    row_block = pl.BlockSpec((1, 1, chans, columns), lambda r: (0, r, 0, 0))
    spread, share_out = jnp.asarray(plan.spread()), jnp.asarray(plan.share_out())
    lines, wide = ranks * plan.group, 2 * plan.half + plan.both
    grad_pre, sent = call(
        functools.partial(column_kernel, plan),
        (extents, layer_input, pre_activation, cotangent, table, spread, share_out),
        (sds((local_rows, chans, columns), BF16), sds((lines, wide), BF16)),
        "columns",
        2 * local_rows * 2 * chans * columns * 2 * MODES,
        grid=(local_rows,),
        in_specs=[smem, row_block, row_block, row_block, whole(table), whole(spread), whole(share_out)],
        out_specs=(
            pl.BlockSpec((1, chans, columns), lambda r: (r, 0, 0)),
            pl.BlockSpec((lines, wide), lambda r: (0, 0)),
        ),
        scratch_shapes=[
            pltpu.VMEM((2 * chans, columns), BF16),
            pltpu.VMEM((local_rows, 2, ranks, 2 * plan.half), BF16),
            pltpu.VMEM((chans, chans), F32),
        ],
    )
    received = exchange(sent)

    mode_lines = ranks * plan.steps * 8
    sent, weight_share = call(
        functools.partial(row_kernel, plan),
        (forward_turn, received),
        (sds((mode_lines, plan.half), BF16), sds((plan.group, plan.both), F32)),
        "rows",
        2 * forward_turn.size * plan.half,
    )
    modes = exchange(sent)
    shares = every_sample(weight_share, samples)
    if samples > 2:
        shares = [sum(shares[1:], shares[0])]

    chunks = 4 if plan.exact and ranks % 4 == 0 else 1
    owners = ranks // chunks
    if plan.exact:
        held_shape, held_block = (plan.steps, PA), (plan.steps, owners * plan.pairs)
    else:
        held_shape, held_block = (1, plan.held), (1, plan.held)
    held_spec = pl.BlockSpec(
        held_block + (chans, plan.both), lambda n: (0, n if plan.exact else 0, 0, 0)
    )
    mode_block = pl.BlockSpec((owners * plan.steps * 8, plan.half), lambda n: (n, 0))
    mixed = plan.steps * plan.pairs
    back_width = -(-(mixed + 1) // 2) * plan.both
    held = spectral.reshape(held_shape + spectral.shape[1:])
    sent = call(
        functools.partial(mix_kernel, plan, owners, len(shares)),
        (*shares, modes, held),
        (sds((ranks * 8, back_width), BF16),),
        "mix",
        16 * spectral.size,
        grid=(chunks,),
        in_specs=[*(whole(s) for s in shares), mode_block, held_spec],
        out_specs=(pl.BlockSpec((owners * 8, back_width), lambda n: (n, 0)),),
    )[0]
    returned = exchange(sent)

    every = every_sample(modes, samples)
    grad_spectral = call(
        functools.partial(outer_kernel, plan, owners, samples),
        tuple(every),
        (sds(held_shape + spectral.shape[1:], F32),),
        "outer",
        16 * samples * spectral.size,
        grid=(chunks,),
        in_specs=[mode_block] * samples,
        out_specs=(held_spec,),
    )[0].reshape(spectral.shape)

    weight_scale = 1.0 / math.sqrt(samples * active * SLAB * columns)
    share_in = jnp.asarray(plan.share_in())
    sent, grad_weight = call(
        functools.partial(adjoint_kernel, plan, weight_scale),
        (backward_turn, returned, share_in),
        (sds((lines, plan.half), BF16), sds((chans, chans), F32)),
        "adjoint",
        2 * backward_turn.size * plan.pairs * chans,
    )
    local_back = exchange(sent)

    step = 512
    gather_back = jnp.asarray(plan.gather_back())
    grad_input = call(
        functools.partial(spatial_kernel, plan, step),
        (extents, local_back, gather_back, weight, table, grad_pre),
        (sds(layer_input.shape, BF16),),
        "spatial",
        2 * local_rows * chans * columns * (table.shape[0] + chans),
        grid=(columns // step,),
        in_specs=[
            smem,
            whole(local_back),
            whole(gather_back),
            whole(weight),
            pl.BlockSpec((table.shape[0], step), lambda n: (0, n)),
            pl.BlockSpec((local_rows, chans, step), lambda n: (0, 0, n)),
        ],
        out_specs=(pl.BlockSpec((1, local_rows, chans, step), lambda n: (0, 0, 0, n)),),
        scratch_shapes=[pltpu.VMEM((local_rows * chans, table.shape[0]), BF16)],
    )[0]
    return (grad_input, grad_spectral, grad_weight)


def solution(mesh):
    return jax.shard_map(
        shards,
        mesh=mesh,
        in_specs=(
            P("batch", "rows", None, None),
            P("batch", "rows", None, None),
            P("batch", "rows", None, None),
            P(),
            P("rows", None, None),
            P("batch", None),
            P("batch", None),
        ),
        out_specs=(P("batch", "rows", None, None), P("rows", None, None), P()),
        check_vma=False,
    )
```

time: 309 us -> 79 us (0.26); the launches traced: 304 us -> 78 us
  local copies, waits for them, and re-layouts: 152 us -> 3.77 us
  blocking collectives: 57.2 us -> 0 us
  Pallas kernels: 0 us -> 27.1 us
  other arithmetic: 31.5 us -> 7.15 us
  matrix products: 16.2 us -> 0 us
  between operations: 14.3 us -> 0.75 us
  starting transfers between devices: 17.2 us -> 21.1 us
    psum x1 -> x0, blocking collectives: 42.4 us -> none  [shards(): grad_weight = lax.psum(local_weight, ('batch', 'rows'))]
    unnamed x31 -> x22, local copies, waits for them, and re-layouts: 36.7 us -> 3.44 us
    pallas_call x0 -> x6, Pallas kernels: none -> 27.1 us  [call(): pl.pallas_call(body, out_shape=outs, name=name, cost_estimate=pl.CostEsti...]
    transpose x4 -> x1, local copies, waits for them, and re-layouts: 26.1 us -> 0.07 us  [rows_side(): return (spread.transpose(shape_order).reshape(-1), part, odd)]
    concatenate x2 -> x0, local copies, waits for them, and re-layouts: 18.2 us -> none  [row_adjoint(): joined = jnp.concatenate([upper, lower], axis=0)]
    another operation x3 -> x0, local copies, waits for them, and re-layouts: 17.2 us -> none  [the longest x2 12.3 us: row_combine(): jnp.stack([real_part, imag_part], axis=2) * scale]
    reshape x5 -> x0, local copies, waits for them, and re-layouts: 17.1 us -> none  [the longest x1 9.32 us: to_blocks(): shaped.transpose(2, 3, 1, 5, 0, 4)]
    all_to_all x5 -> x0, local copies, waits for them, and re-layouts: 16.3 us -> none  [the longest x1 12.1 us: shards(): lax.all_to_all(to_blocks(spectra, PA), 'rows', split_axis=4, concat_axis=...]
  transfers between devices with their start and end apart: 4 -> 6, of which waited for: 2 -> 5; matrix products, arithmetic and copies ran while one was open for 24% -> 10% of each run, Pallas kernels for 0% -> 11%
where the time goes in v1:
time: 79 us; the launch traced here: 78 us
  Pallas kernels  27.1 us (34%)
  starting transfers between devices  21.1 us (27%)
  waiting for transfers between devices  18.2 us (23%)
  other arithmetic  7.15 us (9%)
  local copies, waits for them, and re-layouts  3.77 us (5%)
    pallas_call x6, Pallas kernels, call(): pl.pallas_call(body, out_shape=outs, name=name, cost_estimate=pl.CostEsti...  27.1 us
    all_to_all x4, starting transfers between devices, exchange(): lax.all_to_all(value, 'rows', split_axis=0, concat_axis=0, tiled=True)  18 us
    all_to_all x4, waiting for transfers between devices, exchange(): lax.all_to_all(value, 'rows', split_axis=0, concat_axis=0, tiled=True)  15.8 us
    convert_element_type x2, other arithmetic, turn_table(): return jnp.where(mo == ro, value, 0.0).astype(BF16)  5.71 us
    unnamed x22, local copies, waits for them, and re-layouts  3.44 us
    ppermute x2, starting transfers between devices, every_sample(): return [value, lax.ppermute(value, 'batch', [(0, 1), (1, 0)])]  3.07 us
    ppermute x2, waiting for transfers between devices, every_sample(): return [value, lax.ppermute(value, 'batch', [(0, 1), (1, 0)])]  2.35 us
  transfers between devices with their start and end apart: 6, of which 5 were waited for; matrix products, arithmetic and copies ran while one was open for 10% of the time, Pallas kernels for 11%

profile of v1, /device:TPU:0, one launch (start us, length us, event | category | flops | bytes accessed | tf_op | source)
XLA Modules:
  0.0 78.0 jit_solution(14527265786286553564)
XLA Ops:
  0.6 0.0 copy-start.5
  0.6 0.0 copy-start.6
  0.7 0.0 copy-start.9
  0.7 0.0 copy-start.8
  0.7 0.0 copy-start.10
  0.7 5.6 %columns.1 = (bf16[4,64,2048]{2,1,0:T(8,128)(2,1)}, bf16[128,896]{1,0:T(8,128)(2,1)}) custom-call(s32[1,32]{1,0:T(1,128)} %ext_ref.3, bf16[1,4,64,2048]{3,2,1,0:T(8,128)(2,1)} %x_ref.1, bf16[1,4,64,2048]{3,2,1,0:T(8,128)(2,1)} %pre_ref.1, bf16[1,4,64,2048]{3,2,1,0:T(8,128)(2,1)} %cot_ref.1, bf16[192,2048]{1,0:T(8,128)(2,1)} %constant.57.clone.tab_ref, ...), custom_call_target="tpu_custom_call" | custom-call | flops 402653184 | bytes 5259392 | tf_op jit(solution)/shard_map/columns/pallas_call | solution.py:326
  6.3 7.4 %all-to-all-start = ((bf16[16,8,896]{2,1,0:T(8,128)(2,1)}), bf16[16,8,896]{2,1,0:T(8,128)(2,1)S(1)}, u32[]{:S(2)}, u32[]{:S(2)}) async-start(bf16[16,8,896]{2,1,0:T(8,128)(2,1)} %bitcast.22), calls=%async_computation | async-start | bytes 458752 | tf_op jit(solution)/shard_map/all_to_all | solution.py:337
  13.7 0.7 multiply_bitcast_fusion
  14.4 0.8 %broadcast_add_fusion = s32[32,2]{1,0:T(8,128)S(1)} fusion(s32[32,2]{1,0:T(8,128)} %constant.76, s32[32]{0:T(128)S(1)} %multiply_bitcast_fusion), kind=kLoop, calls=%fused_computation.22 | loop fusion | flops 64 | bytes 640 | tf_op jit(solution)/shard_map/add | solution.py:93
  15.2 0.1 reshape.41
  15.3 0.1 transpose.16
  15.4 0.1 mul.70
  15.5 3.3 %fusion.11.turn_ref = bf16[384,256]{1,0:T(8,128)(2,1)} fusion(s32[256]{0:T(256)} %constant.75, s32[384]{0:T(512)} %constant.60.clone, s32[256]{0:T(256)S(1)} %mul.70, s32[384]{0:T(512)} %constant.59.clone, s32[256]{0:T(256)} %constant.63.clone, s32[384]{0:T(512)} %constant.62.clone), kind=kLoop, calls=%fused_computation.17 | loop fusion | flops 1966080 | bytes 204288 | tf_op jit(solution)/shard_map/convert_element_type | solution.py:87
  18.8 4.4 %all-to-all-done = bf16[16,8,896]{2,1,0:T(8,128)(2,1)S(1)} async-done(((bf16[16,8,896]{2,1,0:T(8,128)(2,1)}), bf16[16,8,896]{2,1,0:T(8,128)(2,1)S(1)}, u32[]{:S(2)}, u32[]{:S(2)}) %all-to-all-start) | async-done | bytes 229408 | tf_op jit(solution)/shard_map/all_to_all | solution.py:337
  23.2 0.0 copy-start.1
  23.2 0.7 copy-done.1
  23.9 2.0 %rows.1 = (bf16[384,384]{1,0:T(8,128)(2,1)}, f32[8,128]{1,0:T(8,128)}) custom-call(bf16[384,256]{1,0:T(8,128)(2,1)} %fusion.11.turn_ref, bf16[128,896]{1,0:T(8,128)(2,1)} %bitcast.17), custom_call_target="tpu_custom_call" | custom-call | flops 75497472 | bytes 724992 | tf_op jit(solution)/shard_map/rows/pallas_call | solution.py:326
  25.9 3.5 %all-to-all-start.1 = ((bf16[16,24,384]{2,1,0:T(8,128)(2,1)}), bf16[16,24,384]{2,1,0:T(8,128)(2,1)S(1)}, u32[]{:S(2)}, u32[]{:S(2)}) async-start(bf16[16,24,384]{2,1,0:T(8,128)(2,1)} %bitcast.21), calls=%async_computation.1 | async-start | bytes 589824 | tf_op jit(solution)/shard_map/all_to_all | solution.py:337
  29.5 1.5 %collective-permute-start = (f32[8,128]{1,0:T(8,128)}, f32[8,128]{1,0:T(8,128)S(1)}, u32[]{:S(2)}, u32[]{:S(2)}) collective-permute-start(f32[8,128]{1,0:T(8,128)} %get-tuple-element.10.refs_0_), channel_id=1, source_target_pairs={{0,16},{16,0},{1,17},{17,1},{2,18},{18,2},{3,19},{19,3},{4,20},{20... | collective-permute-start | bytes 12296 | tf_op jit(solution)/shard_map/ppermute | solution.py:344
  31.0 2.3 %collective-permute-done.refs_1_ = f32[8,128]{1,0:T(8,128)S(1)} collective-permute-done((f32[8,128]{1,0:T(8,128)}, f32[8,128]{1,0:T(8,128)S(1)}, u32[]{:S(2)}, u32[]{:S(2)}) %collective-permute-start) | collective-permute-done | bytes 4128 | tf_op jit(solution)/shard_map/ppermute | solution.py:344
  33.4 0.0 copy-start.7
  33.4 6.6 %all-to-all-done.1 = bf16[16,24,384]{2,1,0:T(8,128)(2,1)S(1)} async-done(((bf16[16,24,384]{2,1,0:T(8,128)(2,1)}), bf16[16,24,384]{2,1,0:T(8,128)(2,1)S(1)}, u32[]{:S(2)}, u32[]{:S(2)}) %all-to-all-start.1) | async-done | bytes 294944 | tf_op jit(solution)/shard_map/all_to_all | solution.py:337
  40.0 0.0 copy-start
  40.0 0.0 copy-done.7
  40.0 0.7 copy-done
  40.7 6.7 %mix.1 = bf16[128,640]{1,0:T(8,128)(2,1)} custom-call(f32[8,128]{1,0:T(8,128)} %get-tuple-element.10.refs_0_, f32[8,128]{1,0:T(8,128)} %copy-done.7, bf16[384,384]{1,0:T(8,128)(2,1)} %bitcast.13, bf16[3,48,64,128]{3,2,1,0:T(8,128)(2,1)} %bitcast.16), custom_call_target="tpu_custom_call" | custom-call | flops 18874368 | bytes 2826240 | tf_op jit(solution)/shard_map/mix/pallas_call | solution.py:326
  47.4 3.5 %all-to-all-start.2 = ((bf16[16,8,640]{2,1,0:T(8,128)(2,1)}), bf16[16,8,640]{2,1,0:T(8,128)(2,1)S(1)}, u32[]{:S(2)}, u32[]{:S(2)}) async-start(bf16[16,8,640]{2,1,0:T(8,128)(2,1)} %bitcast.18), calls=%async_computation.2 | async-start | bytes 327680 | tf_op jit(solution)/shard_map/all_to_all | solution.py:337
  50.9 1.5 %collective-permute-start.1 = (bf16[384,384]{1,0:T(8,128)(2,1)}, bf16[384,384]{1,0:T(8,128)(2,1)S(1)}, u32[]{:S(2)}, u32[]{:S(2)}) collective-permute-start(bf16[384,384]{1,0:T(8,128)(2,1)} %bitcast.14), channel_id=1, source_target_pairs={{0,16},{16,0},{1,17},{17,1},{2,18},{18,2},{3,19},{19,3},{4,20},{20... | collective-permute-start | bytes 884744 | tf_op jit(solution)/shard_map/ppermute | solution.py:344
  52.5 0.0 copy-done.5
  52.5 0.0 copy-done.6
  52.5 0.0 copy-done.9
  52.5 0.0 copy-done.8
  52.5 0.0 copy-done.10
  52.5 2.4 %fusion.5.turn_ref = bf16[256,384]{1,0:T(8,128)(2,1)} fusion(s32[256]{0:T(256)S(1)} %copy-done.9, s32[384]{0:T(512)S(1)} %copy-done.6, s32[256]{0:T(256)S(1)} %mul.70, s32[384]{0:T(512)S(1)} %copy-done.8, s32[384]{0:T(512)S(1)} %copy-done.5, s32[256]{0:T(256)S(1)} %copy-done.10), kind=kLoop, calls=%fused_computation.11 | loop fusion | flops 1966080 | bytes 204288 | tf_op jit(solution)/shard_map/convert_element_type | solution.py:87
  54.9 4.4 %all-to-all-done.2 = bf16[16,8,640]{2,1,0:T(8,128)(2,1)S(1)} async-done(((bf16[16,8,640]{2,1,0:T(8,128)(2,1)}), bf16[16,8,640]{2,1,0:T(8,128)(2,1)S(1)}, u32[]{:S(2)}, u32[]{:S(2)}) %all-to-all-start.2) | async-done | bytes 163872 | tf_op jit(solution)/shard_map/all_to_all | solution.py:337
  59.3 0.0 copy-start.2
  59.3 0.7 copy-done.2
  60.0 2.0 %adjoint.1 = (bf16[128,384]{1,0:T(8,128)(2,1)}, f32[64,64]{1,0:T(8,128)}) custom-call(bf16[256,384]{1,0:T(8,128)(2,1)} %fusion.5.turn_ref, bf16[128,640]{1,0:T(8,128)(2,1)} %bitcast.19, bf16[64,128]{1,0:T(8,128)(2,1)} %constant.67.clone.share_ref), custom_call_target="tpu_custom_call" | custom-call | flops 37748736 | bytes 491520 | tf_op jit(solution)/shard_map/adjoint/pallas_call | solution.py:326
  62.0 3.5 %all-to-all-start.3 = ((bf16[16,8,384]{2,1,0:T(8,128)(2,1)}), bf16[16,8,384]{2,1,0:T(8,128)(2,1)S(1)}, u32[]{:S(2)}, u32[]{:S(2)}) async-start(bf16[16,8,384]{2,1,0:T(8,128)(2,1)} %bitcast.23), calls=%async_computation.3 | async-start | bytes 196608 | tf_op jit(solution)/shard_map/all_to_all | solution.py:337
  65.5 0.0 collective-permute-done.1.refs_1_
  65.5 0.0 copy-start.4
  65.5 0.7 copy-done.4
  66.2 6.2 %outer.1 = f32[3,48,64,128]{3,2,1,0:T(8,128)} custom-call(bf16[384,384]{1,0:T(8,128)(2,1)} %bitcast.15, bf16[384,384]{1,0:T(8,128)(2,1)} %copy-done.4), custom_call_target="tpu_custom_call" | custom-call | flops 37748736 | bytes 5308416 | tf_op jit(solution)/shard_map/outer/pallas_call | solution.py:326
  72.5 0.4 all-to-all-done.3
  72.8 0.0 copy-start.3
  72.8 0.6 copy-done.3
  73.5 4.6 %spatial.1 = bf16[1,4,64,2048]{3,2,1,0:T(8,128)(2,1)} custom-call(s32[1,32]{1,0:T(1,128)} %ext_ref.3, bf16[128,384]{1,0:T(8,128)(2,1)} %bitcast.20, bf16[128,128]{1,0:T(8,128)(2,1)} %constant.68.clone.back_ref, bf16[64,64]{1,0:T(8,128)(2,1)} %w_ref.1, bf16[192,2048]{1,0:T(8,128)(2,1)} %constant.57.clone.tab_ref, bf16[4,64,2048]{2,1,0:T(8,128)(2,1)} %get-tuple-element.13.gp_ref), custom_call_target="tpu_custom_call" | custom-call | flops 268435456 | bytes 3022976 | tf_op jit(solution)/shard_map/spatial/pallas_call | solution.py:326
Async XLA Ops:
  0.6 51.8 %copy-start.5 = (s32[384]{0:T(512)S(1)}, s32[384]{0:T(512)}, u32[]{:S(2)}) copy-start(s32[384]{0:T(512)} %constant.62.clone) | copy-start | bytes 4612
  0.6 51.8 %copy-start.6 = (s32[384]{0:T(512)S(1)}, s32[384]{0:T(512)}, u32[]{:S(2)}) copy-start(s32[384]{0:T(512)} %constant.60.clone) | copy-start | bytes 4612
  0.7 51.8 %copy-start.9 = (s32[256]{0:T(256)S(1)}, s32[256]{0:T(256)}, u32[]{:S(2)}) copy-start(s32[256]{0:T(256)} %constant.74) | copy-start | bytes 3076
  0.7 51.8 %copy-start.8 = (s32[384]{0:T(512)S(1)}, s32[384]{0:T(512)}, u32[]{:S(2)}) copy-start(s32[384]{0:T(512)} %constant.64.clone) | copy-start | bytes 4612
  0.7 51.8 %copy-start.10 = (s32[256]{0:T(256)S(1)}, s32[256]{0:T(256)}, u32[]{:S(2)}) copy-start(s32[256]{0:T(256)} %constant.61.clone) | copy-start | bytes 3076
  6.3 16.9 %all-to-all-start = ((bf16[16,8,896]{2,1,0:T(8,128)(2,1)}), bf16[16,8,896]{2,1,0:T(8,128)(2,1)S(1)}, u32[]{:S(2)}, u32[]{:S(2)}) async-start(bf16[16,8,896]{2,1,0:T(8,128)(2,1)} %bitcast.22), calls=%async_computation | async-start | bytes 458752 | tf_op jit(solution)/shard_map/all_to_all | solution.py:337
  23.2 0.7 copy-start.1
  25.9 14.1 %all-to-all-start.1 = ((bf16[16,24,384]{2,1,0:T(8,128)(2,1)}), bf16[16,24,384]{2,1,0:T(8,128)(2,1)S(1)}, u32[]{:S(2)}, u32[]{:S(2)}) async-start(bf16[16,24,384]{2,1,0:T(8,128)(2,1)} %bitcast.21), calls=%async_computation.1 | async-start | bytes 589824 | tf_op jit(solution)/shard_map/all_to_all | solution.py:337
  29.5 3.9 %collective-permute-start = (f32[8,128]{1,0:T(8,128)}, f32[8,128]{1,0:T(8,128)S(1)}, u32[]{:S(2)}, u32[]{:S(2)}) collective-permute-start(f32[8,128]{1,0:T(8,128)} %get-tuple-element.10.refs_0_), channel_id=1, source_target_pairs={{0,16},{16,0},{1,17},{17,1},{2,18},{18,2},{3,19},{19,3},{4,20},{20... | collective-permute-start | bytes 12296 | tf_op jit(solution)/shard_map/ppermute | solution.py:344
  33.4 6.6 %copy-start.7 = (f32[8,128]{1,0:T(8,128)}, f32[8,128]{1,0:T(8,128)S(1)}, u32[]{:S(2)}) copy-start(f32[8,128]{1,0:T(8,128)S(1)} %collective-permute-done.refs_1_) | copy-start | bytes 12292
  40.0 0.7 copy-start
  47.4 11.9 %all-to-all-start.2 = ((bf16[16,8,640]{2,1,0:T(8,128)(2,1)}), bf16[16,8,640]{2,1,0:T(8,128)(2,1)S(1)}, u32[]{:S(2)}, u32[]{:S(2)}) async-start(bf16[16,8,640]{2,1,0:T(8,128)(2,1)} %bitcast.18), calls=%async_computation.2 | async-start | bytes 327680 | tf_op jit(solution)/shard_map/all_to_all | solution.py:337
  50.9 14.6 %collective-permute-start.1 = (bf16[384,384]{1,0:T(8,128)(2,1)}, bf16[384,384]{1,0:T(8,128)(2,1)S(1)}, u32[]{:S(2)}, u32[]{:S(2)}) collective-permute-start(bf16[384,384]{1,0:T(8,128)(2,1)} %bitcast.14), channel_id=1, source_target_pairs={{0,16},{16,0},{1,17},{17,1},{2,18},{18,2},{3,19},{19,3},{4,20},{20... | collective-permute-start | bytes 884744 | tf_op jit(solution)/shard_map/ppermute | solution.py:344
  59.3 0.7 copy-start.2
  62.0 10.9 %all-to-all-start.3 = ((bf16[16,8,384]{2,1,0:T(8,128)(2,1)}), bf16[16,8,384]{2,1,0:T(8,128)(2,1)S(1)}, u32[]{:S(2)}, u32[]{:S(2)}) async-start(bf16[16,8,384]{2,1,0:T(8,128)(2,1)} %bitcast.23), calls=%async_computation.3 | async-start | bytes 196608 | tf_op jit(solution)/shard_map/all_to_all | solution.py:337
  65.5 0.7 copy-start.4
  72.8 0.6 copy-start.3

commit v2 on v1

--- a/solution.py
+++ b/solution.py
@@ -15,7 +15,6 @@
 MODES = 96
 F32 = jnp.float32
 BF16 = jnp.bfloat16
-VMEM_LIMIT = 56 * 1024 * 1024
 
 
 class Plan:
@@ -110,66 +109,112 @@
     return forward, backward
 
 
-def gelu_slope(values):
-    return (
-        0.5 * (1.0 + lax.erf(values * 0.7071067811865476))
-        + values * jnp.exp(-0.5 * values * values) * 0.3989422804014327
-    )
-
-
+LOG_PEAK = math.log2(0.3989422804014327)
 NT = (((1,), (1,)), ((), ()))
 TN = (((0,), (0,)), ((), ()))
 
 
+def mask_rows(extent, start, width, rows):
+    column = lax.broadcasted_iota(jnp.int32, (16, width), 1) + start
+    few = jnp.where(column < extent, 1.0, 0.0).astype(BF16)
+    return jnp.concatenate([few] * (rows // 16), axis=0)
+
+
 def column_kernel(
-    plan, ext_ref, x_ref, pre_ref, cot_ref, tab_ref, spread_ref, share_ref,
-    gp_ref, out_ref, v_ref, stage_ref, gw_ref,
+    plan, ext_ref, x_hbm, pre_hbm, cot_hbm, tab_hbm, spread_hbm, share_hbm, gp_hbm, out_ref,
+    x_ref, pre_ref, cot_ref, lines_ref, spread_ref, share_ref, stage_ref, in_sems, misc_sems,
 ):
-    row = pl.program_id(0)
     chans, ranks = plan.channels, plan.ranks
     slots = plan.local_rows // SLAB
-    extent = ext_ref[0, lax.axis_index("rows") * slots + row // SLAB]
-    step = 256
-    for start in range(0, plan.columns, step):
-        cols = slice(start, start + step)
-        live = lax.broadcasted_iota(jnp.int32, (chans, step), 1) + start < extent
-        kept = jnp.where(live, x_ref[0, 0, :, cols].astype(F32), 0.0).astype(BF16)
-        slope = gelu_slope(pre_ref[0, 0, :, cols].astype(F32))
-        grad = jnp.where(live, cot_ref[0, 0, :, cols].astype(F32) * slope, 0.0).astype(BF16)
-        v_ref[:chans, cols] = kept
-        v_ref[chans:, cols] = grad
-        gp_ref[0, :, cols] = grad
-    spec = lax.dot_general(tab_ref[...], v_ref[...], NT, preferred_element_type=F32).astype(BF16)
-    weight = lax.dot_general(v_ref[:chans], v_ref[chans:], NT, preferred_element_type=F32)
-    for pair in range(plan.pairs):
-        for part in range(2):
-            for odd in range(2):
-                base = ((pair * 2 + part) * 2 + odd) * ranks
-                lane = (odd * plan.pairs + pair) * plan.both
-                stage_ref[row, part, :, lane : lane + plan.both] = spec[base : base + ranks]
-
-    @pl.when(row == 0)
-    def _():
-        gw_ref[...] = weight
-
-    @pl.when(row > 0)
-    def _():
-        gw_ref[...] += weight
-
-    @pl.when(row == plan.local_rows - 1)
-    def _():
-        wide = 2 * plan.half
-        staged = stage_ref[...].reshape(plan.group * ranks, wide)
-        out_ref[:, :wide] = jnp.dot(
-            spread_ref[...], staged, preferred_element_type=F32
-        ).astype(BF16)
-        total = gw_ref[...]
-        high = total.astype(BF16)
-        low = (total - high.astype(F32)).astype(BF16)
-        split = jnp.concatenate([high, low], axis=1)
-        out_ref[:, wide:] = jnp.dot(
-            share_ref[...], split, preferred_element_type=F32
-        ).astype(BF16)
+    freqs = tab_hbm.shape[0]
+    first = lax.axis_index("rows") * slots
+    loads, tables, saves = [], [], []
+    for slot in range(slots):
+        rows = pl.ds(slot * SLAB, SLAB)
+        loads.append(
+            [
+                pltpu.make_async_copy(src.at[0, rows], dst.at[slot], in_sems.at[slot, n])
+                for n, (src, dst) in enumerate(
+                    ((pre_hbm, pre_ref), (cot_hbm, cot_ref), (x_hbm, x_ref))
+                )
+            ]
+        )
+        tables.append(
+            pltpu.make_async_copy(tab_hbm, lines_ref.at[slot, pl.ds(0, freqs)], in_sems.at[slot, 3])
+        )
+        saves.append(
+            pltpu.make_async_copy(
+                lines_ref.at[slot, pl.ds(freqs + SLAB * chans, SLAB * chans)],
+                gp_hbm.at[pl.ds(slot * SLAB * chans, SLAB * chans)],
+                in_sems.at[slot, 4],
+            )
+        )
+    small = [
+        pltpu.make_async_copy(spread_hbm, spread_ref, misc_sems.at[0]),
+        pltpu.make_async_copy(share_hbm, share_ref, misc_sems.at[1]),
+    ]
+    for slot in range(slots):
+        for copy in loads[slot]:
+            copy.start()
+        tables[slot].start()
+    for copy in small:
+        copy.start()
+
+    width = 256
+    lane = lax.broadcasted_iota(jnp.int32, (freqs, plan.both), 1)
+    total = jnp.zeros((chans, chans), F32)
+    for slot in range(slots):
+        extent = ext_ref[0, first + slot]
+        for copy in loads[slot]:
+            copy.wait()
+        for start in range(0, plan.columns, width):
+            cols = slice(start, start + width)
+            live = mask_rows(extent, start, width, chans)
+            for row in range(SLAB):
+                value = pre_ref[slot, row, :, cols].astype(F32)
+                turned = value * 0.7071067811865476
+                bell = jnp.exp2(turned * turned * -1.4426950408889634 + LOG_PEAK)
+                slope = value * bell + (0.5 + 0.5 * lax.erf(turned))
+                cot = (cot_ref[slot, row, :, cols] * live).astype(F32)
+                base = freqs + row * chans
+                lines_ref[slot, base : base + chans, cols] = x_ref[slot, row, :, cols] * live
+                base += SLAB * chans
+                lines_ref[slot, base : base + chans, cols] = (cot * slope).astype(BF16)
+        saves[slot].start()
+        tables[slot].wait()
+        edge = freqs + SLAB * chans
+        sums = lax.dot_general(
+            lines_ref[slot, :edge], lines_ref[slot, freqs:], NT, preferred_element_type=F32
+        )
+        for row in range(SLAB):
+            base = freqs + row * chans
+            side = SLAB * chans + row * chans
+            total = total + sums[base : base + chans, side : side + chans]
+        inputs, grads = sums[:freqs, : plan.both], sums[:freqs, plan.both :]
+        near = jnp.where(lane < chans, inputs, pltpu.roll(grads, chans, axis=1)).astype(BF16)
+        far = jnp.where(lane < chans, pltpu.roll(inputs, chans, axis=1), grads).astype(BF16)
+        for row, spec in enumerate((near, far)):
+            for pair in range(plan.pairs):
+                for part in range(2):
+                    for odd in range(2):
+                        base = ((pair * 2 + part) * 2 + odd) * ranks
+                        lanes = (odd * plan.pairs + pair) * plan.both
+                        line = ((slot * SLAB + row) * 2 + part) * ranks
+                        stage_ref[line : line + ranks, lanes : lanes + plan.both] = spec[
+                            base : base + ranks
+                        ]
+    for copy in small:
+        copy.wait()
+    wide = 2 * plan.half
+    out_ref[:, :wide] = jnp.dot(
+        spread_ref[...], stage_ref[...], preferred_element_type=F32
+    ).astype(BF16)
+    high = total.astype(BF16)
+    low = (total - high.astype(F32)).astype(BF16)
+    split = jnp.concatenate([high, low], axis=1)
+    out_ref[:, wide:] = jnp.dot(share_ref[...], split, preferred_element_type=F32).astype(BF16)
+    for copy in saves:
+        copy.wait()
 
 
 def row_kernel(plan, turn_ref, in_ref, out_ref, share_ref):
@@ -201,44 +246,90 @@
     return lax.rem(k * plan.held, PA)
 
 
-def mix_kernel(plan, owners, samples, *refs):
-    share_refs, (in_ref, spec_ref, out_ref) = refs[:samples], refs[samples:]
-    chans = plan.channels
+def slot_order(plan):
+    order = []
+    for step in range(plan.steps):
+        order += [(step, pair) for pair in range(plan.pairs - plan.pairs % 2)]
+    if plan.pairs % 2:
+        order += [(step, plan.pairs - 1) for step in range(plan.steps)]
+    return order
+
+
+def mix_kernel(plan, samples, *refs):
+    share_refs, (in_ref, spec_ref, out_hbm, out_ref, sems) = refs[:samples], refs[samples:]
+    chans, both = plan.channels, plan.both
     total = share_refs[0][...]
     for ref in share_refs[1:]:
         total = total + ref[...]
-    total = total[:8, :chans]
+    total = total[:8, :]
     high = total.astype(BF16).astype(F32)
     low = pltpu.roll(total - high, plan.share, axis=0)
     row = lax.broadcasted_iota(jnp.int32, total.shape, 0)
+    lane = lax.broadcasted_iota(jnp.int32, total.shape, 1)
     zero = jnp.zeros_like(total)
     shared = jnp.where(row < plan.share, high, jnp.where(row < 2 * plan.share, low, zero))
-
-    def body(local, carry):
-        owner = pl.program_id(0) * owners + local
-        pieces = []
+    order = slot_order(plan)
+
+    def one_owner(owner):
+        blocks = {}
         for step in range(plan.steps):
-            for pair in range(plan.pairs):
-                start = pl.multiple_of(local * (8 * plan.steps) + 8 * step, 8)
-                tile = in_ref[pl.ds(start, 8), pair * plan.both : (pair + 1) * plan.both]
-                left = out_pair(tile.astype(F32), chans).astype(BF16)
-                if plan.exact:
-                    right = spec_ref[step, local * plan.pairs + pair]
-                else:
-                    place, ok = where_held(plan, owner, step, pair, mode_offset(plan))
-                    right = spec_ref[0, place]
-                piece = lax.dot_general(left, right, NT, preferred_element_type=F32)
-                if not plan.exact:
+            start = (owner * plan.steps + step) * 8
+            left = [
+                out_pair(in_ref[start : start + 8, p * both : (p + 1) * both].astype(F32), chans)
+                for p in range(plan.pairs)
+            ]
+            if plan.exact:
+                base = (step * PA + owner * plan.pairs) * chans
+                right = spec_ref[base : base + plan.pairs * chans]
+                value = lax.dot_general(
+                    jnp.concatenate(left, axis=0).astype(BF16), right, NT,
+                    preferred_element_type=F32,
+                )
+                for p in range(plan.pairs):
+                    cols = slice((p // 2) * both, (p // 2) * both + both)
+                    piece = value[8 * p : 8 * p + 8]
+                    if (p // 2) * both + both > piece.shape[1]:
+                        piece = piece[:, (p // 2) * both :]
+                        piece = jnp.concatenate([piece, jnp.zeros_like(piece)], axis=1)
+                    else:
+                        piece = piece[:, cols]
+                    blocks[step, p] = (piece, p % 2)
+            else:
+                for p in range(plan.pairs):
+                    place, ok = where_held(plan, owner, step, p, mode_offset(plan))
+                    right = spec_ref[pl.ds(pl.multiple_of(place * chans, chans), chans)]
+                    piece = lax.dot_general(
+                        left[p].astype(BF16), right, NT, preferred_element_type=F32
+                    )
                     piece = jnp.where(ok, piece, 0.0)
-                pieces.append(piece)
-        if len(pieces) % 2 == 0:
-            pieces.append(jnp.zeros_like(shared))
-        pieces.append(shared)
-        joined = jnp.concatenate(pieces[:-2] + [pieces[-2], pieces[-1]], axis=1)
-        out_ref[pl.ds(pl.multiple_of(local * 8, 8), 8), :] = joined.astype(BF16)
-        return carry
-
-    lax.fori_loop(0, owners, body, 0)
+                    blocks[step, p] = (jnp.concatenate([piece, piece], axis=1), 0)
+        places = [blocks[key] for key in order]
+        while len(places) % 2 == 0:
+            places.append((zero, 0))
+        places.append((shared, 0))
+
+        def at(block, side):
+            value, held = block
+            return value if held == side else pltpu.roll(value, chans, axis=1)
+
+        tiles = [
+            jnp.where(lane < chans, at(places[n], 0), at(places[n + 1], 1))
+            for n in range(0, len(places), 2)
+        ]
+        out_ref[owner * 8 : owner * 8 + 8, :] = jnp.concatenate(tiles, axis=1).astype(BF16)
+
+    chunks = sems.shape[0]
+    each = plan.ranks // chunks
+    copies = []
+    for chunk in range(chunks):
+        for owner in range(chunk * each, (chunk + 1) * each):
+            one_owner(owner)
+        lines = pl.ds(chunk * each * 8, each * 8)
+        copy = pltpu.make_async_copy(out_ref.at[lines], out_hbm.at[lines], sems.at[chunk])
+        copy.start()
+        copies.append(copy)
+    for copy in copies:
+        copy.wait()
 
 
 def outer_kernel(plan, owners, samples, *refs):
@@ -276,8 +367,13 @@
 
 def adjoint_kernel(plan, weight_scale, turn_ref, in_ref, share_ref, out_ref, gw_ref):
     chans = plan.channels
-    span = plan.pairs * chans
-    parts = [in_ref[:, s * span : (s + 1) * span] for s in range(plan.steps)]
+    order = slot_order(plan)
+    parts = []
+    for step in range(plan.steps):
+        places = [order.index((step, pair)) for pair in range(plan.pairs)]
+        parts.append(
+            jnp.concatenate([in_ref[:, n * chans : (n + 1) * chans] for n in places], axis=1)
+        )
     sums = jnp.dot(turn_ref[...], jnp.concatenate(parts, axis=0), preferred_element_type=F32)
     sums = sums * plan.scale
     real, imag = sums[: sums.shape[0] // 2], sums[sums.shape[0] // 2 :]
@@ -291,44 +387,52 @@
     gw_ref[...] = total * weight_scale
 
 
-def spatial_kernel(plan, step, ext_ref, in_ref, back_ref, w_ref, tab_ref, gp_ref, out_ref, left_ref):
+def spatial_kernel(
+    plan, step, ext_ref, in_ref, back_ref, w_ref, tab_ref, gp_ref, out_hbm, left_ref, out_ref, sems
+):
     chans, rows = plan.channels, plan.local_rows
     block = 2 * plan.ranks
     slots = rows // SLAB
     first = lax.axis_index("rows") * slots
-
-    @pl.when(pl.program_id(0) == 0)
-    def _():
-        ordered = jnp.dot(back_ref[...], in_ref[...], preferred_element_type=F32)
-        for row in range(rows):
-            lines = ordered[row * block : (row + 1) * block]
-            pieces = [
-                lines[:, b * chans : (b + 1) * chans] for b in range(2 * plan.pairs)
-            ]
-            stacked = jnp.concatenate(pieces, axis=0)
-            left_ref[row * chans : (row + 1) * chans] = stacked.T.astype(BF16)
-
-    spatial = jnp.dot(left_ref[...], tab_ref[...], preferred_element_type=F32)
-    column = lax.broadcasted_iota(jnp.int32, (chans, step), 1) + pl.program_id(0) * step
+    ordered = jnp.dot(back_ref[...], in_ref[...], preferred_element_type=F32)
     for row in range(rows):
-        direct = jnp.dot(w_ref[...], gp_ref[row], preferred_element_type=F32)
-        value = spatial[row * chans : (row + 1) * chans] + direct
-        live = column < ext_ref[0, first + row // SLAB]
-        out_ref[0, row] = jnp.where(live, value, 0.0).astype(BF16)
+        lines = ordered[row * block : (row + 1) * block]
+        pieces = [lines[:, b * chans : (b + 1) * chans] for b in range(2 * plan.pairs)]
+        stacked = jnp.concatenate(pieces, axis=0)
+        left_ref[row * chans : (row + 1) * chans] = stacked.T.astype(BF16)
+    copies = []
+    for n in range(plan.columns // step):
+        cols = slice(n * step, (n + 1) * step)
+        spatial = jnp.dot(left_ref[...], tab_ref[:, cols], preferred_element_type=F32)
+        for slot in range(slots):
+            live = mask_rows(ext_ref[0, first + slot], n * step, step, chans)
+            for row in range(slot * SLAB, (slot + 1) * SLAB):
+                lines = slice(row * chans, (row + 1) * chans)
+                direct = jnp.dot(w_ref[...], gp_ref[lines, cols], preferred_element_type=F32)
+                out_ref[row, :, cols] = (spatial[lines] + direct).astype(BF16) * live
+        copy = pltpu.make_async_copy(
+            out_ref.at[:, :, pl.ds(n * step, step)],
+            out_hbm.at[0, :, :, pl.ds(n * step, step)],
+            sems.at[n],
+        )
+        copy.start()
+        copies.append(copy)
+    for copy in copies:
+        copy.wait()
 
 
 def whole(array):
     return pl.BlockSpec(array.shape, lambda *_: (0,) * array.ndim)
 
 
-def call(body, args, outs, name, flops, **kw):
+def call(body, args, outs, name, flops, mib, **kw):
     size = sum(a.size * a.dtype.itemsize for a in (*args, *outs))
     return pl.pallas_call(
         body,
         out_shape=outs,
         name=name,
         cost_estimate=pl.CostEstimate(flops=flops, bytes_accessed=size, transcendentals=0),
-        compiler_params=pltpu.CompilerParams(vmem_limit_bytes=VMEM_LIMIT),
+        compiler_params=pltpu.CompilerParams(vmem_limit_bytes=mib * 1024 * 1024),
         **kw,
     )(*args)
 
@@ -356,25 +460,32 @@
     table = jnp.asarray(plan.column_table())
     forward_turn, backward_turn = turn_tables(plan, slab_ids[0])
 
-    row_block = pl.BlockSpec((1, 1, chans, columns), lambda r: (0, r, 0, 0))
     spread, share_out = jnp.asarray(plan.spread()), jnp.asarray(plan.share_out())
     lines, wide = ranks * plan.group, 2 * plan.half + plan.both
+    slots = local_rows // SLAB
+    freqs = table.shape[0]
+    hbm = pl.BlockSpec(memory_space=pltpu.HBM)
+    vmem = pl.BlockSpec(memory_space=pltpu.VMEM)
+    stored = (slots, SLAB, chans, columns)
     grad_pre, sent = call(
         functools.partial(column_kernel, plan),
         (extents, layer_input, pre_activation, cotangent, table, spread, share_out),
-        (sds((local_rows, chans, columns), BF16), sds((lines, wide), BF16)),
+        (sds((local_rows * chans, columns), BF16), sds((lines, wide), BF16)),
         "columns",
         2 * local_rows * 2 * chans * columns * 2 * MODES,
-        grid=(local_rows,),
-        in_specs=[smem, row_block, row_block, row_block, whole(table), whole(spread), whole(share_out)],
-        out_specs=(
-            pl.BlockSpec((1, chans, columns), lambda r: (r, 0, 0)),
-            pl.BlockSpec((lines, wide), lambda r: (0, 0)),
-        ),
+        62,
+        in_specs=[smem] + [hbm] * 6,
+        out_specs=(hbm, vmem),
         scratch_shapes=[
-            pltpu.VMEM((2 * chans, columns), BF16),
-            pltpu.VMEM((local_rows, 2, ranks, 2 * plan.half), BF16),
-            pltpu.VMEM((chans, chans), F32),
+            pltpu.VMEM(stored, BF16),
+            pltpu.VMEM(stored, BF16),
+            pltpu.VMEM(stored, BF16),
+            pltpu.VMEM((slots, freqs + 2 * SLAB * chans, columns), BF16),
+            pltpu.VMEM(spread.shape, BF16),
+            pltpu.VMEM(share_out.shape, BF16),
+            pltpu.VMEM((plan.group * ranks, 2 * plan.half), BF16),
+            pltpu.SemaphoreType.DMA((slots, 5)),
+            pltpu.SemaphoreType.DMA((2,)),
         ],
     )
     received = exchange(sent)
@@ -386,6 +497,7 @@
         (sds((mode_lines, plan.half), BF16), sds((plan.group, plan.both), F32)),
         "rows",
         2 * forward_turn.size * plan.half,
+        16,
     )
     modes = exchange(sent)
     shares = every_sample(weight_share, samples)
@@ -404,16 +516,17 @@
     mode_block = pl.BlockSpec((owners * plan.steps * 8, plan.half), lambda n: (n, 0))
     mixed = plan.steps * plan.pairs
     back_width = -(-(mixed + 1) // 2) * plan.both
-    held = spectral.reshape(held_shape + spectral.shape[1:])
     sent = call(
-        functools.partial(mix_kernel, plan, owners, len(shares)),
-        (*shares, modes, held),
+        functools.partial(mix_kernel, plan, len(shares)),
+        (*shares, modes, spectral.reshape(-1, plan.both)),
         (sds((ranks * 8, back_width), BF16),),
         "mix",
         16 * spectral.size,
-        grid=(chunks,),
-        in_specs=[*(whole(s) for s in shares), mode_block, held_spec],
-        out_specs=(pl.BlockSpec((owners * 8, back_width), lambda n: (n, 0)),),
+        16,
+        in_specs=[vmem] * (len(shares) + 2),
+        out_specs=(hbm,),
+        scratch_shapes=[pltpu.VMEM((ranks * 8, back_width), BF16)]
+        + [pltpu.SemaphoreType.DMA((chunks,))],
     )[0]
     returned = exchange(sent)
 
@@ -424,6 +537,7 @@
         (sds(held_shape + spectral.shape[1:], F32),),
         "outer",
         16 * samples * spectral.size,
+        16,
         grid=(chunks,),
         in_specs=[mode_block] * samples,
         out_specs=(held_spec,),
@@ -437,6 +551,7 @@
         (sds((lines, plan.half), BF16), sds((chans, chans), F32)),
         "adjoint",
         2 * backward_turn.size * plan.pairs * chans,
+        16,
     )
     local_back = exchange(sent)
 
@@ -448,17 +563,14 @@
         (sds(layer_input.shape, BF16),),
         "spatial",
         2 * local_rows * chans * columns * (table.shape[0] + chans),
-        grid=(columns // step,),
-        in_specs=[
-            smem,
-            whole(local_back),
-            whole(gather_back),
-            whole(weight),
-            pl.BlockSpec((table.shape[0], step), lambda n: (0, n)),
-            pl.BlockSpec((local_rows, chans, step), lambda n: (0, 0, n)),
+        16,
+        in_specs=[smem] + [vmem] * 5,
+        out_specs=(hbm,),
+        scratch_shapes=[
+            pltpu.VMEM((local_rows * chans, table.shape[0]), BF16),
+            pltpu.VMEM((local_rows, chans, columns), BF16),
+            pltpu.SemaphoreType.DMA((columns // step,)),
         ],
-        out_specs=(pl.BlockSpec((1, local_rows, chans, step), lambda n: (0, 0, 0, n)),),
-        scratch_shapes=[pltpu.VMEM((local_rows * chans, table.shape[0]), BF16)],
     )[0]
     return (grad_input, grad_spectral, grad_weight)
 

time: 79 us -> 69.8 us (0.88)
  Pallas kernels: 27.1 us -> 18.1 us
  waiting for transfers between devices: 18.2 us -> 21 us
  local copies, waits for them, and re-layouts: 3.77 us -> 2.05 us
  other arithmetic: 7.15 us -> 5.9 us
    pallas_call x6, Pallas kernels: 27.1 us -> 18.1 us  [call(): pl.pallas_call(body, out_shape=outs, name=name, cost_estimate=pl.CostEsti...]
    all_to_all x4, waiting for transfers between devices: 15.8 us -> 18.9 us  [exchange(): lax.all_to_all(value, 'rows', split_axis=0, concat_axis=0, tiled=True)]
    unnamed x22 -> x24, local copies, waits for them, and re-layouts: 3.44 us -> 1.73 us
    convert_element_type x2, other arithmetic: 5.71 us -> 4.46 us  [turn_table(): return jnp.where(mo == ro, value, 0.0).astype(BF16)]
  transfers between devices with their start and end apart: 6 -> 6, of which waited for: 5 -> 5; matrix products, arithmetic and copies ran while one was open for 10% -> 9% of each run, Pallas kernels for 11% -> 9%
where the time goes in v2:
time: 69.8 us; the launch traced here: 69.1 us
  starting transfers between devices  21.3 us (31%)
  waiting for transfers between devices  21 us (30%)
  Pallas kernels  18.1 us (26%)
  other arithmetic  5.9 us (8%)
  local copies, waits for them, and re-layouts  2.05 us (3%)
  between operations  0.81 us (1%)
    all_to_all x4, waiting for transfers between devices, exchange(): lax.all_to_all(value, 'rows', split_axis=0, concat_axis=0, tiled=True)  18.9 us
    all_to_all x4, starting transfers between devices, exchange(): lax.all_to_all(value, 'rows', split_axis=0, concat_axis=0, tiled=True)  18.1 us
    pallas_call x6, Pallas kernels, call(): pl.pallas_call(body, out_shape=outs, name=name, cost_estimate=pl.CostEsti...  18.1 us
    convert_element_type x2, other arithmetic, turn_table(): return jnp.where(mo == ro, value, 0.0).astype(BF16)  4.46 us
    ppermute x2, starting transfers between devices, every_sample(): return [value, lax.ppermute(value, 'batch', [(0, 1), (1, 0)])]  3.13 us
    ppermute x2, waiting for transfers between devices, every_sample(): return [value, lax.ppermute(value, 'batch', [(0, 1), (1, 0)])]  2.11 us
    unnamed x24, local copies, waits for them, and re-layouts  1.73 us
  transfers between devices with their start and end apart: 6, of which 5 were waited for; matrix products, arithmetic and copies ran while one was open for 9% of the time, Pallas kernels for 9%

profile of v2, /device:TPU:0, one launch (start us, length us, event | category | flops | bytes accessed | tf_op | source)
XLA Modules:
  0.0 69.1 jit_solution(9978137316978607050)
XLA Ops:
  0.6 0.0 copy-start.7
  0.6 0.0 copy-start.8
  0.7 0.0 copy-start.10
  0.7 0.0 copy-start.9
  0.7 0.0 copy-start.11
  0.7 0.0 copy-start.5
  0.7 6.1 %columns.1 = (bf16[256,2048]{1,0:T(8,128)(2,1)}, bf16[128,896]{1,0:T(8,128)(2,1)}) custom-call(s32[1,32]{1,0:T(1,128)} %ext_ref.3, bf16[1,4,64,2048]{3,2,1,0:T(8,128)(2,1)} %x_hbm.1, bf16[1,4,64,2048]{3,2,1,0:T(8,128)(2,1)} %pre_hbm.1, bf16[1,4,64,2048]{3,2,1,0:T(8,128)(2,1)} %cot_hbm.1, bf16[192,2048]{1,0:T(8,128)(2,1)} %constant.57.clone.tab_hbm.tab_ref, ...), custom_call_target="tpu_custom_call" | custom-call | flops 402653184 | bytes 5259392 | tf_op jit(solution)/shard_map/columns/pallas_call | solution.py:430
  6.8 7.4 %all-to-all-start = ((bf16[16,8,896]{2,1,0:T(8,128)(2,1)}), bf16[16,8,896]{2,1,0:T(8,128)(2,1)S(1)}, u32[]{:S(2)}, u32[]{:S(2)}) async-start(bf16[16,8,896]{2,1,0:T(8,128)(2,1)} %bitcast.20), calls=%async_computation | async-start | bytes 458752 | tf_op jit(solution)/shard_map/all_to_all | solution.py:441
  14.2 0.7 multiply_bitcast_fusion
  14.9 0.8 %broadcast_add_fusion = s32[32,2]{1,0:T(8,128)S(1)} fusion(s32[32,2]{1,0:T(8,128)} %constant.76, s32[32]{0:T(128)S(1)} %multiply_bitcast_fusion), kind=kLoop, calls=%fused_computation.22 | loop fusion | flops 64 | bytes 640 | tf_op jit(solution)/shard_map/add | solution.py:92
  15.7 0.1 reshape.41
  15.8 0.1 transpose.16
  15.9 0.1 mul.70
  16.0 2.6 %fusion.11.turn_ref = bf16[384,256]{1,0:T(8,128)(2,1)S(1)} fusion(s32[256]{0:T(256)} %constant.75, s32[384]{0:T(512)} %constant.60.clone, s32[256]{0:T(256)S(1)} %mul.70, s32[384]{0:T(512)} %constant.59.clone, s32[256]{0:T(256)} %constant.63.clone, s32[384]{0:T(512)} %constant.62.clone), kind=kLoop, calls=%fused_computation.17 | loop fusion | flops 1966080 | bytes 204288 | tf_op jit(solution)/shard_map/convert_element_type | solution.py:86
  18.7 5.1 %all-to-all-done = bf16[16,8,896]{2,1,0:T(8,128)(2,1)S(1)} async-done(((bf16[16,8,896]{2,1,0:T(8,128)(2,1)}), bf16[16,8,896]{2,1,0:T(8,128)(2,1)S(1)}, u32[]{:S(2)}, u32[]{:S(2)}) %all-to-all-start) | async-done | bytes 229408 | tf_op jit(solution)/shard_map/all_to_all | solution.py:441
  23.7 1.0 %rows.1 = (bf16[384,384]{1,0:T(8,128)(2,1)}, f32[8,128]{1,0:T(8,128)S(1)}) custom-call(bf16[384,256]{1,0:T(8,128)(2,1)S(1)} %fusion.11.turn_ref, bf16[128,896]{1,0:T(8,128)(2,1)S(1)} %bitcast.16), custom_call_target="tpu_custom_call" | custom-call | flops 75497472 | bytes 724992 | tf_op jit(solution)/shard_map/rows/pallas_call | solution.py:430
  24.7 0.0 copy-start.3
  24.7 0.0 copy-start.4
  24.7 0.0 copy-start.6
  24.7 3.7 %all-to-all-start.1 = ((bf16[16,24,384]{2,1,0:T(8,128)(2,1)}), bf16[16,24,384]{2,1,0:T(8,128)(2,1)S(1)}, u32[]{:S(2)}, u32[]{:S(2)}) async-start(bf16[16,24,384]{2,1,0:T(8,128)(2,1)} %bitcast.3), calls=%async_computation.1 | async-start | bytes 589824 | tf_op jit(solution)/shard_map/all_to_all | solution.py:441
  28.4 0.0 copy-start
  28.4 1.6 %collective-permute-start = (f32[8,128]{1,0:T(8,128)S(1)}, f32[8,128]{1,0:T(8,128)S(1)}, u32[]{:S(2)}, u32[]{:S(2)}) collective-permute-start(f32[8,128]{1,0:T(8,128)S(1)} %get-tuple-element.10.refs_0_), channel_id=1, source_target_pairs={{0,16},{16,0},{1,17},{17,1},{2,18},{18,2},{3,19},{19,3},{4,20},{20... | collective-permute-start | bytes 12296 | tf_op jit(solution)/shard_map/ppermute | solution.py:448
  30.0 2.1 %collective-permute-done.refs_1_ = f32[8,128]{1,0:T(8,128)S(1)} collective-permute-done((f32[8,128]{1,0:T(8,128)S(1)}, f32[8,128]{1,0:T(8,128)S(1)}, u32[]{:S(2)}, u32[]{:S(2)}) %collective-permute-start) | collective-permute-done | bytes 4128 | tf_op jit(solution)/shard_map/ppermute | solution.py:448
  32.1 6.8 %all-to-all-done.1 = bf16[16,24,384]{2,1,0:T(8,128)(2,1)S(1)} async-done(((bf16[16,24,384]{2,1,0:T(8,128)(2,1)}), bf16[16,24,384]{2,1,0:T(8,128)(2,1)S(1)}, u32[]{:S(2)}, u32[]{:S(2)}) %all-to-all-start.1) | async-done | bytes 294944 | tf_op jit(solution)/shard_map/all_to_all | solution.py:441
  38.9 0.0 copy-start.1
  38.9 1.7 %copy-done.1 = bf16[144,64,128]{2,1,0:T(8,128)(2,1)S(1)} copy-done((bf16[144,64,128]{2,1,0:T(8,128)(2,1)S(1)}, bf16[144,64,128]{2,1,0:T(8,128)(2,1)}, u32[]{:S(2)}) %copy-start.1) | copy-done | bytes 2359320
  40.5 2.3 %mix.1 = bf16[128,640]{1,0:T(8,128)(2,1)} custom-call(f32[8,128]{1,0:T(8,128)S(1)} %get-tuple-element.10.refs_0_, f32[8,128]{1,0:T(8,128)S(1)} %collective-permute-done.refs_1_, bf16[384,384]{1,0:T(8,128)(2,1)S(1)} %bitcast.12, bf16[9216,128]{1,0:T(8,128)(2,1)S(1)} %bitcast.15), custom_call_target="tpu_custom_call" | custom-call | flops 18874368 | bytes 2826240 | tf_op jit(solution)/shard_map/mix/pallas_call | solution.py:430
  42.9 3.5 %all-to-all-start.2 = ((bf16[16,8,640]{2,1,0:T(8,128)(2,1)}), bf16[16,8,640]{2,1,0:T(8,128)(2,1)S(1)}, u32[]{:S(2)}, u32[]{:S(2)}) async-start(bf16[16,8,640]{2,1,0:T(8,128)(2,1)} %bitcast.6), calls=%async_computation.2 | async-start | bytes 327680 | tf_op jit(solution)/shard_map/all_to_all | solution.py:441
  46.4 1.6 %collective-permute-start.1 = (bf16[384,384]{1,0:T(8,128)(2,1)S(1)}, bf16[384,384]{1,0:T(8,128)(2,1)S(1)}, u32[]{:S(2)}, u32[]{:S(2)}) collective-permute-start(bf16[384,384]{1,0:T(8,128)(2,1)S(1)} %bitcast.13), channel_id=1, source_target_pairs={{0,16},{16,0},{1,17},{17,1},{2,18},{18,2},{3,19},{19,3},{4,20},{20... | collective-permute-start | bytes 884744 | tf_op jit(solution)/shard_map/ppermute | solution.py:448
  48.0 0.0 copy-done.7
  48.0 0.0 copy-done.8
  48.0 0.0 copy-done.10
  48.0 0.0 copy-done.9
  48.0 0.0 copy-done.11
  48.0 1.8 %fusion.5.turn_ref = bf16[256,384]{1,0:T(8,128)(2,1)S(1)} fusion(s32[256]{0:T(256)S(1)} %copy-done.10, s32[384]{0:T(512)S(1)} %copy-done.8, s32[256]{0:T(256)S(1)} %mul.70, s32[384]{0:T(512)S(1)} %copy-done.9, s32[384]{0:T(512)S(1)} %copy-done.7, s32[256]{0:T(256)S(1)} %copy-done.11), kind=kLoop, calls=%fused_computation.11 | loop fusion | flops 1966080 | bytes 204288 | tf_op jit(solution)/shard_map/convert_element_type | solution.py:86
  49.8 5.0 %all-to-all-done.2 = bf16[16,8,640]{2,1,0:T(8,128)(2,1)S(1)} async-done(((bf16[16,8,640]{2,1,0:T(8,128)(2,1)}), bf16[16,8,640]{2,1,0:T(8,128)(2,1)S(1)}, u32[]{:S(2)}, u32[]{:S(2)}) %all-to-all-start.2) | async-done | bytes 163872 | tf_op jit(solution)/shard_map/all_to_all | solution.py:441
  54.8 0.0 copy-done.5
  54.8 1.0 %adjoint.1 = (bf16[128,384]{1,0:T(8,128)(2,1)}, f32[64,64]{1,0:T(8,128)}) custom-call(bf16[256,384]{1,0:T(8,128)(2,1)S(1)} %fusion.5.turn_ref, bf16[128,640]{1,0:T(8,128)(2,1)S(1)} %bitcast.17, bf16[64,128]{1,0:T(8,128)(2,1)S(1)} %copy-done.5), custom_call_target="tpu_custom_call" | custom-call | flops 37748736 | bytes 491520 | tf_op jit(solution)/shard_map/adjoint/pallas_call | solution.py:430
  55.8 3.5 %all-to-all-start.3 = ((bf16[16,8,384]{2,1,0:T(8,128)(2,1)}), bf16[16,8,384]{2,1,0:T(8,128)(2,1)S(1)}, u32[]{:S(2)}, u32[]{:S(2)}) async-start(bf16[16,8,384]{2,1,0:T(8,128)(2,1)} %bitcast.8), calls=%async_computation.3 | async-start | bytes 196608 | tf_op jit(solution)/shard_map/all_to_all | solution.py:441
  59.3 0.0 collective-permute-done.1.refs_1_
  59.3 5.3 %outer.1 = f32[3,48,64,128]{3,2,1,0:T(8,128)} custom-call(bf16[384,384]{1,0:T(8,128)(2,1)S(1)} %bitcast.14, bf16[384,384]{1,0:T(8,128)(2,1)S(1)} %collective-permute-done.1.refs_1_), custom_call_target="tpu_custom_call" | custom-call | flops 37748736 | bytes 5308416 | tf_op jit(solution)/shard_map/outer/pallas_call | solution.py:430
  64.6 2.0 %all-to-all-done.3 = bf16[16,8,384]{2,1,0:T(8,128)(2,1)S(1)} async-done(((bf16[16,8,384]{2,1,0:T(8,128)(2,1)}), bf16[16,8,384]{2,1,0:T(8,128)(2,1)S(1)}, u32[]{:S(2)}, u32[]{:S(2)}) %all-to-all-start.3) | async-done | bytes 98336 | tf_op jit(solution)/shard_map/all_to_all | solution.py:441
  66.6 0.0 copy-done.3
  66.6 0.0 copy-done.4
  66.6 0.0 copy-done.6
  66.7 0.0 copy-done
  66.7 0.0 copy-done.2
  66.7 2.4 %spatial.1 = bf16[1,4,64,2048]{3,2,1,0:T(8,128)(2,1)} custom-call(s32[1,32]{1,0:T(1,128)S(1)} %copy-done.6, bf16[128,384]{1,0:T(8,128)(2,1)S(1)} %bitcast.18, bf16[128,128]{1,0:T(8,128)(2,1)S(1)} %copy-done.3, bf16[64,64]{1,0:T(8,128)(2,1)S(1)} %copy-done.4, bf16[192,2048]{1,0:T(8,128)(2,1)S(1)} %copy-done, bf16[256,2048]{1,0:T(8,128)(2,1)S(1)} %copy-done.2), custom_call_target="tpu_custom_call" | custom-call | flops 268435456 | bytes 3022976 | tf_op jit(solution)/shard_map/spatial/pallas_call | solution.py:430
  (1 shorter events, 0.0 us)
Async XLA Ops:
  0.6 47.3 %copy-start.7 = (s32[384]{0:T(512)S(1)}, s32[384]{0:T(512)}, u32[]{:S(2)}) copy-start(s32[384]{0:T(512)} %constant.62.clone) | copy-start | bytes 4612
  0.6 47.3 %copy-start.8 = (s32[384]{0:T(512)S(1)}, s32[384]{0:T(512)}, u32[]{:S(2)}) copy-start(s32[384]{0:T(512)} %constant.60.clone) | copy-start | bytes 4612
  0.7 47.3 %copy-start.10 = (s32[256]{0:T(256)S(1)}, s32[256]{0:T(256)}, u32[]{:S(2)}) copy-start(s32[256]{0:T(256)} %constant.74) | copy-start | bytes 3076
  0.7 47.3 %copy-start.9 = (s32[384]{0:T(512)S(1)}, s32[384]{0:T(512)}, u32[]{:S(2)}) copy-start(s32[384]{0:T(512)} %constant.64.clone) | copy-start | bytes 4612
  0.7 47.3 %copy-start.11 = (s32[256]{0:T(256)S(1)}, s32[256]{0:T(256)}, u32[]{:S(2)}) copy-start(s32[256]{0:T(256)} %constant.61.clone) | copy-start | bytes 3076
  0.7 54.1 %copy-start.5 = (bf16[64,128]{1,0:T(8,128)(2,1)S(1)}, bf16[64,128]{1,0:T(8,128)(2,1)}, u32[]{:S(2)}) copy-start(bf16[64,128]{1,0:T(8,128)(2,1)} %constant.67.clone.share_ref) | copy-start | bytes 49156
  6.8 16.9 %all-to-all-start = ((bf16[16,8,896]{2,1,0:T(8,128)(2,1)}), bf16[16,8,896]{2,1,0:T(8,128)(2,1)S(1)}, u32[]{:S(2)}, u32[]{:S(2)}) async-start(bf16[16,8,896]{2,1,0:T(8,128)(2,1)} %bitcast.20), calls=%async_computation | async-start | bytes 458752 | tf_op jit(solution)/shard_map/all_to_all | solution.py:441
  24.7 42.0 %copy-start.3 = (bf16[128,128]{1,0:T(8,128)(2,1)S(1)}, bf16[128,128]{1,0:T(8,128)(2,1)}, u32[]{:S(2)}) copy-start(bf16[128,128]{1,0:T(8,128)(2,1)} %constant.68.clone.back_ref) | copy-start | bytes 98308
  24.7 42.0 %copy-start.4 = (bf16[64,64]{1,0:T(8,128)(2,1)S(1)}, bf16[64,64]{1,0:T(8,128)(2,1)}, u32[]{:S(2)}) copy-start(bf16[64,64]{1,0:T(8,128)(2,1)} %w_ref.1) | copy-start | bytes 24580
  24.7 42.0 %copy-start.6 = (s32[1,32]{1,0:T(1,128)S(1)}, s32[1,32]{1,0:T(1,128)}, u32[]{:S(2)}) copy-start(s32[1,32]{1,0:T(1,128)} %ext_ref.3) | copy-start | bytes 388
  24.7 14.2 %all-to-all-start.1 = ((bf16[16,24,384]{2,1,0:T(8,128)(2,1)}), bf16[16,24,384]{2,1,0:T(8,128)(2,1)S(1)}, u32[]{:S(2)}, u32[]{:S(2)}) async-start(bf16[16,24,384]{2,1,0:T(8,128)(2,1)} %bitcast.3), calls=%async_computation.1 | async-start | bytes 589824 | tf_op jit(solution)/shard_map/all_to_all | solution.py:441
  28.4 38.3 %copy-start = (bf16[192,2048]{1,0:T(8,128)(2,1)S(1)}, bf16[192,2048]{1,0:T(8,128)(2,1)}, u32[]{:S(2)}) copy-start(bf16[192,2048]{1,0:T(8,128)(2,1)} %constant.57.clone.tab_hbm.tab_ref) | copy-start | bytes 2359300
  28.4 3.7 %collective-permute-start = (f32[8,128]{1,0:T(8,128)S(1)}, f32[8,128]{1,0:T(8,128)S(1)}, u32[]{:S(2)}, u32[]{:S(2)}) collective-permute-start(f32[8,128]{1,0:T(8,128)S(1)} %get-tuple-element.10.refs_0_), channel_id=1, source_target_pairs={{0,16},{16,0},{1,17},{17,1},{2,18},{18,2},{3,19},{19,3},{4,20},{20... | collective-permute-start | bytes 12296 | tf_op jit(solution)/shard_map/ppermute | solution.py:448
  38.9 1.7 %copy-start.1 = (bf16[144,64,128]{2,1,0:T(8,128)(2,1)S(1)}, bf16[144,64,128]{2,1,0:T(8,128)(2,1)}, u32[]{:S(2)}) copy-start(bf16[144,64,128]{2,1,0:T(8,128)(2,1)} %param.27) | copy-start | bytes 7077892
  40.5 26.1 %copy-start.2 = (bf16[256,2048]{1,0:T(8,128)(2,1)S(1)}, bf16[256,2048]{1,0:T(8,128)(2,1)}, u32[]{:S(2)}) copy-start(bf16[256,2048]{1,0:T(8,128)(2,1)} %get-tuple-element.13.gp_ref) | copy-start | bytes 3145732
  42.9 11.9 %all-to-all-start.2 = ((bf16[16,8,640]{2,1,0:T(8,128)(2,1)}), bf16[16,8,640]{2,1,0:T(8,128)(2,1)S(1)}, u32[]{:S(2)}, u32[]{:S(2)}) async-start(bf16[16,8,640]{2,1,0:T(8,128)(2,1)} %bitcast.6), calls=%async_computation.2 | async-start | bytes 327680 | tf_op jit(solution)/shard_map/all_to_all | solution.py:441
  46.4 12.9 %collective-permute-start.1 = (bf16[384,384]{1,0:T(8,128)(2,1)S(1)}, bf16[384,384]{1,0:T(8,128)(2,1)S(1)}, u32[]{:S(2)}, u32[]{:S(2)}) collective-permute-start(bf16[384,384]{1,0:T(8,128)(2,1)S(1)} %bitcast.13), channel_id=1, source_target_pairs={{0,16},{16,0},{1,17},{17,1},{2,18},{18,2},{3,19},{19,3},{4,20},{20... | collective-permute-start | bytes 884744 | tf_op jit(solution)/shard_map/ppermute | solution.py:448
  55.8 10.9 %all-to-all-start.3 = ((bf16[16,8,384]{2,1,0:T(8,128)(2,1)}), bf16[16,8,384]{2,1,0:T(8,128)(2,1)S(1)}, u32[]{:S(2)}, u32[]{:S(2)}) async-start(bf16[16,8,384]{2,1,0:T(8,128)(2,1)} %bitcast.8), calls=%async_computation.3 | async-start | bytes 196608 | tf_op jit(solution)/shard_map/all_to_all | solution.py:441

commit v3 on v2

--- a/solution.py
+++ b/solution.py
@@ -15,6 +15,7 @@
 MODES = 96
 F32 = jnp.float32
 BF16 = jnp.bfloat16
+COLUMN_PARTS = 2
 
 
 class Plan:
@@ -61,12 +62,6 @@
     def gather_back(self):
         return self.spread().T
 
-    def share_out(self):
-        out = np.zeros((self.ranks * self.group, self.channels), np.float32)
-        for i in range(self.channels):
-            out[(i // self.share) * self.group + i % self.share, i] = 1.0
-        return out.astype(jnp.bfloat16)
-
     def share_in(self):
         out = np.zeros((self.channels, self.ranks * 8), np.float32)
         for i in range(self.channels):
@@ -109,88 +104,105 @@
     return forward, backward
 
 
-LOG_PEAK = math.log2(0.3989422804014327)
+LOG_PEAK = math.log2(2.0 * 0.3989422804014327)
 NT = (((1,), (1,)), ((), ()))
 TN = (((0,), (0,)), ((), ()))
 
 
-def mask_rows(extent, start, width, rows):
+def mask_rows(extent, start, width, rows, value=1.0):
     column = lax.broadcasted_iota(jnp.int32, (16, width), 1) + start
-    few = jnp.where(column < extent, 1.0, 0.0).astype(BF16)
+    few = jnp.where(column < extent, value, 0.0).astype(BF16)
     return jnp.concatenate([few] * (rows // 16), axis=0)
 
 
 def column_kernel(
-    plan, ext_ref, x_hbm, pre_hbm, cot_hbm, tab_hbm, spread_hbm, share_hbm, gp_hbm, out_ref,
-    x_ref, pre_ref, cot_ref, lines_ref, spread_ref, share_ref, stage_ref, in_sems, misc_sems,
+    plan, ext_hbm, x_hbm, pre_hbm, cot_hbm, tab_hbm, spread_hbm, gp_hbm, out_ref,
+    ext_ref, x_ref, pre_ref, cot_ref, lines_ref, tab_ref, spread_ref, stage_ref, in_sems,
+    out_sems, misc_sems,
 ):
     chans, ranks = plan.channels, plan.ranks
     slots = plan.local_rows // SLAB
     freqs = tab_hbm.shape[0]
+    side, part_width, width = SLAB * chans, plan.columns // COLUMN_PARTS, 256
     first = lax.axis_index("rows") * slots
-    loads, tables, saves = [], [], []
-    for slot in range(slots):
-        rows = pl.ds(slot * SLAB, SLAB)
-        loads.append(
-            [
-                pltpu.make_async_copy(src.at[0, rows], dst.at[slot], in_sems.at[slot, n])
-                for n, (src, dst) in enumerate(
-                    ((pre_hbm, pre_ref), (cot_hbm, cot_ref), (x_hbm, x_ref))
-                )
-            ]
+    units = [
+        (slot, begin) for slot in range(slots) for begin in range(0, plan.columns, part_width)
+    ]
+    loads = {}
+    for slot, begin in units:
+        rows, cols = pl.ds(slot * SLAB, SLAB), pl.ds(begin, part_width)
+        loads[slot, begin] = [
+            pltpu.make_async_copy(
+                src.at[0, rows, :, cols],
+                dst.at[slot, :, :, cols],
+                in_sems.at[slot, begin // part_width, n],
+            )
+            for n, (src, dst) in enumerate(
+                ((pre_hbm, pre_ref), (cot_hbm, cot_ref), (x_hbm, x_ref))
+            )
+        ]
+    table = pltpu.make_async_copy(tab_hbm, tab_ref, misc_sems.at[1])
+    saves = [
+        pltpu.make_async_copy(
+            lines_ref.at[slot, pl.ds(side, side)], gp_hbm.at[pl.ds(slot * side, side)],
+            out_sems.at[slot],
         )
-        tables.append(
-            pltpu.make_async_copy(tab_hbm, lines_ref.at[slot, pl.ds(0, freqs)], in_sems.at[slot, 3])
-        )
-        saves.append(
-            pltpu.make_async_copy(
-                lines_ref.at[slot, pl.ds(freqs + SLAB * chans, SLAB * chans)],
-                gp_hbm.at[pl.ds(slot * SLAB * chans, SLAB * chans)],
-                in_sems.at[slot, 4],
-            )
-        )
-    small = [
-        pltpu.make_async_copy(spread_hbm, spread_ref, misc_sems.at[0]),
-        pltpu.make_async_copy(share_hbm, share_ref, misc_sems.at[1]),
+        for slot in range(slots)
     ]
-    for slot in range(slots):
-        for copy in loads[slot]:
+    small = pltpu.make_async_copy(spread_hbm, spread_ref, misc_sems.at[0])
+    extents = pltpu.make_async_copy(ext_hbm, ext_ref, misc_sems.at[2])
+    extents.start()
+    for slot, begin in units:
+        for copy in loads[slot, begin]:
             copy.start()
-        tables[slot].start()
-    for copy in small:
-        copy.start()
-
-    width = 256
+        if (slot, begin) == units[COLUMN_PARTS - 1]:
+            table.start()
+    small.start()
     lane = lax.broadcasted_iota(jnp.int32, (freqs, plan.both), 1)
-    total = jnp.zeros((chans, chans), F32)
-    for slot in range(slots):
+
+    def prepare(slot, begin):
         extent = ext_ref[0, first + slot]
-        for copy in loads[slot]:
-            copy.wait()
-        for start in range(0, plan.columns, width):
+        for start in range(begin, begin + part_width, width):
             cols = slice(start, start + width)
-            live = mask_rows(extent, start, width, chans)
+            ones = mask_rows(extent, start, width, chans)
+            halves = mask_rows(extent, start, width, chans, 0.5)
             for row in range(SLAB):
                 value = pre_ref[slot, row, :, cols].astype(F32)
                 turned = value * 0.7071067811865476
                 bell = jnp.exp2(turned * turned * -1.4426950408889634 + LOG_PEAK)
-                slope = value * bell + (0.5 + 0.5 * lax.erf(turned))
-                cot = (cot_ref[slot, row, :, cols] * live).astype(F32)
-                base = freqs + row * chans
-                lines_ref[slot, base : base + chans, cols] = x_ref[slot, row, :, cols] * live
-                base += SLAB * chans
-                lines_ref[slot, base : base + chans, cols] = (cot * slope).astype(BF16)
+                slope = value * bell + (1.0 + lax.erf(turned))
+                half_cot = (cot_ref[slot, row, :, cols] * halves).astype(F32)
+                base = row * chans
+                lines_ref[slot, base : base + chans, cols] = x_ref[slot, row, :, cols] * ones
+                base += side
+                lines_ref[slot, base : base + chans, cols] = (half_cot * slope).astype(BF16)
+
+    def contract(slot):
+        return lax.dot_general(
+            tab_ref[...], lines_ref[slot], NT, preferred_element_type=F32
+        )
+
+    extents.wait()
+    sums_of = {}
+    for slot in range(slots):
+        begins = range(0, plan.columns, part_width)
+        if slot == 0:
+            for begin in begins:
+                for copy in loads[slot, begin]:
+                    copy.wait()
+                prepare(slot, begin)
+            table.wait()
+        else:
+            for begin in begins:
+                for copy in loads[slot, begin]:
+                    copy.wait()
+            for begin in begins:
+                prepare(slot, begin)
+            sums_of[slot - 1] = contract(slot - 1)
         saves[slot].start()
-        tables[slot].wait()
-        edge = freqs + SLAB * chans
-        sums = lax.dot_general(
-            lines_ref[slot, :edge], lines_ref[slot, freqs:], NT, preferred_element_type=F32
-        )
-        for row in range(SLAB):
-            base = freqs + row * chans
-            side = SLAB * chans + row * chans
-            total = total + sums[base : base + chans, side : side + chans]
-        inputs, grads = sums[:freqs, : plan.both], sums[:freqs, plan.both :]
+    sums_of[slots - 1] = contract(slots - 1)
+    for slot in range(slots):
+        inputs, grads = sums_of[slot][:, :side], sums_of[slot][:, side:]
         near = jnp.where(lane < chans, inputs, pltpu.roll(grads, chans, axis=1)).astype(BF16)
         far = jnp.where(lane < chans, pltpu.roll(inputs, chans, axis=1), grads).astype(BF16)
         for row, spec in enumerate((near, far)):
@@ -203,28 +215,34 @@
                         stage_ref[line : line + ranks, lanes : lanes + plan.both] = spec[
                             base : base + ranks
                         ]
-    for copy in small:
-        copy.wait()
-    wide = 2 * plan.half
-    out_ref[:, :wide] = jnp.dot(
-        spread_ref[...], stage_ref[...], preferred_element_type=F32
-    ).astype(BF16)
-    high = total.astype(BF16)
-    low = (total - high.astype(F32)).astype(BF16)
-    split = jnp.concatenate([high, low], axis=1)
-    out_ref[:, wide:] = jnp.dot(share_ref[...], split, preferred_element_type=F32).astype(BF16)
+    small.wait()
+    out_ref[...] = jnp.dot(spread_ref[...], stage_ref[...], preferred_element_type=F32).astype(BF16)
     for copy in saves:
         copy.wait()
 
 
-def row_kernel(plan, turn_ref, in_ref, out_ref, share_ref):
+def weight_kernel(x_ref, gp_ref, out_ref):
+    part = lax.dot_general(x_ref[0, 0], gp_ref[...], NT, preferred_element_type=F32)
+
+    @pl.when(pl.program_id(0) == 0)
+    def _():
+        out_ref[...] = part
+
+    @pl.when(pl.program_id(0) > 0)
+    def _():
+        out_ref[...] += part
+
+
+def in_two(total):
+    high = total.astype(BF16).astype(F32)
+    return high, (total - high).astype(BF16).astype(F32)
+
+
+def row_kernel(plan, turn_ref, in_ref, out_ref):
     half = plan.half
-    stacked = jnp.concatenate([in_ref[:, :half], in_ref[:, half : 2 * half]], axis=0)
+    stacked = jnp.concatenate([in_ref[:, :half], in_ref[:, half:]], axis=0)
     sums = jnp.dot(turn_ref[...], stacked, preferred_element_type=F32)
     out_ref[...] = (sums * plan.scale).astype(BF16)
-    pieces = in_ref[:, 2 * half :].astype(F32).reshape(plan.ranks, plan.group, plan.both)
-    summed = jnp.sum(pieces, axis=0)
-    share_ref[...] = summed + pltpu.roll(summed, plan.channels, axis=1)
 
 
 def out_pair(tile, chans):
@@ -256,79 +274,123 @@
 
 
 def mix_kernel(plan, samples, *refs):
-    share_refs, (in_ref, spec_ref, out_hbm, out_ref, sems) = refs[:samples], refs[samples:]
+    share_refs = refs[:samples]
+    in_ref, head_ref, rest_hbm, out_hbm, rest_ref, out_ref, last_ref, sems, spec_sems = refs[samples:]
     chans, both = plan.channels, plan.both
     total = share_refs[0][...]
     for ref in share_refs[1:]:
         total = total + ref[...]
-    total = total[:8, :]
-    high = total.astype(BF16).astype(F32)
-    low = pltpu.roll(total - high, plan.share, axis=0)
-    row = lax.broadcasted_iota(jnp.int32, total.shape, 0)
-    lane = lax.broadcasted_iota(jnp.int32, total.shape, 1)
-    zero = jnp.zeros_like(total)
-    shared = jnp.where(row < plan.share, high, jnp.where(row < 2 * plan.share, low, zero))
+    high, low = in_two(total)
+    lane = lax.broadcasted_iota(jnp.int32, (8, both), 1)
+    share = plan.share
     order = slot_order(plan)
-
-    def one_owner(owner):
-        blocks = {}
+    head = head_ref.shape[0]
+
+    def left_of(owner, step):
+        start = (owner * plan.steps + step) * 8
+        tiles = [
+            out_pair(in_ref[start : start + 8, p * both : (p + 1) * both].astype(F32), chans)
+            for p in range(plan.pairs)
+        ]
+        return jnp.concatenate(tiles, axis=0).astype(BF16)
+
+    def weights_of(base, count):
+        if base + count <= head:
+            return head_ref[base : base + count]
+        return rest_ref[base - head : base - head + count]
+
+    def put(owner, step, pair, piece):
+        value, held = piece
+        place = order.index((step, pair))
+        if held != place % 2:
+            value = pltpu.roll(value, chans, axis=1)
+        lanes = slice(place * chans, (place + 1) * chans)
+        half = slice((place % 2) * chans, (place % 2 + 1) * chans)
+        out_ref[owner * 8 : owner * 8 + 8, lanes] = value[:, half]
+
+    def mix_general(owner):
         for step in range(plan.steps):
-            start = (owner * plan.steps + step) * 8
-            left = [
-                out_pair(in_ref[start : start + 8, p * both : (p + 1) * both].astype(F32), chans)
-                for p in range(plan.pairs)
-            ]
-            if plan.exact:
-                base = (step * PA + owner * plan.pairs) * chans
-                right = spec_ref[base : base + plan.pairs * chans]
-                value = lax.dot_general(
-                    jnp.concatenate(left, axis=0).astype(BF16), right, NT,
-                    preferred_element_type=F32,
+            left = left_of(owner, step)
+            for p in range(plan.pairs):
+                place, ok = where_held(plan, owner, step, p, mode_offset(plan))
+                right = head_ref[pl.ds(pl.multiple_of(place * chans, chans), chans)]
+                piece = lax.dot_general(
+                    left[8 * p : 8 * p + 8], right, NT, preferred_element_type=F32
                 )
-                for p in range(plan.pairs):
-                    cols = slice((p // 2) * both, (p // 2) * both + both)
-                    piece = value[8 * p : 8 * p + 8]
-                    if (p // 2) * both + both > piece.shape[1]:
-                        piece = piece[:, (p // 2) * both :]
-                        piece = jnp.concatenate([piece, jnp.zeros_like(piece)], axis=1)
-                    else:
-                        piece = piece[:, cols]
-                    blocks[step, p] = (piece, p % 2)
-            else:
-                for p in range(plan.pairs):
-                    place, ok = where_held(plan, owner, step, p, mode_offset(plan))
-                    right = spec_ref[pl.ds(pl.multiple_of(place * chans, chans), chans)]
-                    piece = lax.dot_general(
-                        left[p].astype(BF16), right, NT, preferred_element_type=F32
-                    )
-                    piece = jnp.where(ok, piece, 0.0)
-                    blocks[step, p] = (jnp.concatenate([piece, piece], axis=1), 0)
-        places = [blocks[key] for key in order]
-        while len(places) % 2 == 0:
-            places.append((zero, 0))
-        places.append((shared, 0))
-
-        def at(block, side):
-            value, held = block
-            return value if held == side else pltpu.roll(value, chans, axis=1)
-
-        tiles = [
-            jnp.where(lane < chans, at(places[n], 0), at(places[n + 1], 1))
-            for n in range(0, len(places), 2)
-        ]
-        out_ref[owner * 8 : owner * 8 + 8, :] = jnp.concatenate(tiles, axis=1).astype(BF16)
-
+                piece = jnp.where(ok, piece, 0.0)
+                put(owner, step, p, (jnp.concatenate([piece, piece], axis=1), 0))
+
+    def mix_two(owners, step):
+        rows = 8 * plan.pairs
+        lefts, rights = [], []
+        for m, owner in enumerate(owners):
+            left = left_of(owner, step)
+            blank = jnp.zeros_like(left)
+            lefts.append(
+                jnp.concatenate([left if k == m else blank for k in range(len(owners))], axis=1)
+            )
+            base = (step * PA + owner * plan.pairs) * chans
+            rights.append(weights_of(base, plan.pairs * chans))
+        values = lax.dot_general(
+            jnp.concatenate(lefts, axis=0), jnp.concatenate(rights, axis=1), NT,
+            preferred_element_type=F32,
+        )
+        for m, owner in enumerate(owners):
+            for p in range(0, plan.pairs, 2):
+                piece = values[m * rows + 8 * p : m * rows + 8 * p + 8, (p // 2) * both :]
+                if p + 1 < plan.pairs:
+                    after = values[
+                        m * rows + 8 * p + 8 : m * rows + 8 * p + 16, (p // 2) * both :
+                    ]
+                    tile = jnp.where(lane < chans, piece[:, :both], after[:, :both])
+                    place = order.index((step, p)) * chans
+                    out_ref[owner * 8 : owner * 8 + 8, place : place + both] = tile
+                else:
+                    single = piece[:, :chans]
+                    put(owner, step, p, (jnp.concatenate([single, single], axis=1), 0))
+
+    loads = [
+        pltpu.make_async_copy(
+            rest_hbm.at[pl.ds(head + n * PA * chans, PA * chans)],
+            rest_ref.at[pl.ds(n * PA * chans, PA * chans)],
+            spec_sems.at[n],
+        )
+        for n in range(plan.steps - head // (PA * chans) if plan.exact else 0)
+    ]
+    for copy in loads:
+        copy.start()
+    places = out_ref.shape[1] // chans
+    for owner in range(plan.ranks):
+        lines = slice(owner * 8, owner * 8 + 8)
+        if places - 1 > len(order):
+            out_ref[lines, len(order) * chans : (places - 1) * chans] = jnp.zeros(
+                (8, (places - 1 - len(order)) * chans), F32
+            )
+        rows = slice(owner * share, (owner + 1) * share)
+        pieces = [high[rows], low[rows]]
+        if 2 * share < 8:
+            pieces.append(jnp.zeros((8 - 2 * share, chans), F32))
+        out_ref[lines, (places - 1) * chans :] = jnp.concatenate(pieces, axis=0)
+    if plan.exact:
+        for step in range(plan.steps):
+            if step >= plan.steps - len(loads):
+                loads[step - plan.steps + len(loads)].wait()
+            for owner in range(0, plan.ranks, 2):
+                mix_two(range(owner, min(owner + 2, plan.ranks)), step)
+    else:
+        for owner in range(plan.ranks):
+            mix_general(owner)
     chunks = sems.shape[0]
-    each = plan.ranks // chunks
-    copies = []
+    each = plan.ranks * 8 // chunks
+    saves = []
     for chunk in range(chunks):
-        for owner in range(chunk * each, (chunk + 1) * each):
-            one_owner(owner)
-        lines = pl.ds(chunk * each * 8, each * 8)
-        copy = pltpu.make_async_copy(out_ref.at[lines], out_hbm.at[lines], sems.at[chunk])
+        lines = slice(chunk * each, (chunk + 1) * each)
+        last_ref[lines] = out_ref[lines].astype(BF16)
+        span = pl.ds(chunk * each, each)
+        copy = pltpu.make_async_copy(last_ref.at[span], out_hbm.at[span], sems.at[chunk])
         copy.start()
-        copies.append(copy)
-    for copy in copies:
+        saves.append(copy)
+    for copy in saves:
         copy.wait()
 
 
@@ -365,7 +427,7 @@
     lax.fori_loop(0, owners, body, 0)
 
 
-def adjoint_kernel(plan, weight_scale, turn_ref, in_ref, share_ref, out_ref, gw_ref):
+def adjoint_kernel(plan, turn_ref, in_ref, out_ref):
     chans = plan.channels
     order = slot_order(plan)
     parts = []
@@ -381,26 +443,41 @@
     for pair in range(plan.pairs):
         cols = slice(pair * chans, (pair + 1) * chans)
         pieces += [real[:, cols], imag[:, cols]]
-    out_ref[...] = jnp.concatenate(pieces, axis=1).astype(BF16)
-    shared = in_ref[:, in_ref.shape[1] - chans :]
-    total = jnp.dot(share_ref[...], shared, preferred_element_type=F32)
-    gw_ref[...] = total * weight_scale
+    out_ref[:, : plan.half] = jnp.concatenate(pieces, axis=1).astype(BF16)
+    shared = in_ref[:, in_ref.shape[1] - chans :].astype(F32)
+    summed = jnp.sum(shared.reshape(plan.ranks, 8, chans), axis=0)
+    share = plan.share
+    high, low = in_two(summed[:share] + summed[share : 2 * share])
+    pieces = [high, low]
+    if 2 * share < 8:
+        pieces.append(jnp.zeros((8 - 2 * share, chans), F32))
+    block = jnp.concatenate(pieces, axis=0)
+    block = jnp.concatenate([block, jnp.zeros((8, plan.both - chans), F32)], axis=1)
+    out_ref[:, plan.half :] = jnp.concatenate([block] * plan.ranks, axis=0).astype(BF16)
 
 
 def spatial_kernel(
-    plan, step, ext_ref, in_ref, back_ref, w_ref, tab_ref, gp_ref, out_hbm, left_ref, out_ref, sems
+    plan, step, weight_scale, ext_hbm, in_ref, back_ref, share_ref, w_ref, tab_ref, gp_ref,
+    out_hbm, gw_hbm, ext_ref, left_ref, out_ref, gw_ref, sems, ext_sem, gw_sem,
 ):
     chans, rows = plan.channels, plan.local_rows
     block = 2 * plan.ranks
     slots = rows // SLAB
     first = lax.axis_index("rows") * slots
-    ordered = jnp.dot(back_ref[...], in_ref[...], preferred_element_type=F32)
+    extents = pltpu.make_async_copy(ext_hbm, ext_ref, ext_sem)
+    extents.start()
+    ordered = jnp.dot(back_ref[...], in_ref[:, : plan.half], preferred_element_type=F32)
     for row in range(rows):
         lines = ordered[row * block : (row + 1) * block]
         pieces = [lines[:, b * chans : (b + 1) * chans] for b in range(2 * plan.pairs)]
         stacked = jnp.concatenate(pieces, axis=0)
         left_ref[row * chans : (row + 1) * chans] = stacked.T.astype(BF16)
-    copies = []
+    shared = in_ref[:, plan.half : plan.half + chans]
+    total = jnp.dot(share_ref[...], shared, preferred_element_type=F32)
+    gw_ref[...] = total * weight_scale
+    copies = [pltpu.make_async_copy(gw_ref, gw_hbm, gw_sem)]
+    copies[0].start()
+    extents.wait()
     for n in range(plan.columns // step):
         cols = slice(n * step, (n + 1) * step)
         spatial = jnp.dot(left_ref[...], tab_ref[:, cols], preferred_element_type=F32)
@@ -437,6 +514,10 @@
     )(*args)
 
 
+def stay(value):
+    return pltpu.with_memory_space_constraint(value, pltpu.HBM)
+
+
 def exchange(value):
     return lax.all_to_all(value, "rows", split_axis=0, concat_axis=0, tiled=True)
 
@@ -456,12 +537,11 @@
     plan = Plan(lax.axis_size("rows"), local_rows, chans, columns, spectral.shape[0])
     ranks, active = plan.ranks, slab_ids.shape[1]
     sds = jax.ShapeDtypeStruct
-    smem = pl.BlockSpec(memory_space=pltpu.SMEM)
     table = jnp.asarray(plan.column_table())
     forward_turn, backward_turn = turn_tables(plan, slab_ids[0])
 
-    spread, share_out = jnp.asarray(plan.spread()), jnp.asarray(plan.share_out())
-    lines, wide = ranks * plan.group, 2 * plan.half + plan.both
+    spread = jnp.asarray(plan.spread())
+    lines, wide = ranks * plan.group, 2 * plan.half
     slots = local_rows // SLAB
     freqs = table.shape[0]
     hbm = pl.BlockSpec(memory_space=pltpu.HBM)
@@ -469,40 +549,56 @@
     stored = (slots, SLAB, chans, columns)
     grad_pre, sent = call(
         functools.partial(column_kernel, plan),
-        (extents, layer_input, pre_activation, cotangent, table, spread, share_out),
+        (extents, layer_input, pre_activation, cotangent, table, spread),
         (sds((local_rows * chans, columns), BF16), sds((lines, wide), BF16)),
         "columns",
         2 * local_rows * 2 * chans * columns * 2 * MODES,
         62,
-        in_specs=[smem] + [hbm] * 6,
+        in_specs=[hbm] * 6,
         out_specs=(hbm, vmem),
         scratch_shapes=[
+            pltpu.SMEM(extents.shape, jnp.int32),
             pltpu.VMEM(stored, BF16),
             pltpu.VMEM(stored, BF16),
             pltpu.VMEM(stored, BF16),
-            pltpu.VMEM((slots, freqs + 2 * SLAB * chans, columns), BF16),
+            pltpu.VMEM((slots, 2 * SLAB * chans, columns), BF16),
+            pltpu.VMEM(table.shape, BF16),
             pltpu.VMEM(spread.shape, BF16),
-            pltpu.VMEM(share_out.shape, BF16),
             pltpu.VMEM((plan.group * ranks, 2 * plan.half), BF16),
-            pltpu.SemaphoreType.DMA((slots, 5)),
-            pltpu.SemaphoreType.DMA((2,)),
+            pltpu.SemaphoreType.DMA((slots, COLUMN_PARTS, 3)),
+            pltpu.SemaphoreType.DMA((slots,)),
+            pltpu.SemaphoreType.DMA((3,)),
         ],
     )
     received = exchange(sent)
+    local_weight = call(
+        weight_kernel,
+        (stay(layer_input), stay(grad_pre)),
+        (sds((chans, chans), F32),),
+        "weights",
+        2 * layer_input.size * chans,
+        16,
+        grid=(local_rows,),
+        in_specs=[
+            pl.BlockSpec((1, 1, chans, columns), lambda r: (0, r, 0, 0)),
+            pl.BlockSpec((chans, columns), lambda r: (r, 0)),
+        ],
+        out_specs=(pl.BlockSpec((chans, chans), lambda r: (0, 0)),),
+    )[0]
+    shares = every_sample(local_weight, samples)
+    if samples > 2:
+        shares = [sum(shares[1:], shares[0])]
 
     mode_lines = ranks * plan.steps * 8
-    sent, weight_share = call(
+    sent = call(
         functools.partial(row_kernel, plan),
         (forward_turn, received),
-        (sds((mode_lines, plan.half), BF16), sds((plan.group, plan.both), F32)),
+        (sds((mode_lines, plan.half), BF16),),
         "rows",
         2 * forward_turn.size * plan.half,
         16,
-    )
+    )[0]
     modes = exchange(sent)
-    shares = every_sample(weight_share, samples)
-    if samples > 2:
-        shares = [sum(shares[1:], shares[0])]
 
     chunks = 4 if plan.exact and ranks % 4 == 0 else 1
     owners = ranks // chunks
@@ -516,17 +612,25 @@
     mode_block = pl.BlockSpec((owners * plan.steps * 8, plan.half), lambda n: (n, 0))
     mixed = plan.steps * plan.pairs
     back_width = -(-(mixed + 1) // 2) * plan.both
+    flat = spectral.reshape(-1, plan.both)
+    resident = max(plan.steps - 1, 1)
+    head = resident * PA * chans if plan.exact else flat.shape[0]
     sent = call(
         functools.partial(mix_kernel, plan, len(shares)),
-        (*shares, modes, spectral.reshape(-1, plan.both)),
+        (*shares, modes, flat[:head], stay(flat)),
         (sds((ranks * 8, back_width), BF16),),
         "mix",
         16 * spectral.size,
         16,
-        in_specs=[vmem] * (len(shares) + 2),
+        in_specs=[vmem] * (len(shares) + 2) + [hbm],
         out_specs=(hbm,),
-        scratch_shapes=[pltpu.VMEM((ranks * 8, back_width), BF16)]
-        + [pltpu.SemaphoreType.DMA((chunks,))],
+        scratch_shapes=[
+            pltpu.VMEM((max(flat.shape[0] - head, 8), plan.both), BF16),
+            pltpu.VMEM((ranks * 8, back_width), F32),
+            pltpu.VMEM((ranks * 8, back_width), BF16),
+            pltpu.SemaphoreType.DMA((chunks,)),
+            pltpu.SemaphoreType.DMA((plan.steps,)),
+        ],
     )[0]
     returned = exchange(sent)
 
@@ -544,34 +648,37 @@
     )[0].reshape(spectral.shape)
 
     weight_scale = 1.0 / math.sqrt(samples * active * SLAB * columns)
-    share_in = jnp.asarray(plan.share_in())
-    sent, grad_weight = call(
-        functools.partial(adjoint_kernel, plan, weight_scale),
-        (backward_turn, returned, share_in),
-        (sds((lines, plan.half), BF16), sds((chans, chans), F32)),
+    sent = call(
+        functools.partial(adjoint_kernel, plan),
+        (backward_turn, returned),
+        (sds((lines, plan.half + plan.both), BF16),),
         "adjoint",
         2 * backward_turn.size * plan.pairs * chans,
         16,
-    )
+    )[0]
     local_back = exchange(sent)
 
     step = 512
-    gather_back = jnp.asarray(plan.gather_back())
-    grad_input = call(
-        functools.partial(spatial_kernel, plan, step),
-        (extents, local_back, gather_back, weight, table, grad_pre),
-        (sds(layer_input.shape, BF16),),
+    gather_back, share_in = jnp.asarray(plan.gather_back()), jnp.asarray(plan.share_in())
+    grad_input, grad_weight = call(
+        functools.partial(spatial_kernel, plan, step, weight_scale),
+        (extents, local_back, gather_back, share_in, weight, table, grad_pre),
+        (sds(layer_input.shape, BF16), sds((chans, chans), F32)),
         "spatial",
         2 * local_rows * chans * columns * (table.shape[0] + chans),
         16,
-        in_specs=[smem] + [vmem] * 5,
-        out_specs=(hbm,),
+        in_specs=[hbm] + [vmem] * 6,
+        out_specs=(hbm, hbm),
         scratch_shapes=[
+            pltpu.SMEM(extents.shape, jnp.int32),
             pltpu.VMEM((local_rows * chans, table.shape[0]), BF16),
             pltpu.VMEM((local_rows, chans, columns), BF16),
+            pltpu.VMEM((chans, chans), F32),
             pltpu.SemaphoreType.DMA((columns // step,)),
+            pltpu.SemaphoreType.DMA,
+            pltpu.SemaphoreType.DMA,
         ],
-    )[0]
+    )
     return (grad_input, grad_spectral, grad_weight)
 
 

time: 69.8 us -> 66.3 us (0.950)
  waiting for transfers between devices: 21 us -> 18.7 us
  other arithmetic: 5.9 us -> 3.78 us
  Pallas kernels: 18.1 us -> 19.4 us
    unnamed x24 -> x32, local copies, waits for them, and re-layouts: 1.73 us -> 0.1 us
    slice x0 -> x1, local copies, waits for them, and re-layouts: none -> 1.53 us  [shards(): flat[:head]]
    pallas_call x6 -> x7, Pallas kernels: 18.1 us -> 19.4 us  [call(): pl.pallas_call(body, out_shape=outs, name=name, cost_estimate=pl.CostEsti...]
    ppermute x2, waiting for transfers between devices: 2.11 us -> 0.9 us  [every_sample(): return [value, lax.ppermute(value, 'batch', [(0, 1), (1, 0)])]]
    all_to_all x4, waiting for transfers between devices: 18.9 us -> 17.8 us  [exchange(): lax.all_to_all(value, 'rows', split_axis=0, concat_axis=0, tiled=True)]
    convert_element_type x2, other arithmetic: 4.46 us -> 3.71 us  [turn_table(): return jnp.where(mo == ro, value, 0.0).astype(BF16)]
    add x1, other arithmetic: 0.79 us -> 0.07 us  [turn_tables(): jnp.repeat(slab_list, SLAB) * SLAB]
  transfers between devices with their start and end apart: 6 -> 6, of which waited for: 5 -> 5; matrix products, arithmetic and copies ran while one was open for 9% -> 9% of each run, Pallas kernels for 9% -> 14%
where the time goes in v3:
time: 66.3 us; the launch traced here: 65.8 us
  starting transfers between devices  21.1 us (32%)
  Pallas kernels  19.4 us (29%)
  waiting for transfers between devices  18.7 us (28%)
  other arithmetic  3.78 us (6%)
  local copies, waits for them, and re-layouts  1.95 us (3%)
  between operations  0.92 us (1%)
    pallas_call x7, Pallas kernels, call(): pl.pallas_call(body, out_shape=outs, name=name, cost_estimate=pl.CostEsti...  19.4 us
    all_to_all x4, starting transfers between devices, exchange(): lax.all_to_all(value, 'rows', split_axis=0, concat_axis=0, tiled=True)  18 us
    all_to_all x4, waiting for transfers between devices, exchange(): lax.all_to_all(value, 'rows', split_axis=0, concat_axis=0, tiled=True)  17.8 us
    convert_element_type x2, other arithmetic, turn_table(): return jnp.where(mo == ro, value, 0.0).astype(BF16)  3.71 us
    ppermute x2, starting transfers between devices, every_sample(): return [value, lax.ppermute(value, 'batch', [(0, 1), (1, 0)])]  3.11 us
    slice x1, local copies, waits for them, and re-layouts, shards(): flat[:head]  1.53 us
  transfers between devices with their start and end apart: 6, of which 5 were waited for; matrix products, arithmetic and copies ran while one was open for 9% of the time, Pallas kernels for 14%

profile of v3, /device:TPU:0, one launch (start us, length us, event | category | flops | bytes accessed | tf_op | source)
XLA Modules:
  0.0 65.8 jit_solution(14383835053014040637)
XLA Ops:
  0.6 0.0 copy-start.6
  0.6 0.0 copy-start.7
  0.7 0.0 copy-start.8
  0.7 0.0 copy-start.13
  0.7 0.0 copy-start.14
  0.7 0.0 copy-start.10
  0.7 0.0 copy-start.15
  0.7 4.4 %columns.1 = (bf16[256,2048]{1,0:T(8,128)(2,1)}, bf16[128,768]{1,0:T(8,128)(2,1)}) custom-call(s32[1,32]{1,0:T(1,128)} %ext_hbm.3, bf16[1,4,64,2048]{3,2,1,0:T(8,128)(2,1)} %x_ref.1, bf16[1,4,64,2048]{3,2,1,0:T(8,128)(2,1)} %pre_hbm.1, bf16[1,4,64,2048]{3,2,1,0:T(8,128)(2,1)} %cot_hbm.1, bf16[192,2048]{1,0:T(8,128)(2,1)} %constant.55.clone.tab_hbm.tab_ref, ...), custom_call_target="tpu_custom_call" | custom-call | flops 402653184 | bytes 5210240 | tf_op jit(solution)/shard_map/columns/pallas_call | solution.py:507
  5.1 7.4 %all-to-all-start = ((bf16[16,8,768]{2,1,0:T(8,128)(2,1)}), bf16[16,8,768]{2,1,0:T(8,128)(2,1)S(1)}, u32[]{:S(2)}, u32[]{:S(2)}) async-start(bf16[16,8,768]{2,1,0:T(8,128)(2,1)} %bitcast.22), calls=%async_computation | async-start | bytes 393216 | tf_op jit(solution)/shard_map/all_to_all | solution.py:522
  12.6 0.0 copy-done.15
  12.6 0.0 copy-done.6
  12.6 0.1 broadcast_add_fusion
  12.7 0.1 reshape.42
  12.8 0.1 transpose.16
  12.8 0.1 mul.70
  13.0 0.0 copy-done.7
  13.0 0.0 copy-done.8
  13.0 0.0 copy-done.13
  13.0 0.0 copy-done.14
  13.0 0.0 copy-done.10
  13.1 1.9 %fusion.11.turn_ref = bf16[384,256]{1,0:T(8,128)(2,1)S(1)} fusion(s32[256]{0:T(256)S(1)} %copy-done.13, s32[384]{0:T(512)S(1)} %copy-done.8, s32[256]{0:T(256)S(1)} %mul.70, s32[384]{0:T(512)S(1)} %copy-done.10, s32[256]{0:T(256)S(1)} %copy-done.14, s32[384]{0:T(512)S(1)} %copy-done.7), kind=kLoop, calls=%fused_computation.17 | loop fusion | flops 1966080 | bytes 204288 | tf_op jit(solution)/shard_map/convert_element_type | solution.py:81
  15.0 6.6 %all-to-all-done = bf16[16,8,768]{2,1,0:T(8,128)(2,1)S(1)} async-done(((bf16[16,8,768]{2,1,0:T(8,128)(2,1)}), bf16[16,8,768]{2,1,0:T(8,128)(2,1)S(1)}, u32[]{:S(2)}, u32[]{:S(2)}) %all-to-all-start) | async-done | bytes 196640 | tf_op jit(solution)/shard_map/all_to_all | solution.py:522
  21.5 1.0 %rows.1 = bf16[384,384]{1,0:T(8,128)(2,1)} custom-call(bf16[384,256]{1,0:T(8,128)(2,1)S(1)} %fusion.11.turn_ref, bf16[128,768]{1,0:T(8,128)(2,1)S(1)} %bitcast.17), custom_call_target="tpu_custom_call" | custom-call | flops 75497472 | bytes 688128 | tf_op jit(solution)/shard_map/rows/pallas_call | solution.py:507
  22.5 3.5 %all-to-all-start.1 = ((bf16[16,24,384]{2,1,0:T(8,128)(2,1)}), bf16[16,24,384]{2,1,0:T(8,128)(2,1)S(1)}, u32[]{:S(2)}, u32[]{:S(2)}) async-start(bf16[16,24,384]{2,1,0:T(8,128)(2,1)} %bitcast.3), calls=%async_computation.1 | async-start | bytes 589824 | tf_op jit(solution)/shard_map/all_to_all | solution.py:522
  26.0 2.8 %weights.1.refs_0_ = f32[64,64]{1,0:T(8,128)S(1)} custom-call(bf16[1,4,64,2048]{3,2,1,0:T(8,128)(2,1)} %x_ref.1, bf16[256,2048]{1,0:T(8,128)(2,1)} %get-tuple-element.7.gp_ref), custom_call_target="tpu_custom_call" | custom-call | flops 67108864 | bytes 2113536 | tf_op jit(solution)/shard_map/weights/pallas_call | solution.py:507
  28.9 1.6 %collective-permute-start = (f32[64,64]{1,0:T(8,128)S(1)}, f32[64,64]{1,0:T(8,128)S(1)}, u32[]{:S(2)}, u32[]{:S(2)}) collective-permute-start(f32[64,64]{1,0:T(8,128)S(1)} %weights.1.refs_0_), channel_id=1, source_target_pairs={{0,16},{16,0},{1,17},{17,1},{2,18},{18,2},{3,19},{19,3},{4,20},{20... | collective-permute-start | bytes 49160 | tf_op jit(solution)/shard_map/ppermute | solution.py:529
  30.4 1.5 %slice.6 = bf16[96,64,128]{2,1,0:T(8,128)(2,1)S(1)} slice(bf16[144,64,128]{2,1,0:T(8,128)(2,1)} %param.26), slice={[0:96], [0:64], [0:128]} | slice | bytes 3145728 | tf_op jit(solution)/shard_map/slice | solution.py:620
  31.9 0.9 %collective-permute-done.refs_1_ = f32[64,64]{1,0:T(8,128)S(1)} collective-permute-done((f32[64,64]{1,0:T(8,128)S(1)}, f32[64,64]{1,0:T(8,128)S(1)}, u32[]{:S(2)}, u32[]{:S(2)}) %collective-permute-start) | collective-permute-done | bytes 16416 | tf_op jit(solution)/shard_map/ppermute | solution.py:529
  32.8 3.7 %all-to-all-done.1 = bf16[16,24,384]{2,1,0:T(8,128)(2,1)S(1)} async-done(((bf16[16,24,384]{2,1,0:T(8,128)(2,1)}), bf16[16,24,384]{2,1,0:T(8,128)(2,1)S(1)}, u32[]{:S(2)}, u32[]{:S(2)}) %all-to-all-start.1) | async-done | bytes 294944 | tf_op jit(solution)/shard_map/all_to_all | solution.py:522
  36.6 2.8 %mix.1 = bf16[128,640]{1,0:T(8,128)(2,1)} custom-call(f32[64,64]{1,0:T(8,128)S(1)} %weights.1.refs_0_, f32[64,64]{1,0:T(8,128)S(1)} %collective-permute-done.refs_1_, bf16[384,384]{1,0:T(8,128)(2,1)S(1)} %bitcast.14, bf16[6144,128]{1,0:T(8,128)(2,1)S(1)} %bitcast.13, bf16[9216,128]{1,0:T(8,128)(2,1)} %bitcast.20), custom_call_target="tpu_custom_call" | custom-call | flops 18874368 | bytes 4423680 | tf_op jit(solution)/shard_map/mix/pallas_call | solution.py:507
  39.4 3.5 %all-to-all-start.2 = ((bf16[16,8,640]{2,1,0:T(8,128)(2,1)}), bf16[16,8,640]{2,1,0:T(8,128)(2,1)S(1)}, u32[]{:S(2)}, u32[]{:S(2)}) async-start(bf16[16,8,640]{2,1,0:T(8,128)(2,1)} %bitcast.7), calls=%async_computation.2 | async-start | bytes 327680 | tf_op jit(solution)/shard_map/all_to_all | solution.py:522
  42.9 1.6 %collective-permute-start.1 = (bf16[384,384]{1,0:T(8,128)(2,1)S(1)}, bf16[384,384]{1,0:T(8,128)(2,1)S(1)}, u32[]{:S(2)}, u32[]{:S(2)}) collective-permute-start(bf16[384,384]{1,0:T(8,128)(2,1)S(1)} %bitcast.15), channel_id=1, source_target_pairs={{0,16},{16,0},{1,17},{17,1},{2,18},{18,2},{3,19},{19,3},{4,20},{20... | collective-permute-start | bytes 884744 | tf_op jit(solution)/shard_map/ppermute | solution.py:529
  44.5 0.0 copy-done.9
  44.5 0.0 copy-done.12
  44.5 1.8 %fusion.5.turn_ref = bf16[256,384]{1,0:T(8,128)(2,1)S(1)} fusion(s32[256]{0:T(256)S(1)} %copy-done.11, s32[384]{0:T(512)S(1)} %copy-done.8, s32[256]{0:T(256)S(1)} %mul.70, s32[384]{0:T(512)S(1)} %copy-done.9, s32[384]{0:T(512)S(1)} %copy-done.7, s32[256]{0:T(256)S(1)} %copy-done.12), kind=kLoop, calls=%fused_computation.11 | loop fusion | flops 1966080 | bytes 204288 | tf_op jit(solution)/shard_map/convert_element_type | solution.py:81
  46.3 5.0 %all-to-all-done.2 = bf16[16,8,640]{2,1,0:T(8,128)(2,1)S(1)} async-done(((bf16[16,8,640]{2,1,0:T(8,128)(2,1)}), bf16[16,8,640]{2,1,0:T(8,128)(2,1)S(1)}, u32[]{:S(2)}, u32[]{:S(2)}) %all-to-all-start.2) | async-done | bytes 163872 | tf_op jit(solution)/shard_map/all_to_all | solution.py:522
  51.3 1.0 %adjoint.1 = bf16[128,512]{1,0:T(8,128)(2,1)} custom-call(bf16[256,384]{1,0:T(8,128)(2,1)S(1)} %fusion.5.turn_ref, bf16[128,640]{1,0:T(8,128)(2,1)S(1)} %bitcast.18), custom_call_target="tpu_custom_call" | custom-call | flops 37748736 | bytes 491520 | tf_op jit(solution)/shard_map/adjoint/pallas_call | solution.py:507
  52.3 3.5 %all-to-all-start.3 = ((bf16[16,8,512]{2,1,0:T(8,128)(2,1)}), bf16[16,8,512]{2,1,0:T(8,128)(2,1)S(1)}, u32[]{:S(2)}, u32[]{:S(2)}) async-start(bf16[16,8,512]{2,1,0:T(8,128)(2,1)} %bitcast.9), calls=%async_computation.3 | async-start | bytes 262144 | tf_op jit(solution)/shard_map/all_to_all | solution.py:522
  55.8 0.0 copy-start
  55.8 0.0 copy-start.1
  55.8 0.0 copy-start.2
  55.9 0.0 copy-start.3
  55.9 0.0 copy-start.4
  55.9 0.0 copy-start.5
  55.9 0.0 collective-permute-done.1.refs_1_
  55.9 5.3 %outer.1 = f32[3,48,64,128]{3,2,1,0:T(8,128)} custom-call(bf16[384,384]{1,0:T(8,128)(2,1)S(1)} %bitcast.16, bf16[384,384]{1,0:T(8,128)(2,1)S(1)} %collective-permute-done.1.refs_1_), custom_call_target="tpu_custom_call" | custom-call | flops 37748736 | bytes 5308416 | tf_op jit(solution)/shard_map/outer/pallas_call | solution.py:507
  61.2 2.5 %all-to-all-done.3 = bf16[16,8,512]{2,1,0:T(8,128)(2,1)S(1)} async-done(((bf16[16,8,512]{2,1,0:T(8,128)(2,1)}), bf16[16,8,512]{2,1,0:T(8,128)(2,1)S(1)}, u32[]{:S(2)}, u32[]{:S(2)}) %all-to-all-start.3) | async-done | bytes 131104 | tf_op jit(solution)/shard_map/all_to_all | solution.py:522
  63.7 2.0 %spatial.1 = (bf16[1,4,64,2048]{3,2,1,0:T(8,128)(2,1)}, f32[64,64]{1,0:T(8,128)}) custom-call(s32[1,32]{1,0:T(1,128)S(1)} %copy-done.5, bf16[128,512]{1,0:T(8,128)(2,1)S(1)} %bitcast.19, bf16[128,128]{1,0:T(8,128)(2,1)S(1)} %copy-done.2, bf16[64,128]{1,0:T(8,128)(2,1)S(1)} %copy-done.4, bf16[64,64]{1,0:T(8,128)(2,1)S(1)} %copy-done.3, ...), custom_call_target="tpu_custom_call" | custom-call | flops 268435456 | bytes 3088512 | tf_op jit(solution)/shard_map/spatial/pallas_call | solution.py:507
  (11 shorter events, 0.0 us)
Async XLA Ops:
  0.6 12.0 %copy-start.6 = (s32[32,2]{1,0:T(8,128)S(1)}, s32[32,2]{1,0:T(8,128)}, u32[]{:S(2)}) copy-start(s32[32,2]{1,0:T(8,128)} %constant.73) | copy-start | bytes 772
  0.6 12.4 %copy-start.7 = (s32[384]{0:T(512)S(1)}, s32[384]{0:T(512)}, u32[]{:S(2)}) copy-start(s32[384]{0:T(512)} %constant.60.clone) | copy-start | bytes 4612
  0.7 12.4 %copy-start.8 = (s32[384]{0:T(512)S(1)}, s32[384]{0:T(512)}, u32[]{:S(2)}) copy-start(s32[384]{0:T(512)} %constant.58.clone) | copy-start | bytes 4612
  0.7 12.4 %copy-start.13 = (s32[256]{0:T(256)S(1)}, s32[256]{0:T(256)}, u32[]{:S(2)}) copy-start(s32[256]{0:T(256)} %constant.72) | copy-start | bytes 3076
  0.7 12.4 %copy-start.14 = (s32[256]{0:T(256)S(1)}, s32[256]{0:T(256)}, u32[]{:S(2)}) copy-start(s32[256]{0:T(256)} %constant.61.clone) | copy-start | bytes 3076
  0.7 12.3 %copy-start.10 = (s32[384]{0:T(512)S(1)}, s32[384]{0:T(512)}, u32[]{:S(2)}) copy-start(s32[384]{0:T(512)} %constant.57.clone) | copy-start | bytes 4612
  0.7 11.9 %copy-start.15 = (s32[1,32]{1,0:T(1,128)S(1)}, s32[1,32]{1,0:T(1,128)}, u32[]{:S(2)}) copy-start(s32[1,32]{1,0:T(1,128)} %param.27) | copy-start | bytes 388
  5.1 16.4 %all-to-all-start = ((bf16[16,8,768]{2,1,0:T(8,128)(2,1)}), bf16[16,8,768]{2,1,0:T(8,128)(2,1)S(1)}, u32[]{:S(2)}, u32[]{:S(2)}) async-start(bf16[16,8,768]{2,1,0:T(8,128)(2,1)} %bitcast.22), calls=%async_computation | async-start | bytes 393216 | tf_op jit(solution)/shard_map/all_to_all | solution.py:522
  22.5 14.1 %all-to-all-start.1 = ((bf16[16,24,384]{2,1,0:T(8,128)(2,1)}), bf16[16,24,384]{2,1,0:T(8,128)(2,1)S(1)}, u32[]{:S(2)}, u32[]{:S(2)}) async-start(bf16[16,24,384]{2,1,0:T(8,128)(2,1)} %bitcast.3), calls=%async_computation.1 | async-start | bytes 589824 | tf_op jit(solution)/shard_map/all_to_all | solution.py:522
  28.9 4.0 %collective-permute-start = (f32[64,64]{1,0:T(8,128)S(1)}, f32[64,64]{1,0:T(8,128)S(1)}, u32[]{:S(2)}, u32[]{:S(2)}) collective-permute-start(f32[64,64]{1,0:T(8,128)S(1)} %weights.1.refs_0_), channel_id=1, source_target_pairs={{0,16},{16,0},{1,17},{17,1},{2,18},{18,2},{3,19},{19,3},{4,20},{20... | collective-permute-start | bytes 49160 | tf_op jit(solution)/shard_map/ppermute | solution.py:529
  36.6 7.9 %copy-start.9 = (s32[384]{0:T(512)S(1)}, s32[384]{0:T(512)}, u32[]{:S(2)}) copy-start(s32[384]{0:T(512)} %constant.62.clone) | copy-start | bytes 4612
  36.6 7.9 %copy-start.11 = (s32[256]{0:T(256)S(1)}, s32[256]{0:T(256)}, u32[]{:S(2)}) copy-start(s32[256]{0:T(256)} %constant.71) | copy-start | bytes 3076
  36.6 7.9 %copy-start.12 = (s32[256]{0:T(256)S(1)}, s32[256]{0:T(256)}, u32[]{:S(2)}) copy-start(s32[256]{0:T(256)} %constant.59.clone) | copy-start | bytes 3076
  39.4 11.9 %all-to-all-start.2 = ((bf16[16,8,640]{2,1,0:T(8,128)(2,1)}), bf16[16,8,640]{2,1,0:T(8,128)(2,1)S(1)}, u32[]{:S(2)}, u32[]{:S(2)}) async-start(bf16[16,8,640]{2,1,0:T(8,128)(2,1)} %bitcast.7), calls=%async_computation.2 | async-start | bytes 327680 | tf_op jit(solution)/shard_map/all_to_all | solution.py:522
  42.9 13.0 %collective-permute-start.1 = (bf16[384,384]{1,0:T(8,128)(2,1)S(1)}, bf16[384,384]{1,0:T(8,128)(2,1)S(1)}, u32[]{:S(2)}, u32[]{:S(2)}) collective-permute-start(bf16[384,384]{1,0:T(8,128)(2,1)S(1)} %bitcast.15), channel_id=1, source_target_pairs={{0,16},{16,0},{1,17},{17,1},{2,18},{18,2},{3,19},{19,3},{4,20},{20... | collective-permute-start | bytes 884744 | tf_op jit(solution)/shard_map/ppermute | solution.py:529
  52.3 11.4 %all-to-all-start.3 = ((bf16[16,8,512]{2,1,0:T(8,128)(2,1)}), bf16[16,8,512]{2,1,0:T(8,128)(2,1)S(1)}, u32[]{:S(2)}, u32[]{:S(2)}) async-start(bf16[16,8,512]{2,1,0:T(8,128)(2,1)} %bitcast.9), calls=%async_computation.3 | async-start | bytes 262144 | tf_op jit(solution)/shard_map/all_to_all | solution.py:522
  55.8 7.9 %copy-start = (bf16[256,2048]{1,0:T(8,128)(2,1)S(1)}, bf16[256,2048]{1,0:T(8,128)(2,1)}, u32[]{:S(2)}) copy-start(bf16[256,2048]{1,0:T(8,128)(2,1)} %get-tuple-element.7.gp_ref) | copy-start | bytes 3145732
  55.8 7.9 %copy-start.1 = (bf16[192,2048]{1,0:T(8,128)(2,1)S(1)}, bf16[192,2048]{1,0:T(8,128)(2,1)}, u32[]{:S(2)}) copy-start(bf16[192,2048]{1,0:T(8,128)(2,1)} %constant.55.clone.tab_hbm.tab_ref) | copy-start | bytes 2359300
  55.8 7.9 %copy-start.2 = (bf16[128,128]{1,0:T(8,128)(2,1)S(1)}, bf16[128,128]{1,0:T(8,128)(2,1)}, u32[]{:S(2)}) copy-start(bf16[128,128]{1,0:T(8,128)(2,1)} %constant.64.clone.back_ref) | copy-start | bytes 98308
  55.9 7.8 %copy-start.3 = (bf16[64,64]{1,0:T(8,128)(2,1)S(1)}, bf16[64,64]{1,0:T(8,128)(2,1)}, u32[]{:S(2)}) copy-start(bf16[64,64]{1,0:T(8,128)(2,1)} %w_ref.1) | copy-start | bytes 24580
  55.9 7.8 %copy-start.4 = (bf16[64,128]{1,0:T(8,128)(2,1)S(1)}, bf16[64,128]{1,0:T(8,128)(2,1)}, u32[]{:S(2)}) copy-start(bf16[64,128]{1,0:T(8,128)(2,1)} %constant.65.clone.share_ref) | copy-start | bytes 49156
  55.9 7.8 %copy-start.5 = (s32[1,32]{1,0:T(1,128)S(1)}, s32[1,32]{1,0:T(1,128)}, u32[]{:S(2)}) copy-start(s32[1,32]{1,0:T(1,128)} %ext_hbm.3) | copy-start | bytes 388

commit v4 on v3

--- a/solution.py
+++ b/solution.py
@@ -109,9 +109,9 @@
 TN = (((0,), (0,)), ((), ()))
 
 
-def mask_rows(extent, start, width, rows, value=1.0):
+def mask_rows(extent, start, width, rows):
     column = lax.broadcasted_iota(jnp.int32, (16, width), 1) + start
-    few = jnp.where(column < extent, value, 0.0).astype(BF16)
+    few = jnp.where(column < extent, 1.0, 0.0).astype(BF16)
     return jnp.concatenate([few] * (rows // 16), axis=0)
 
 
@@ -122,8 +122,7 @@
 ):
     chans, ranks = plan.channels, plan.ranks
     slots = plan.local_rows // SLAB
-    freqs = tab_hbm.shape[0]
-    side, part_width, width = SLAB * chans, plan.columns // COLUMN_PARTS, 256
+    part_width, width = plan.columns // COLUMN_PARTS, 256
     first = lax.axis_index("rows") * slots
     units = [
         (slot, begin) for slot in range(slots) for begin in range(0, plan.columns, part_width)
@@ -143,10 +142,14 @@
         ]
     table = pltpu.make_async_copy(tab_hbm, tab_ref, misc_sems.at[1])
     saves = [
-        pltpu.make_async_copy(
-            lines_ref.at[slot, pl.ds(side, side)], gp_hbm.at[pl.ds(slot * side, side)],
-            out_sems.at[slot],
-        )
+        [
+            pltpu.make_async_copy(
+                lines_ref.at[slot, pl.ds(row * plan.both + chans, chans)],
+                gp_hbm.at[pl.ds((slot * SLAB + row) * chans, chans)],
+                out_sems.at[slot, row],
+            )
+            for row in range(SLAB)
+        ]
         for slot in range(slots)
     ]
     small = pltpu.make_async_copy(spread_hbm, spread_ref, misc_sems.at[0])
@@ -158,23 +161,22 @@
         if (slot, begin) == units[COLUMN_PARTS - 1]:
             table.start()
     small.start()
-    lane = lax.broadcasted_iota(jnp.int32, (freqs, plan.both), 1)
 
     def prepare(slot, begin):
         extent = ext_ref[0, first + slot]
         for start in range(begin, begin + part_width, width):
             cols = slice(start, start + width)
             ones = mask_rows(extent, start, width, chans)
-            halves = mask_rows(extent, start, width, chans, 0.5)
+            halves = ones * BF16(0.5)
             for row in range(SLAB):
                 value = pre_ref[slot, row, :, cols].astype(F32)
                 turned = value * 0.7071067811865476
                 bell = jnp.exp2(turned * turned * -1.4426950408889634 + LOG_PEAK)
                 slope = value * bell + (1.0 + lax.erf(turned))
                 half_cot = (cot_ref[slot, row, :, cols] * halves).astype(F32)
-                base = row * chans
+                base = row * plan.both
                 lines_ref[slot, base : base + chans, cols] = x_ref[slot, row, :, cols] * ones
-                base += side
+                base += chans
                 lines_ref[slot, base : base + chans, cols] = (half_cot * slope).astype(BF16)
 
     def contract(slot):
@@ -199,13 +201,12 @@
             for begin in begins:
                 prepare(slot, begin)
             sums_of[slot - 1] = contract(slot - 1)
-        saves[slot].start()
+        for copy in saves[slot]:
+            copy.start()
     sums_of[slots - 1] = contract(slots - 1)
     for slot in range(slots):
-        inputs, grads = sums_of[slot][:, :side], sums_of[slot][:, side:]
-        near = jnp.where(lane < chans, inputs, pltpu.roll(grads, chans, axis=1)).astype(BF16)
-        far = jnp.where(lane < chans, pltpu.roll(inputs, chans, axis=1), grads).astype(BF16)
-        for row, spec in enumerate((near, far)):
+        for row in range(SLAB):
+            spec = sums_of[slot][:, row * plan.both : (row + 1) * plan.both].astype(BF16)
             for pair in range(plan.pairs):
                 for part in range(2):
                     for odd in range(2):
@@ -217,8 +218,9 @@
                         ]
     small.wait()
     out_ref[...] = jnp.dot(spread_ref[...], stage_ref[...], preferred_element_type=F32).astype(BF16)
-    for copy in saves:
-        copy.wait()
+    for copies in saves:
+        for copy in copies:
+            copy.wait()
 
 
 def weight_kernel(x_ref, gp_ref, out_ref):
@@ -275,7 +277,7 @@
 
 def mix_kernel(plan, samples, *refs):
     share_refs = refs[:samples]
-    in_ref, head_ref, rest_hbm, out_hbm, rest_ref, out_ref, last_ref, sems, spec_sems = refs[samples:]
+    in_ref, head_ref, rest_hbm, out_hbm, rest_ref, out_ref, last_ref, sems, spec_sem = refs[samples:]
     chans, both = plan.channels, plan.both
     total = share_refs[0][...]
     for ref in share_refs[1:]:
@@ -349,16 +351,10 @@
                     single = piece[:, :chans]
                     put(owner, step, p, (jnp.concatenate([single, single], axis=1), 0))
 
-    loads = [
-        pltpu.make_async_copy(
-            rest_hbm.at[pl.ds(head + n * PA * chans, PA * chans)],
-            rest_ref.at[pl.ds(n * PA * chans, PA * chans)],
-            spec_sems.at[n],
-        )
-        for n in range(plan.steps - head // (PA * chans) if plan.exact else 0)
-    ]
-    for copy in loads:
-        copy.start()
+    rest = plan.steps * PA * chans - head if plan.exact else 0
+    if rest:
+        load = pltpu.make_async_copy(rest_hbm.at[pl.ds(head, rest)], rest_ref, spec_sem)
+        load.start()
     places = out_ref.shape[1] // chans
     for owner in range(plan.ranks):
         lines = slice(owner * 8, owner * 8 + 8)
@@ -372,11 +368,15 @@
             pieces.append(jnp.zeros((8 - 2 * share, chans), F32))
         out_ref[lines, (places - 1) * chans :] = jnp.concatenate(pieces, axis=0)
     if plan.exact:
+        waited = rest == 0
         for step in range(plan.steps):
-            if step >= plan.steps - len(loads):
-                loads[step - plan.steps + len(loads)].wait()
             for owner in range(0, plan.ranks, 2):
-                mix_two(range(owner, min(owner + 2, plan.ranks)), step)
+                owners = range(owner, min(owner + 2, plan.ranks))
+                end = (step * PA + (owners[-1] + 1) * plan.pairs) * chans
+                if end > head and not waited:
+                    load.wait()
+                    waited = True
+                mix_two(owners, step)
     else:
         for owner in range(plan.ranks):
             mix_general(owner)
@@ -543,7 +543,7 @@
     spread = jnp.asarray(plan.spread())
     lines, wide = ranks * plan.group, 2 * plan.half
     slots = local_rows // SLAB
-    freqs = table.shape[0]
+
     hbm = pl.BlockSpec(memory_space=pltpu.HBM)
     vmem = pl.BlockSpec(memory_space=pltpu.VMEM)
     stored = (slots, SLAB, chans, columns)
@@ -566,7 +566,7 @@
             pltpu.VMEM(spread.shape, BF16),
             pltpu.VMEM((plan.group * ranks, 2 * plan.half), BF16),
             pltpu.SemaphoreType.DMA((slots, COLUMN_PARTS, 3)),
-            pltpu.SemaphoreType.DMA((slots,)),
+            pltpu.SemaphoreType.DMA((slots, SLAB)),
             pltpu.SemaphoreType.DMA((3,)),
         ],
     )
@@ -585,6 +585,7 @@
         ],
         out_specs=(pl.BlockSpec((chans, chans), lambda r: (0, 0)),),
     )[0]
+    received, local_weight = lax.optimization_barrier((received, local_weight))
     shares = every_sample(local_weight, samples)
     if samples > 2:
         shares = [sum(shares[1:], shares[0])]
@@ -613,8 +614,8 @@
     mixed = plan.steps * plan.pairs
     back_width = -(-(mixed + 1) // 2) * plan.both
     flat = spectral.reshape(-1, plan.both)
-    resident = max(plan.steps - 1, 1)
-    head = resident * PA * chans if plan.exact else flat.shape[0]
+    owners_two = ranks * plan.steps // 2
+    head = (5 * owners_two // 3) * plan.pairs * chans if plan.exact else flat.shape[0]
     sent = call(
         functools.partial(mix_kernel, plan, len(shares)),
         (*shares, modes, flat[:head], stay(flat)),
@@ -629,7 +630,7 @@
             pltpu.VMEM((ranks * 8, back_width), F32),
             pltpu.VMEM((ranks * 8, back_width), BF16),
             pltpu.SemaphoreType.DMA((chunks,)),
-            pltpu.SemaphoreType.DMA((plan.steps,)),
+            pltpu.SemaphoreType.DMA,
         ],
     )[0]
     returned = exchange(sent)

time: 66.3 us -> 66.1 us (level)
  no operation moved by 1% of the time
where the time goes in v4:
time: 66.1 us; the launch traced here: 65.5 us
  starting transfers between devices  21.1 us (32%)
  Pallas kernels  19.1 us (29%)
  waiting for transfers between devices  18.5 us (28%)
  other arithmetic  3.78 us (6%)
  local copies, waits for them, and re-layouts  2.12 us (3%)
  between operations  0.92 us (1%)
    pallas_call x7, Pallas kernels, call(): pl.pallas_call(body, out_shape=outs, name=name, cost_estimate=pl.CostEsti...  19.1 us
    all_to_all x4, starting transfers between devices, exchange(): lax.all_to_all(value, 'rows', split_axis=0, concat_axis=0, tiled=True)  18 us
    all_to_all x4, waiting for transfers between devices, exchange(): lax.all_to_all(value, 'rows', split_axis=0, concat_axis=0, tiled=True)  17.8 us
    convert_element_type x2, other arithmetic, turn_table(): return jnp.where(mo == ro, value, 0.0).astype(BF16)  3.71 us
    ppermute x2, starting transfers between devices, every_sample(): return [value, lax.ppermute(value, 'batch', [(0, 1), (1, 0)])]  3.11 us
    slice x1, local copies, waits for them, and re-layouts, shards(): flat[:head]  1.7 us
  transfers between devices with their start and end apart: 6, of which 5 were waited for; matrix products, arithmetic and copies ran while one was open for 9% of the time, Pallas kernels for 14%

profile of v4, /device:TPU:0, one launch (start us, length us, event | category | flops | bytes accessed | tf_op | source)
XLA Modules:
  0.0 65.5 jit_solution(5641431355499327270)
XLA Ops:
  0.6 0.0 copy-start.6
  0.6 0.0 copy-start.7
  0.7 0.0 copy-start.8
  0.7 0.0 copy-start.10
  0.7 0.0 copy-start.13
  0.7 0.0 copy-start.14
  0.7 0.0 copy-start.15
  0.7 4.4 %columns.1 = (bf16[256,2048]{1,0:T(8,128)(2,1)}, bf16[128,768]{1,0:T(8,128)(2,1)}) custom-call(s32[1,32]{1,0:T(1,128)} %ext_hbm.3, bf16[1,4,64,2048]{3,2,1,0:T(8,128)(2,1)} %x_ref.1, bf16[1,4,64,2048]{3,2,1,0:T(8,128)(2,1)} %pre_hbm.1, bf16[1,4,64,2048]{3,2,1,0:T(8,128)(2,1)} %cot_hbm.1, bf16[192,2048]{1,0:T(8,128)(2,1)} %constant.55.clone.tab_hbm.tab_ref, ...), custom_call_target="tpu_custom_call" | custom-call | flops 402653184 | bytes 5210240 | tf_op jit(solution)/shard_map/columns/pallas_call | solution.py:507
  5.1 7.4 %all-to-all-start = ((bf16[16,8,768]{2,1,0:T(8,128)(2,1)}), bf16[16,8,768]{2,1,0:T(8,128)(2,1)S(1)}, u32[]{:S(2)}, u32[]{:S(2)}) async-start(bf16[16,8,768]{2,1,0:T(8,128)(2,1)} %bitcast.22), calls=%async_computation | async-start | bytes 393216 | tf_op jit(solution)/shard_map/all_to_all | solution.py:522
  12.5 0.0 copy-done.15
  12.5 0.0 copy-done.6
  12.5 0.1 broadcast_add_fusion
  12.6 0.1 reshape.42
  12.7 0.1 transpose.16
  12.8 0.1 mul.70
  12.9 2.8 %weights.1.refs_0_ = f32[64,64]{1,0:T(8,128)S(1)} custom-call(bf16[1,4,64,2048]{3,2,1,0:T(8,128)(2,1)} %x_ref.1, bf16[256,2048]{1,0:T(8,128)(2,1)} %get-tuple-element.10.gp_ref), custom_call_target="tpu_custom_call" | custom-call | flops 67108864 | bytes 2113536 | tf_op jit(solution)/shard_map/weights/pallas_call | solution.py:507
  15.8 0.0 copy-done.7
  15.8 0.0 copy-done.8
  15.8 0.0 copy-done.10
  15.8 0.0 copy-done.13
  15.8 1.9 %fusion.11.turn_ref = bf16[384,256]{1,0:T(8,128)(2,1)S(1)} fusion(s32[256]{0:T(256)S(1)} %copy-done.13, s32[384]{0:T(512)S(1)} %copy-done.8, s32[256]{0:T(256)S(1)} %mul.70, s32[384]{0:T(512)S(1)} %copy-done.10, s32[256]{0:T(256)S(1)} %copy-done.14, s32[384]{0:T(512)S(1)} %copy-done.7), kind=kLoop, calls=%fused_computation.17 | loop fusion | flops 1966080 | bytes 204288 | tf_op jit(solution)/shard_map/convert_element_type | solution.py:81
  17.7 3.8 %all-to-all-done = bf16[16,8,768]{2,1,0:T(8,128)(2,1)S(1)} async-done(((bf16[16,8,768]{2,1,0:T(8,128)(2,1)}), bf16[16,8,768]{2,1,0:T(8,128)(2,1)S(1)}, u32[]{:S(2)}, u32[]{:S(2)}) %all-to-all-start) | async-done | bytes 196640 | tf_op jit(solution)/shard_map/all_to_all | solution.py:522
  21.5 1.0 %rows.1 = bf16[384,384]{1,0:T(8,128)(2,1)} custom-call(bf16[384,256]{1,0:T(8,128)(2,1)S(1)} %fusion.11.turn_ref, bf16[128,768]{1,0:T(8,128)(2,1)S(1)} %bitcast.17), custom_call_target="tpu_custom_call" | custom-call | flops 75497472 | bytes 688128 | tf_op jit(solution)/shard_map/rows/pallas_call | solution.py:507
  22.4 3.5 %all-to-all-start.1 = ((bf16[16,24,384]{2,1,0:T(8,128)(2,1)}), bf16[16,24,384]{2,1,0:T(8,128)(2,1)S(1)}, u32[]{:S(2)}, u32[]{:S(2)}) async-start(bf16[16,24,384]{2,1,0:T(8,128)(2,1)} %bitcast.3), calls=%async_computation.1 | async-start | bytes 589824 | tf_op jit(solution)/shard_map/all_to_all | solution.py:522
  26.0 1.6 %collective-permute-start = (f32[64,64]{1,0:T(8,128)S(1)}, f32[64,64]{1,0:T(8,128)S(1)}, u32[]{:S(2)}, u32[]{:S(2)}) collective-permute-start(f32[64,64]{1,0:T(8,128)S(1)} %weights.1.refs_0_), channel_id=1, source_target_pairs={{0,16},{16,0},{1,17},{17,1},{2,18},{18,2},{3,19},{19,3},{4,20},{20... | collective-permute-start | bytes 49160 | tf_op jit(solution)/shard_map/ppermute | solution.py:529
  27.5 1.7 %slice.6 = bf16[120,64,128]{2,1,0:T(8,128)(2,1)S(1)} slice(bf16[144,64,128]{2,1,0:T(8,128)(2,1)} %param.26), slice={[0:120], [0:64], [0:128]} | slice | bytes 3932160 | tf_op jit(solution)/shard_map/slice | solution.py:621
  29.3 0.7 %collective-permute-done.refs_1_ = f32[64,64]{1,0:T(8,128)S(1)} collective-permute-done((f32[64,64]{1,0:T(8,128)S(1)}, f32[64,64]{1,0:T(8,128)S(1)}, u32[]{:S(2)}, u32[]{:S(2)}) %collective-permute-start) | collective-permute-done | bytes 16416 | tf_op jit(solution)/shard_map/ppermute | solution.py:529
  30.0 6.5 %all-to-all-done.1 = bf16[16,24,384]{2,1,0:T(8,128)(2,1)S(1)} async-done(((bf16[16,24,384]{2,1,0:T(8,128)(2,1)}), bf16[16,24,384]{2,1,0:T(8,128)(2,1)S(1)}, u32[]{:S(2)}, u32[]{:S(2)}) %all-to-all-start.1) | async-done | bytes 294944 | tf_op jit(solution)/shard_map/all_to_all | solution.py:522
  36.5 2.6 %mix.1 = bf16[128,640]{1,0:T(8,128)(2,1)} custom-call(f32[64,64]{1,0:T(8,128)S(1)} %weights.1.refs_0_, f32[64,64]{1,0:T(8,128)S(1)} %collective-permute-done.refs_1_, bf16[384,384]{1,0:T(8,128)(2,1)S(1)} %bitcast.14, bf16[7680,128]{1,0:T(8,128)(2,1)S(1)} %bitcast.13, bf16[9216,128]{1,0:T(8,128)(2,1)} %bitcast.20), custom_call_target="tpu_custom_call" | custom-call | flops 18874368 | bytes 4816896 | tf_op jit(solution)/shard_map/mix/pallas_call | solution.py:507
  39.1 3.5 %all-to-all-start.2 = ((bf16[16,8,640]{2,1,0:T(8,128)(2,1)}), bf16[16,8,640]{2,1,0:T(8,128)(2,1)S(1)}, u32[]{:S(2)}, u32[]{:S(2)}) async-start(bf16[16,8,640]{2,1,0:T(8,128)(2,1)} %bitcast.7), calls=%async_computation.2 | async-start | bytes 327680 | tf_op jit(solution)/shard_map/all_to_all | solution.py:522
  42.7 1.6 %collective-permute-start.1 = (bf16[384,384]{1,0:T(8,128)(2,1)S(1)}, bf16[384,384]{1,0:T(8,128)(2,1)S(1)}, u32[]{:S(2)}, u32[]{:S(2)}) collective-permute-start(bf16[384,384]{1,0:T(8,128)(2,1)S(1)} %bitcast.15), channel_id=1, source_target_pairs={{0,16},{16,0},{1,17},{17,1},{2,18},{18,2},{3,19},{19,3},{4,20},{20... | collective-permute-start | bytes 884744 | tf_op jit(solution)/shard_map/ppermute | solution.py:529
  44.2 0.0 copy-done.9
  44.2 0.0 copy-done.12
  44.2 1.8 %fusion.5.turn_ref = bf16[256,384]{1,0:T(8,128)(2,1)S(1)} fusion(s32[256]{0:T(256)S(1)} %copy-done.11, s32[384]{0:T(512)S(1)} %copy-done.8, s32[256]{0:T(256)S(1)} %mul.70, s32[384]{0:T(512)S(1)} %copy-done.9, s32[384]{0:T(512)S(1)} %copy-done.7, s32[256]{0:T(256)S(1)} %copy-done.12), kind=kLoop, calls=%fused_computation.11 | loop fusion | flops 1966080 | bytes 204288 | tf_op jit(solution)/shard_map/convert_element_type | solution.py:81
  46.0 5.0 %all-to-all-done.2 = bf16[16,8,640]{2,1,0:T(8,128)(2,1)S(1)} async-done(((bf16[16,8,640]{2,1,0:T(8,128)(2,1)}), bf16[16,8,640]{2,1,0:T(8,128)(2,1)S(1)}, u32[]{:S(2)}, u32[]{:S(2)}) %all-to-all-start.2) | async-done | bytes 163872 | tf_op jit(solution)/shard_map/all_to_all | solution.py:522
  51.1 1.0 %adjoint.1 = bf16[128,512]{1,0:T(8,128)(2,1)} custom-call(bf16[256,384]{1,0:T(8,128)(2,1)S(1)} %fusion.5.turn_ref, bf16[128,640]{1,0:T(8,128)(2,1)S(1)} %bitcast.18), custom_call_target="tpu_custom_call" | custom-call | flops 37748736 | bytes 491520 | tf_op jit(solution)/shard_map/adjoint/pallas_call | solution.py:507
  52.0 3.5 %all-to-all-start.3 = ((bf16[16,8,512]{2,1,0:T(8,128)(2,1)}), bf16[16,8,512]{2,1,0:T(8,128)(2,1)S(1)}, u32[]{:S(2)}, u32[]{:S(2)}) async-start(bf16[16,8,512]{2,1,0:T(8,128)(2,1)} %bitcast.9), calls=%async_computation.3 | async-start | bytes 262144 | tf_op jit(solution)/shard_map/all_to_all | solution.py:522
  55.6 0.0 copy-start
  55.6 0.0 copy-start.1
  55.6 0.0 copy-start.2
  55.6 0.0 copy-start.3
  55.6 0.0 copy-start.4
  55.6 0.0 copy-start.5
  55.6 0.0 collective-permute-done.1.refs_1_
  55.6 5.3 %outer.1 = f32[3,48,64,128]{3,2,1,0:T(8,128)} custom-call(bf16[384,384]{1,0:T(8,128)(2,1)S(1)} %bitcast.16, bf16[384,384]{1,0:T(8,128)(2,1)S(1)} %collective-permute-done.1.refs_1_), custom_call_target="tpu_custom_call" | custom-call | flops 37748736 | bytes 5308416 | tf_op jit(solution)/shard_map/outer/pallas_call | solution.py:507
  61.0 2.5 %all-to-all-done.3 = bf16[16,8,512]{2,1,0:T(8,128)(2,1)S(1)} async-done(((bf16[16,8,512]{2,1,0:T(8,128)(2,1)}), bf16[16,8,512]{2,1,0:T(8,128)(2,1)S(1)}, u32[]{:S(2)}, u32[]{:S(2)}) %all-to-all-start.3) | async-done | bytes 131104 | tf_op jit(solution)/shard_map/all_to_all | solution.py:522
  63.4 0.0 copy-done.2
  63.5 2.0 %spatial.1 = (bf16[1,4,64,2048]{3,2,1,0:T(8,128)(2,1)}, f32[64,64]{1,0:T(8,128)}) custom-call(s32[1,32]{1,0:T(1,128)S(1)} %copy-done.5, bf16[128,512]{1,0:T(8,128)(2,1)S(1)} %bitcast.19, bf16[128,128]{1,0:T(8,128)(2,1)S(1)} %copy-done.2, bf16[64,128]{1,0:T(8,128)(2,1)S(1)} %copy-done.4, bf16[64,64]{1,0:T(8,128)(2,1)S(1)} %copy-done.3, ...), custom_call_target="tpu_custom_call" | custom-call | flops 268435456 | bytes 3088512 | tf_op jit(solution)/shard_map/spatial/pallas_call | solution.py:507
  (11 shorter events, 0.0 us)
Async XLA Ops:
  0.6 11.9 %copy-start.6 = (s32[32,2]{1,0:T(8,128)S(1)}, s32[32,2]{1,0:T(8,128)}, u32[]{:S(2)}) copy-start(s32[32,2]{1,0:T(8,128)} %constant.73) | copy-start | bytes 772
  0.6 15.1 %copy-start.7 = (s32[384]{0:T(512)S(1)}, s32[384]{0:T(512)}, u32[]{:S(2)}) copy-start(s32[384]{0:T(512)} %constant.60.clone) | copy-start | bytes 4612
  0.7 15.1 %copy-start.8 = (s32[384]{0:T(512)S(1)}, s32[384]{0:T(512)}, u32[]{:S(2)}) copy-start(s32[384]{0:T(512)} %constant.58.clone) | copy-start | bytes 4612
  0.7 15.1 %copy-start.10 = (s32[384]{0:T(512)S(1)}, s32[384]{0:T(512)}, u32[]{:S(2)}) copy-start(s32[384]{0:T(512)} %constant.57.clone) | copy-start | bytes 4612
  0.7 15.1 %copy-start.13 = (s32[256]{0:T(256)S(1)}, s32[256]{0:T(256)}, u32[]{:S(2)}) copy-start(s32[256]{0:T(256)} %constant.72) | copy-start | bytes 3076
  0.7 15.1 %copy-start.14 = (s32[256]{0:T(256)S(1)}, s32[256]{0:T(256)}, u32[]{:S(2)}) copy-start(s32[256]{0:T(256)} %constant.61.clone) | copy-start | bytes 3076
  0.7 11.8 %copy-start.15 = (s32[1,32]{1,0:T(1,128)S(1)}, s32[1,32]{1,0:T(1,128)}, u32[]{:S(2)}) copy-start(s32[1,32]{1,0:T(1,128)} %param.27) | copy-start | bytes 388
  5.1 16.4 %all-to-all-start = ((bf16[16,8,768]{2,1,0:T(8,128)(2,1)}), bf16[16,8,768]{2,1,0:T(8,128)(2,1)S(1)}, u32[]{:S(2)}, u32[]{:S(2)}) async-start(bf16[16,8,768]{2,1,0:T(8,128)(2,1)} %bitcast.22), calls=%async_computation | async-start | bytes 393216 | tf_op jit(solution)/shard_map/all_to_all | solution.py:522
  22.4 14.1 %all-to-all-start.1 = ((bf16[16,24,384]{2,1,0:T(8,128)(2,1)}), bf16[16,24,384]{2,1,0:T(8,128)(2,1)S(1)}, u32[]{:S(2)}, u32[]{:S(2)}) async-start(bf16[16,24,384]{2,1,0:T(8,128)(2,1)} %bitcast.3), calls=%async_computation.1 | async-start | bytes 589824 | tf_op jit(solution)/shard_map/all_to_all | solution.py:522
  26.0 4.0 %collective-permute-start = (f32[64,64]{1,0:T(8,128)S(1)}, f32[64,64]{1,0:T(8,128)S(1)}, u32[]{:S(2)}, u32[]{:S(2)}) collective-permute-start(f32[64,64]{1,0:T(8,128)S(1)} %weights.1.refs_0_), channel_id=1, source_target_pairs={{0,16},{16,0},{1,17},{17,1},{2,18},{18,2},{3,19},{19,3},{4,20},{20... | collective-permute-start | bytes 49160 | tf_op jit(solution)/shard_map/ppermute | solution.py:529
  36.5 7.7 %copy-start.9 = (s32[384]{0:T(512)S(1)}, s32[384]{0:T(512)}, u32[]{:S(2)}) copy-start(s32[384]{0:T(512)} %constant.62.clone) | copy-start | bytes 4612
  36.5 7.7 %copy-start.11 = (s32[256]{0:T(256)S(1)}, s32[256]{0:T(256)}, u32[]{:S(2)}) copy-start(s32[256]{0:T(256)} %constant.71) | copy-start | bytes 3076
  36.5 7.7 %copy-start.12 = (s32[256]{0:T(256)S(1)}, s32[256]{0:T(256)}, u32[]{:S(2)}) copy-start(s32[256]{0:T(256)} %constant.59.clone) | copy-start | bytes 3076
  39.1 11.9 %all-to-all-start.2 = ((bf16[16,8,640]{2,1,0:T(8,128)(2,1)}), bf16[16,8,640]{2,1,0:T(8,128)(2,1)S(1)}, u32[]{:S(2)}, u32[]{:S(2)}) async-start(bf16[16,8,640]{2,1,0:T(8,128)(2,1)} %bitcast.7), calls=%async_computation.2 | async-start | bytes 327680 | tf_op jit(solution)/shard_map/all_to_all | solution.py:522
  42.7 13.0 %collective-permute-start.1 = (bf16[384,384]{1,0:T(8,128)(2,1)S(1)}, bf16[384,384]{1,0:T(8,128)(2,1)S(1)}, u32[]{:S(2)}, u32[]{:S(2)}) collective-permute-start(bf16[384,384]{1,0:T(8,128)(2,1)S(1)} %bitcast.15), channel_id=1, source_target_pairs={{0,16},{16,0},{1,17},{17,1},{2,18},{18,2},{3,19},{19,3},{4,20},{20... | collective-permute-start | bytes 884744 | tf_op jit(solution)/shard_map/ppermute | solution.py:529
  52.0 11.4 %all-to-all-start.3 = ((bf16[16,8,512]{2,1,0:T(8,128)(2,1)}), bf16[16,8,512]{2,1,0:T(8,128)(2,1)S(1)}, u32[]{:S(2)}, u32[]{:S(2)}) async-start(bf16[16,8,512]{2,1,0:T(8,128)(2,1)} %bitcast.9), calls=%async_computation.3 | async-start | bytes 262144 | tf_op jit(solution)/shard_map/all_to_all | solution.py:522
  55.6 7.9 %copy-start = (bf16[256,2048]{1,0:T(8,128)(2,1)S(1)}, bf16[256,2048]{1,0:T(8,128)(2,1)}, u32[]{:S(2)}) copy-start(bf16[256,2048]{1,0:T(8,128)(2,1)} %get-tuple-element.10.gp_ref) | copy-start | bytes 3145732
  55.6 7.9 %copy-start.1 = (bf16[192,2048]{1,0:T(8,128)(2,1)S(1)}, bf16[192,2048]{1,0:T(8,128)(2,1)}, u32[]{:S(2)}) copy-start(bf16[192,2048]{1,0:T(8,128)(2,1)} %constant.55.clone.tab_hbm.tab_ref) | copy-start | bytes 2359300
  55.6 7.9 %copy-start.2 = (bf16[128,128]{1,0:T(8,128)(2,1)S(1)}, bf16[128,128]{1,0:T(8,128)(2,1)}, u32[]{:S(2)}) copy-start(bf16[128,128]{1,0:T(8,128)(2,1)} %constant.64.clone.back_ref) | copy-start | bytes 98308
  55.6 7.8 %copy-start.3 = (bf16[64,64]{1,0:T(8,128)(2,1)S(1)}, bf16[64,64]{1,0:T(8,128)(2,1)}, u32[]{:S(2)}) copy-start(bf16[64,64]{1,0:T(8,128)(2,1)} %w_ref.1) | copy-start | bytes 24580
  55.6 7.8 %copy-start.4 = (bf16[64,128]{1,0:T(8,128)(2,1)S(1)}, bf16[64,128]{1,0:T(8,128)(2,1)}, u32[]{:S(2)}) copy-start(bf16[64,128]{1,0:T(8,128)(2,1)} %constant.65.clone.share_ref) | copy-start | bytes 49156
  55.6 7.8 %copy-start.5 = (s32[1,32]{1,0:T(1,128)S(1)}, s32[1,32]{1,0:T(1,128)}, u32[]{:S(2)}) copy-start(s32[1,32]{1,0:T(1,128)} %ext_hbm.3) | copy-start | bytes 388

commit v5 on v4

--- a/solution.py
+++ b/solution.py
@@ -277,8 +277,14 @@
 
 def mix_kernel(plan, samples, *refs):
     share_refs = refs[:samples]
-    in_ref, head_ref, rest_hbm, out_hbm, rest_ref, out_ref, last_ref, sems, spec_sem = refs[samples:]
-    chans, both = plan.channels, plan.both
+    in_ref, head_ref, rest_hbm, out_hbm, rest_ref, out_ref, sems, spec_sem, order_sem = refs[samples:]
+    chans, both, head = plan.channels, plan.both, head_ref.shape[0]
+    rest = plan.steps * PA * chans - head if plan.exact else 0
+    if rest:
+        load = pltpu.make_async_copy(rest_hbm.at[pl.ds(head, rest)], rest_ref, spec_sem)
+        load.start()
+        pl.semaphore_signal(order_sem, 1)
+        pl.semaphore_wait(order_sem, 1)
     total = share_refs[0][...]
     for ref in share_refs[1:]:
         total = total + ref[...]
@@ -286,7 +292,6 @@
     lane = lax.broadcasted_iota(jnp.int32, (8, both), 1)
     share = plan.share
     order = slot_order(plan)
-    head = head_ref.shape[0]
 
     def left_of(owner, step):
         start = (owner * plan.steps + step) * 8
@@ -308,7 +313,7 @@
             value = pltpu.roll(value, chans, axis=1)
         lanes = slice(place * chans, (place + 1) * chans)
         half = slice((place % 2) * chans, (place % 2 + 1) * chans)
-        out_ref[owner * 8 : owner * 8 + 8, lanes] = value[:, half]
+        out_ref[owner * 8 : owner * 8 + 8, lanes] = value[:, half].astype(BF16)
 
     def mix_general(owner):
         for step in range(plan.steps):
@@ -346,27 +351,23 @@
                     ]
                     tile = jnp.where(lane < chans, piece[:, :both], after[:, :both])
                     place = order.index((step, p)) * chans
-                    out_ref[owner * 8 : owner * 8 + 8, place : place + both] = tile
+                    out_ref[owner * 8 : owner * 8 + 8, place : place + both] = tile.astype(BF16)
                 else:
                     single = piece[:, :chans]
                     put(owner, step, p, (jnp.concatenate([single, single], axis=1), 0))
 
-    rest = plan.steps * PA * chans - head if plan.exact else 0
-    if rest:
-        load = pltpu.make_async_copy(rest_hbm.at[pl.ds(head, rest)], rest_ref, spec_sem)
-        load.start()
     places = out_ref.shape[1] // chans
     for owner in range(plan.ranks):
         lines = slice(owner * 8, owner * 8 + 8)
         if places - 1 > len(order):
             out_ref[lines, len(order) * chans : (places - 1) * chans] = jnp.zeros(
-                (8, (places - 1 - len(order)) * chans), F32
+                (8, (places - 1 - len(order)) * chans), BF16
             )
         rows = slice(owner * share, (owner + 1) * share)
         pieces = [high[rows], low[rows]]
         if 2 * share < 8:
             pieces.append(jnp.zeros((8 - 2 * share, chans), F32))
-        out_ref[lines, (places - 1) * chans :] = jnp.concatenate(pieces, axis=0)
+        out_ref[lines, (places - 1) * chans :] = jnp.concatenate(pieces, axis=0).astype(BF16)
     if plan.exact:
         waited = rest == 0
         for step in range(plan.steps):
@@ -384,10 +385,8 @@
     each = plan.ranks * 8 // chunks
     saves = []
     for chunk in range(chunks):
-        lines = slice(chunk * each, (chunk + 1) * each)
-        last_ref[lines] = out_ref[lines].astype(BF16)
         span = pl.ds(chunk * each, each)
-        copy = pltpu.make_async_copy(last_ref.at[span], out_hbm.at[span], sems.at[chunk])
+        copy = pltpu.make_async_copy(out_ref.at[span], out_hbm.at[span], sems.at[chunk])
         copy.start()
         saves.append(copy)
     for copy in saves:
@@ -627,10 +626,10 @@
         out_specs=(hbm,),
         scratch_shapes=[
             pltpu.VMEM((max(flat.shape[0] - head, 8), plan.both), BF16),
-            pltpu.VMEM((ranks * 8, back_width), F32),
             pltpu.VMEM((ranks * 8, back_width), BF16),
             pltpu.SemaphoreType.DMA((chunks,)),
             pltpu.SemaphoreType.DMA,
+            pltpu.SemaphoreType.REGULAR,
         ],
     )[0]
     returned = exchange(sent)

time: 66.1 us -> 65.6 us (level)
  no operation moved by 1% of the time
where the time goes in v5:
time: 65.6 us; the launch traced here: 65 us
  starting transfers between devices  21.1 us (32%)
  Pallas kernels  18.6 us (28%)
  waiting for transfers between devices  18.5 us (28%)
  other arithmetic  3.78 us (6%)
  local copies, waits for them, and re-layouts  2.12 us (3%)
  between operations  0.92 us (1%)
    pallas_call x7, Pallas kernels, call(): pl.pallas_call(body, out_shape=outs, name=name, cost_estimate=pl.CostEsti...  18.6 us
    all_to_all x4, starting transfers between devices, exchange(): lax.all_to_all(value, 'rows', split_axis=0, concat_axis=0, tiled=True)  18 us
    all_to_all x4, waiting for transfers between devices, exchange(): lax.all_to_all(value, 'rows', split_axis=0, concat_axis=0, tiled=True)  17.8 us
    convert_element_type x2, other arithmetic, turn_table(): return jnp.where(mo == ro, value, 0.0).astype(BF16)  3.71 us
    ppermute x2, starting transfers between devices, every_sample(): return [value, lax.ppermute(value, 'batch', [(0, 1), (1, 0)])]  3.11 us
    slice x1, local copies, waits for them, and re-layouts, shards(): flat[:head]  1.7 us
  transfers between devices with their start and end apart: 6, of which 5 were waited for; matrix products, arithmetic and copies ran while one was open for 9% of the time, Pallas kernels for 14%

profile of v5, /device:TPU:0, one launch (start us, length us, event | category | flops | bytes accessed | tf_op | source)
XLA Modules:
  0.0 65.0 jit_solution(17302858542930574297)
XLA Ops:
  0.6 0.0 copy-start.6
  0.6 0.0 copy-start.7
  0.7 0.0 copy-start.8
  0.7 0.0 copy-start.10
  0.7 0.0 copy-start.13
  0.7 0.0 copy-start.14
  0.7 0.0 copy-start.15
  0.7 4.4 %columns.1 = (bf16[256,2048]{1,0:T(8,128)(2,1)}, bf16[128,768]{1,0:T(8,128)(2,1)}) custom-call(s32[1,32]{1,0:T(1,128)} %ext_hbm.3, bf16[1,4,64,2048]{3,2,1,0:T(8,128)(2,1)} %x_ref.1, bf16[1,4,64,2048]{3,2,1,0:T(8,128)(2,1)} %pre_hbm.1, bf16[1,4,64,2048]{3,2,1,0:T(8,128)(2,1)} %cot_hbm.1, bf16[192,2048]{1,0:T(8,128)(2,1)} %constant.55.clone.tab_hbm.tab_ref, ...), custom_call_target="tpu_custom_call" | custom-call | flops 402653184 | bytes 5210240 | tf_op jit(solution)/shard_map/columns/pallas_call | solution.py:506
  5.1 7.4 %all-to-all-start = ((bf16[16,8,768]{2,1,0:T(8,128)(2,1)}), bf16[16,8,768]{2,1,0:T(8,128)(2,1)S(1)}, u32[]{:S(2)}, u32[]{:S(2)}) async-start(bf16[16,8,768]{2,1,0:T(8,128)(2,1)} %bitcast.22), calls=%async_computation | async-start | bytes 393216 | tf_op jit(solution)/shard_map/all_to_all | solution.py:521
  12.5 0.0 copy-done.15
  12.5 0.0 copy-done.6
  12.5 0.1 broadcast_add_fusion
  12.6 0.1 reshape.42
  12.7 0.1 transpose.16
  12.8 0.1 mul.70
  12.9 2.8 %weights.1.refs_0_ = f32[64,64]{1,0:T(8,128)S(1)} custom-call(bf16[1,4,64,2048]{3,2,1,0:T(8,128)(2,1)} %x_ref.1, bf16[256,2048]{1,0:T(8,128)(2,1)} %get-tuple-element.10.gp_ref), custom_call_target="tpu_custom_call" | custom-call | flops 67108864 | bytes 2113536 | tf_op jit(solution)/shard_map/weights/pallas_call | solution.py:506
  15.8 0.0 copy-done.7
  15.8 0.0 copy-done.8
  15.8 0.0 copy-done.10
  15.8 0.0 copy-done.13
  15.8 0.0 copy-done.14
  15.8 1.9 %fusion.11.turn_ref = bf16[384,256]{1,0:T(8,128)(2,1)S(1)} fusion(s32[256]{0:T(256)S(1)} %copy-done.13, s32[384]{0:T(512)S(1)} %copy-done.8, s32[256]{0:T(256)S(1)} %mul.70, s32[384]{0:T(512)S(1)} %copy-done.10, s32[256]{0:T(256)S(1)} %copy-done.14, s32[384]{0:T(512)S(1)} %copy-done.7), kind=kLoop, calls=%fused_computation.17 | loop fusion | flops 1966080 | bytes 204288 | tf_op jit(solution)/shard_map/convert_element_type | solution.py:81
  17.7 3.8 %all-to-all-done = bf16[16,8,768]{2,1,0:T(8,128)(2,1)S(1)} async-done(((bf16[16,8,768]{2,1,0:T(8,128)(2,1)}), bf16[16,8,768]{2,1,0:T(8,128)(2,1)S(1)}, u32[]{:S(2)}, u32[]{:S(2)}) %all-to-all-start) | async-done | bytes 196640 | tf_op jit(solution)/shard_map/all_to_all | solution.py:521
  21.5 1.0 %rows.1 = bf16[384,384]{1,0:T(8,128)(2,1)} custom-call(bf16[384,256]{1,0:T(8,128)(2,1)S(1)} %fusion.11.turn_ref, bf16[128,768]{1,0:T(8,128)(2,1)S(1)} %bitcast.17), custom_call_target="tpu_custom_call" | custom-call | flops 75497472 | bytes 688128 | tf_op jit(solution)/shard_map/rows/pallas_call | solution.py:506
  22.4 3.5 %all-to-all-start.1 = ((bf16[16,24,384]{2,1,0:T(8,128)(2,1)}), bf16[16,24,384]{2,1,0:T(8,128)(2,1)S(1)}, u32[]{:S(2)}, u32[]{:S(2)}) async-start(bf16[16,24,384]{2,1,0:T(8,128)(2,1)} %bitcast.3), calls=%async_computation.1 | async-start | bytes 589824 | tf_op jit(solution)/shard_map/all_to_all | solution.py:521
  26.0 1.6 %collective-permute-start = (f32[64,64]{1,0:T(8,128)S(1)}, f32[64,64]{1,0:T(8,128)S(1)}, u32[]{:S(2)}, u32[]{:S(2)}) collective-permute-start(f32[64,64]{1,0:T(8,128)S(1)} %weights.1.refs_0_), channel_id=1, source_target_pairs={{0,16},{16,0},{1,17},{17,1},{2,18},{18,2},{3,19},{19,3},{4,20},{20... | collective-permute-start | bytes 49160 | tf_op jit(solution)/shard_map/ppermute | solution.py:528
  27.5 1.7 %slice.6 = bf16[120,64,128]{2,1,0:T(8,128)(2,1)S(1)} slice(bf16[144,64,128]{2,1,0:T(8,128)(2,1)} %param.26), slice={[0:120], [0:64], [0:128]} | slice | bytes 3932160 | tf_op jit(solution)/shard_map/slice | solution.py:620
  29.3 0.7 %collective-permute-done.refs_1_ = f32[64,64]{1,0:T(8,128)S(1)} collective-permute-done((f32[64,64]{1,0:T(8,128)S(1)}, f32[64,64]{1,0:T(8,128)S(1)}, u32[]{:S(2)}, u32[]{:S(2)}) %collective-permute-start) | collective-permute-done | bytes 16416 | tf_op jit(solution)/shard_map/ppermute | solution.py:528
  30.0 6.5 %all-to-all-done.1 = bf16[16,24,384]{2,1,0:T(8,128)(2,1)S(1)} async-done(((bf16[16,24,384]{2,1,0:T(8,128)(2,1)}), bf16[16,24,384]{2,1,0:T(8,128)(2,1)S(1)}, u32[]{:S(2)}, u32[]{:S(2)}) %all-to-all-start.1) | async-done | bytes 294944 | tf_op jit(solution)/shard_map/all_to_all | solution.py:521
  36.5 2.1 %mix.1 = bf16[128,640]{1,0:T(8,128)(2,1)} custom-call(f32[64,64]{1,0:T(8,128)S(1)} %weights.1.refs_0_, f32[64,64]{1,0:T(8,128)S(1)} %collective-permute-done.refs_1_, bf16[384,384]{1,0:T(8,128)(2,1)S(1)} %bitcast.14, bf16[7680,128]{1,0:T(8,128)(2,1)S(1)} %bitcast.13, bf16[9216,128]{1,0:T(8,128)(2,1)} %bitcast.20), custom_call_target="tpu_custom_call" | custom-call | flops 18874368 | bytes 4816896 | tf_op jit(solution)/shard_map/mix/pallas_call | solution.py:506
  38.6 3.5 %all-to-all-start.2 = ((bf16[16,8,640]{2,1,0:T(8,128)(2,1)}), bf16[16,8,640]{2,1,0:T(8,128)(2,1)S(1)}, u32[]{:S(2)}, u32[]{:S(2)}) async-start(bf16[16,8,640]{2,1,0:T(8,128)(2,1)} %bitcast.7), calls=%async_computation.2 | async-start | bytes 327680 | tf_op jit(solution)/shard_map/all_to_all | solution.py:521
  42.1 1.6 %collective-permute-start.1 = (bf16[384,384]{1,0:T(8,128)(2,1)S(1)}, bf16[384,384]{1,0:T(8,128)(2,1)S(1)}, u32[]{:S(2)}, u32[]{:S(2)}) collective-permute-start(bf16[384,384]{1,0:T(8,128)(2,1)S(1)} %bitcast.15), channel_id=1, source_target_pairs={{0,16},{16,0},{1,17},{17,1},{2,18},{18,2},{3,19},{19,3},{4,20},{20... | collective-permute-start | bytes 884744 | tf_op jit(solution)/shard_map/ppermute | solution.py:528
  43.7 0.0 copy-done.12
  43.7 1.8 %fusion.5.turn_ref = bf16[256,384]{1,0:T(8,128)(2,1)S(1)} fusion(s32[256]{0:T(256)S(1)} %copy-done.11, s32[384]{0:T(512)S(1)} %copy-done.8, s32[256]{0:T(256)S(1)} %mul.70, s32[384]{0:T(512)S(1)} %copy-done.9, s32[384]{0:T(512)S(1)} %copy-done.7, s32[256]{0:T(256)S(1)} %copy-done.12), kind=kLoop, calls=%fused_computation.11 | loop fusion | flops 1966080 | bytes 204288 | tf_op jit(solution)/shard_map/convert_element_type | solution.py:81
  45.5 5.0 %all-to-all-done.2 = bf16[16,8,640]{2,1,0:T(8,128)(2,1)S(1)} async-done(((bf16[16,8,640]{2,1,0:T(8,128)(2,1)}), bf16[16,8,640]{2,1,0:T(8,128)(2,1)S(1)}, u32[]{:S(2)}, u32[]{:S(2)}) %all-to-all-start.2) | async-done | bytes 163872 | tf_op jit(solution)/shard_map/all_to_all | solution.py:521
  50.5 1.0 %adjoint.1 = bf16[128,512]{1,0:T(8,128)(2,1)} custom-call(bf16[256,384]{1,0:T(8,128)(2,1)S(1)} %fusion.5.turn_ref, bf16[128,640]{1,0:T(8,128)(2,1)S(1)} %bitcast.18), custom_call_target="tpu_custom_call" | custom-call | flops 37748736 | bytes 491520 | tf_op jit(solution)/shard_map/adjoint/pallas_call | solution.py:506
  51.5 3.5 %all-to-all-start.3 = ((bf16[16,8,512]{2,1,0:T(8,128)(2,1)}), bf16[16,8,512]{2,1,0:T(8,128)(2,1)S(1)}, u32[]{:S(2)}, u32[]{:S(2)}) async-start(bf16[16,8,512]{2,1,0:T(8,128)(2,1)} %bitcast.9), calls=%async_computation.3 | async-start | bytes 262144 | tf_op jit(solution)/shard_map/all_to_all | solution.py:521
  55.0 0.0 copy-start
  55.0 0.0 copy-start.1
  55.1 0.0 copy-start.2
  55.1 0.0 copy-start.3
  55.1 0.0 copy-start.4
  55.1 0.0 copy-start.5
  55.1 0.0 collective-permute-done.1.refs_1_
  55.1 5.3 %outer.1 = f32[3,48,64,128]{3,2,1,0:T(8,128)} custom-call(bf16[384,384]{1,0:T(8,128)(2,1)S(1)} %bitcast.16, bf16[384,384]{1,0:T(8,128)(2,1)S(1)} %collective-permute-done.1.refs_1_), custom_call_target="tpu_custom_call" | custom-call | flops 37748736 | bytes 5308416 | tf_op jit(solution)/shard_map/outer/pallas_call | solution.py:506
  60.4 2.5 %all-to-all-done.3 = bf16[16,8,512]{2,1,0:T(8,128)(2,1)S(1)} async-done(((bf16[16,8,512]{2,1,0:T(8,128)(2,1)}), bf16[16,8,512]{2,1,0:T(8,128)(2,1)S(1)}, u32[]{:S(2)}, u32[]{:S(2)}) %all-to-all-start.3) | async-done | bytes 131104 | tf_op jit(solution)/shard_map/all_to_all | solution.py:521
  62.9 0.0 copy-done
  62.9 2.1 %spatial.1 = (bf16[1,4,64,2048]{3,2,1,0:T(8,128)(2,1)}, f32[64,64]{1,0:T(8,128)}) custom-call(s32[1,32]{1,0:T(1,128)S(1)} %copy-done.5, bf16[128,512]{1,0:T(8,128)(2,1)S(1)} %bitcast.19, bf16[128,128]{1,0:T(8,128)(2,1)S(1)} %copy-done.2, bf16[64,128]{1,0:T(8,128)(2,1)S(1)} %copy-done.4, bf16[64,64]{1,0:T(8,128)(2,1)S(1)} %copy-done.3, ...), custom_call_target="tpu_custom_call" | custom-call | flops 268435456 | bytes 3088512 | tf_op jit(solution)/shard_map/spatial/pallas_call | solution.py:506
  (11 shorter events, 0.0 us)
Async XLA Ops:
  0.6 11.9 %copy-start.6 = (s32[32,2]{1,0:T(8,128)S(1)}, s32[32,2]{1,0:T(8,128)}, u32[]{:S(2)}) copy-start(s32[32,2]{1,0:T(8,128)} %constant.73) | copy-start | bytes 772
  0.6 15.1 %copy-start.7 = (s32[384]{0:T(512)S(1)}, s32[384]{0:T(512)}, u32[]{:S(2)}) copy-start(s32[384]{0:T(512)} %constant.60.clone) | copy-start | bytes 4612
  0.7 15.1 %copy-start.8 = (s32[384]{0:T(512)S(1)}, s32[384]{0:T(512)}, u32[]{:S(2)}) copy-start(s32[384]{0:T(512)} %constant.58.clone) | copy-start | bytes 4612
  0.7 15.1 %copy-start.10 = (s32[384]{0:T(512)S(1)}, s32[384]{0:T(512)}, u32[]{:S(2)}) copy-start(s32[384]{0:T(512)} %constant.57.clone) | copy-start | bytes 4612
  0.7 15.1 %copy-start.13 = (s32[256]{0:T(256)S(1)}, s32[256]{0:T(256)}, u32[]{:S(2)}) copy-start(s32[256]{0:T(256)} %constant.72) | copy-start | bytes 3076
  0.7 15.1 %copy-start.14 = (s32[256]{0:T(256)S(1)}, s32[256]{0:T(256)}, u32[]{:S(2)}) copy-start(s32[256]{0:T(256)} %constant.61.clone) | copy-start | bytes 3076
  0.7 11.8 %copy-start.15 = (s32[1,32]{1,0:T(1,128)S(1)}, s32[1,32]{1,0:T(1,128)}, u32[]{:S(2)}) copy-start(s32[1,32]{1,0:T(1,128)} %param.27) | copy-start | bytes 388
  5.1 16.4 %all-to-all-start = ((bf16[16,8,768]{2,1,0:T(8,128)(2,1)}), bf16[16,8,768]{2,1,0:T(8,128)(2,1)S(1)}, u32[]{:S(2)}, u32[]{:S(2)}) async-start(bf16[16,8,768]{2,1,0:T(8,128)(2,1)} %bitcast.22), calls=%async_computation | async-start | bytes 393216 | tf_op jit(solution)/shard_map/all_to_all | solution.py:521
  22.4 14.1 %all-to-all-start.1 = ((bf16[16,24,384]{2,1,0:T(8,128)(2,1)}), bf16[16,24,384]{2,1,0:T(8,128)(2,1)S(1)}, u32[]{:S(2)}, u32[]{:S(2)}) async-start(bf16[16,24,384]{2,1,0:T(8,128)(2,1)} %bitcast.3), calls=%async_computation.1 | async-start | bytes 589824 | tf_op jit(solution)/shard_map/all_to_all | solution.py:521
  26.0 4.0 %collective-permute-start = (f32[64,64]{1,0:T(8,128)S(1)}, f32[64,64]{1,0:T(8,128)S(1)}, u32[]{:S(2)}, u32[]{:S(2)}) collective-permute-start(f32[64,64]{1,0:T(8,128)S(1)} %weights.1.refs_0_), channel_id=1, source_target_pairs={{0,16},{16,0},{1,17},{17,1},{2,18},{18,2},{3,19},{19,3},{4,20},{20... | collective-permute-start | bytes 49160 | tf_op jit(solution)/shard_map/ppermute | solution.py:528
  36.5 7.2 %copy-start.9 = (s32[384]{0:T(512)S(1)}, s32[384]{0:T(512)}, u32[]{:S(2)}) copy-start(s32[384]{0:T(512)} %constant.62.clone) | copy-start | bytes 4612
  36.5 7.2 %copy-start.11 = (s32[256]{0:T(256)S(1)}, s32[256]{0:T(256)}, u32[]{:S(2)}) copy-start(s32[256]{0:T(256)} %constant.71) | copy-start | bytes 3076
  36.5 7.2 %copy-start.12 = (s32[256]{0:T(256)S(1)}, s32[256]{0:T(256)}, u32[]{:S(2)}) copy-start(s32[256]{0:T(256)} %constant.59.clone) | copy-start | bytes 3076
  38.6 11.9 %all-to-all-start.2 = ((bf16[16,8,640]{2,1,0:T(8,128)(2,1)}), bf16[16,8,640]{2,1,0:T(8,128)(2,1)S(1)}, u32[]{:S(2)}, u32[]{:S(2)}) async-start(bf16[16,8,640]{2,1,0:T(8,128)(2,1)} %bitcast.7), calls=%async_computation.2 | async-start | bytes 327680 | tf_op jit(solution)/shard_map/all_to_all | solution.py:521
  42.1 13.0 %collective-permute-start.1 = (bf16[384,384]{1,0:T(8,128)(2,1)S(1)}, bf16[384,384]{1,0:T(8,128)(2,1)S(1)}, u32[]{:S(2)}, u32[]{:S(2)}) collective-permute-start(bf16[384,384]{1,0:T(8,128)(2,1)S(1)} %bitcast.15), channel_id=1, source_target_pairs={{0,16},{16,0},{1,17},{17,1},{2,18},{18,2},{3,19},{19,3},{4,20},{20... | collective-permute-start | bytes 884744 | tf_op jit(solution)/shard_map/ppermute | solution.py:528
  51.5 11.4 %all-to-all-start.3 = ((bf16[16,8,512]{2,1,0:T(8,128)(2,1)}), bf16[16,8,512]{2,1,0:T(8,128)(2,1)S(1)}, u32[]{:S(2)}, u32[]{:S(2)}) async-start(bf16[16,8,512]{2,1,0:T(8,128)(2,1)} %bitcast.9), calls=%async_computation.3 | async-start | bytes 262144 | tf_op jit(solution)/shard_map/all_to_all | solution.py:521
  55.0 7.9 %copy-start = (bf16[256,2048]{1,0:T(8,128)(2,1)S(1)}, bf16[256,2048]{1,0:T(8,128)(2,1)}, u32[]{:S(2)}) copy-start(bf16[256,2048]{1,0:T(8,128)(2,1)} %get-tuple-element.10.gp_ref) | copy-start | bytes 3145732
  55.0 7.9 %copy-start.1 = (bf16[192,2048]{1,0:T(8,128)(2,1)S(1)}, bf16[192,2048]{1,0:T(8,128)(2,1)}, u32[]{:S(2)}) copy-start(bf16[192,2048]{1,0:T(8,128)(2,1)} %constant.55.clone.tab_hbm.tab_ref) | copy-start | bytes 2359300
  55.1 7.9 %copy-start.2 = (bf16[128,128]{1,0:T(8,128)(2,1)S(1)}, bf16[128,128]{1,0:T(8,128)(2,1)}, u32[]{:S(2)}) copy-start(bf16[128,128]{1,0:T(8,128)(2,1)} %constant.64.clone.back_ref) | copy-start | bytes 98308
  55.1 7.8 %copy-start.3 = (bf16[64,64]{1,0:T(8,128)(2,1)S(1)}, bf16[64,64]{1,0:T(8,128)(2,1)}, u32[]{:S(2)}) copy-start(bf16[64,64]{1,0:T(8,128)(2,1)} %w_ref.1) | copy-start | bytes 24580
  55.1 7.8 %copy-start.4 = (bf16[64,128]{1,0:T(8,128)(2,1)S(1)}, bf16[64,128]{1,0:T(8,128)(2,1)}, u32[]{:S(2)}) copy-start(bf16[64,128]{1,0:T(8,128)(2,1)} %constant.65.clone.share_ref) | copy-start | bytes 49156
  55.1 7.8 %copy-start.5 = (s32[1,32]{1,0:T(1,128)S(1)}, s32[1,32]{1,0:T(1,128)}, u32[]{:S(2)}) copy-start(s32[1,32]{1,0:T(1,128)} %ext_hbm.3) | copy-start | bytes 388

commit v6 on v5

--- a/solution.py
+++ b/solution.py
@@ -223,8 +223,9 @@
             copy.wait()
 
 
-def weight_kernel(x_ref, gp_ref, out_ref):
+def weight_kernel(w_ref, x_ref, gp_ref, out_ref, direct_ref):
     part = lax.dot_general(x_ref[0, 0], gp_ref[...], NT, preferred_element_type=F32)
+    direct_ref[...] = jnp.dot(w_ref[...], gp_ref[...], preferred_element_type=F32).astype(BF16)
 
     @pl.when(pl.program_id(0) == 0)
     def _():
@@ -456,7 +457,7 @@
 
 
 def spatial_kernel(
-    plan, step, weight_scale, ext_hbm, in_ref, back_ref, share_ref, w_ref, tab_ref, gp_ref,
+    plan, step, weight_scale, ext_hbm, in_ref, back_ref, share_ref, tab_ref, direct_ref,
     out_hbm, gw_hbm, ext_ref, left_ref, out_ref, gw_ref, sems, ext_sem, gw_sem,
 ):
     chans, rows = plan.channels, plan.local_rows
@@ -484,8 +485,8 @@
             live = mask_rows(ext_ref[0, first + slot], n * step, step, chans)
             for row in range(slot * SLAB, (slot + 1) * SLAB):
                 lines = slice(row * chans, (row + 1) * chans)
-                direct = jnp.dot(w_ref[...], gp_ref[lines, cols], preferred_element_type=F32)
-                out_ref[row, :, cols] = (spatial[lines] + direct).astype(BF16) * live
+                value = spatial[lines] + direct_ref[lines, cols].astype(F32)
+                out_ref[row, :, cols] = value.astype(BF16) * live
         copy = pltpu.make_async_copy(
             out_ref.at[:, :, pl.ds(n * step, step)],
             out_hbm.at[0, :, :, pl.ds(n * step, step)],
@@ -570,20 +571,24 @@
         ],
     )
     received = exchange(sent)
-    local_weight = call(
+    local_weight, direct = call(
         weight_kernel,
-        (stay(layer_input), stay(grad_pre)),
-        (sds((chans, chans), F32),),
+        (weight, stay(layer_input), stay(grad_pre)),
+        (sds((chans, chans), F32), sds(grad_pre.shape, BF16)),
         "weights",
-        2 * layer_input.size * chans,
+        4 * layer_input.size * chans,
         16,
         grid=(local_rows,),
         in_specs=[
+            pl.BlockSpec((chans, chans), lambda r: (0, 0)),
             pl.BlockSpec((1, 1, chans, columns), lambda r: (0, r, 0, 0)),
             pl.BlockSpec((chans, columns), lambda r: (r, 0)),
         ],
-        out_specs=(pl.BlockSpec((chans, chans), lambda r: (0, 0)),),
-    )[0]
+        out_specs=(
+            pl.BlockSpec((chans, chans), lambda r: (0, 0)),
+            pl.BlockSpec((chans, columns), lambda r: (r, 0)),
+        ),
+    )
     received, local_weight = lax.optimization_barrier((received, local_weight))
     shares = every_sample(local_weight, samples)
     if samples > 2:
@@ -662,12 +667,12 @@
     gather_back, share_in = jnp.asarray(plan.gather_back()), jnp.asarray(plan.share_in())
     grad_input, grad_weight = call(
         functools.partial(spatial_kernel, plan, step, weight_scale),
-        (extents, local_back, gather_back, share_in, weight, table, grad_pre),
+        (extents, local_back, gather_back, share_in, table, direct),
         (sds(layer_input.shape, BF16), sds((chans, chans), F32)),
         "spatial",
-        2 * local_rows * chans * columns * (table.shape[0] + chans),
+        2 * local_rows * chans * columns * table.shape[0],
         16,
-        in_specs=[hbm] + [vmem] * 6,
+        in_specs=[hbm] + [vmem] * 5,
         out_specs=(hbm, hbm),
         scratch_shapes=[
             pltpu.SMEM(extents.shape, jnp.int32),

time: 65.6 us -> 65.3 us (level)
  no operation moved by 1% of the time
where the time goes in v6:
time: 65.3 us; the launch traced here: 64.7 us
  starting transfers between devices  21.1 us (32%)
  Pallas kernels  18.6 us (28%)
  waiting for transfers between devices  18.3 us (28%)
  other arithmetic  3.78 us (6%)
  local copies, waits for them, and re-layouts  2.12 us (3%)
  between operations  0.91 us (1%)
    pallas_call x7, Pallas kernels, call(): pl.pallas_call(body, out_shape=outs, name=name, cost_estimate=pl.CostEsti...  18.6 us
    all_to_all x4, starting transfers between devices, exchange(): lax.all_to_all(value, 'rows', split_axis=0, concat_axis=0, tiled=True)  18 us
    all_to_all x4, waiting for transfers between devices, exchange(): lax.all_to_all(value, 'rows', split_axis=0, concat_axis=0, tiled=True)  17.5 us
    convert_element_type x2, other arithmetic, turn_table(): return jnp.where(mo == ro, value, 0.0).astype(BF16)  3.71 us
    ppermute x2, starting transfers between devices, every_sample(): return [value, lax.ppermute(value, 'batch', [(0, 1), (1, 0)])]  3.11 us
    slice x1, local copies, waits for them, and re-layouts, shards(): flat[:head]  1.7 us
  transfers between devices with their start and end apart: 6, of which 5 were waited for; matrix products, arithmetic and copies ran while one was open for 9% of the time, Pallas kernels for 14%

profile of v6, /device:TPU:0, one launch (start us, length us, event | category | flops | bytes accessed | tf_op | source)
XLA Modules:
  0.0 64.7 jit_solution(5331550695660969794)
XLA Ops:
  0.6 0.0 copy-start.5
  0.6 0.0 copy-start.6
  0.7 0.0 copy-start.7
  0.7 0.0 copy-start.9
  0.7 0.0 copy-start.12
  0.7 0.0 copy-start.13
  0.7 0.0 copy-start.14
  0.7 0.0 copy-start.2
  0.7 4.4 %columns.1 = (bf16[256,2048]{1,0:T(8,128)(2,1)}, bf16[128,768]{1,0:T(8,128)(2,1)}) custom-call(s32[1,32]{1,0:T(1,128)} %ext_hbm.3, bf16[1,4,64,2048]{3,2,1,0:T(8,128)(2,1)} %x_ref.1, bf16[1,4,64,2048]{3,2,1,0:T(8,128)(2,1)} %pre_hbm.1, bf16[1,4,64,2048]{3,2,1,0:T(8,128)(2,1)} %cot_hbm.1, bf16[192,2048]{1,0:T(8,128)(2,1)} %constant.55.clone.tab_hbm.tab_ref, ...), custom_call_target="tpu_custom_call" | custom-call | flops 402653184 | bytes 5210240 | tf_op jit(solution)/shard_map/columns/pallas_call | solution.py:507
  5.1 7.4 %all-to-all-start = ((bf16[16,8,768]{2,1,0:T(8,128)(2,1)}), bf16[16,8,768]{2,1,0:T(8,128)(2,1)S(1)}, u32[]{:S(2)}, u32[]{:S(2)}) async-start(bf16[16,8,768]{2,1,0:T(8,128)(2,1)} %bitcast.22), calls=%async_computation | async-start | bytes 393216 | tf_op jit(solution)/shard_map/all_to_all | solution.py:522
  12.5 0.0 copy-done.14
  12.6 0.0 copy-done.5
  12.6 0.1 broadcast_add_fusion
  12.6 0.1 reshape.42
  12.7 0.1 transpose.16
  12.8 0.1 mul.70
  13.0 0.0 copy-done.2
  13.0 3.0 %weights.1 = (f32[64,64]{1,0:T(8,128)S(1)}, bf16[256,2048]{1,0:T(8,128)(2,1)S(1)}) custom-call(bf16[64,64]{1,0:T(8,128)(2,1)S(1)} %copy-done.2, bf16[1,4,64,2048]{3,2,1,0:T(8,128)(2,1)} %x_ref.1, bf16[256,2048]{1,0:T(8,128)(2,1)} %get-tuple-element.12.gp_ref), custom_call_target="tpu_custom_call" | custom-call | flops 134217728 | bytes 3170304 | tf_op jit(solution)/shard_map/weights/pallas_call | solution.py:507
  16.0 0.0 copy-done.6
  16.0 0.0 copy-done.7
  16.0 0.0 copy-done.9
  16.1 0.0 copy-done.12
  16.1 0.0 copy-done.13
  16.1 1.9 %fusion.11.turn_ref = bf16[384,256]{1,0:T(8,128)(2,1)S(1)} fusion(s32[256]{0:T(256)S(1)} %copy-done.12, s32[384]{0:T(512)S(1)} %copy-done.7, s32[256]{0:T(256)S(1)} %mul.70, s32[384]{0:T(512)S(1)} %copy-done.9, s32[256]{0:T(256)S(1)} %copy-done.13, s32[384]{0:T(512)S(1)} %copy-done.6), kind=kLoop, calls=%fused_computation.17 | loop fusion | flops 1966080 | bytes 204288 | tf_op jit(solution)/shard_map/convert_element_type | solution.py:81
  18.0 3.5 %all-to-all-done = bf16[16,8,768]{2,1,0:T(8,128)(2,1)S(1)} async-done(((bf16[16,8,768]{2,1,0:T(8,128)(2,1)}), bf16[16,8,768]{2,1,0:T(8,128)(2,1)S(1)}, u32[]{:S(2)}, u32[]{:S(2)}) %all-to-all-start) | async-done | bytes 196640 | tf_op jit(solution)/shard_map/all_to_all | solution.py:522
  21.5 1.0 %rows.1 = bf16[384,384]{1,0:T(8,128)(2,1)} custom-call(bf16[384,256]{1,0:T(8,128)(2,1)S(1)} %fusion.11.turn_ref, bf16[128,768]{1,0:T(8,128)(2,1)S(1)} %bitcast.17), custom_call_target="tpu_custom_call" | custom-call | flops 75497472 | bytes 688128 | tf_op jit(solution)/shard_map/rows/pallas_call | solution.py:507
  22.5 3.5 %all-to-all-start.1 = ((bf16[16,24,384]{2,1,0:T(8,128)(2,1)}), bf16[16,24,384]{2,1,0:T(8,128)(2,1)S(1)}, u32[]{:S(2)}, u32[]{:S(2)}) async-start(bf16[16,24,384]{2,1,0:T(8,128)(2,1)} %bitcast.3), calls=%async_computation.1 | async-start | bytes 589824 | tf_op jit(solution)/shard_map/all_to_all | solution.py:522
  26.0 1.6 %collective-permute-start = (f32[64,64]{1,0:T(8,128)S(1)}, f32[64,64]{1,0:T(8,128)S(1)}, u32[]{:S(2)}, u32[]{:S(2)}) collective-permute-start(f32[64,64]{1,0:T(8,128)S(1)} %get-tuple-element.14.refs_0_), channel_id=1, source_target_pairs={{0,16},{16,0},{1,17},{17,1},{2,18},{18,2},{3,19},{19,3},{4,20},{20... | collective-permute-start | bytes 49160 | tf_op jit(solution)/shard_map/ppermute | solution.py:529
  27.6 1.7 %slice.6 = bf16[120,64,128]{2,1,0:T(8,128)(2,1)S(1)} slice(bf16[144,64,128]{2,1,0:T(8,128)(2,1)} %param.26), slice={[0:120], [0:64], [0:128]} | slice | bytes 3932160 | tf_op jit(solution)/shard_map/slice | solution.py:625
  29.3 0.7 %collective-permute-done.refs_1_ = f32[64,64]{1,0:T(8,128)S(1)} collective-permute-done((f32[64,64]{1,0:T(8,128)S(1)}, f32[64,64]{1,0:T(8,128)S(1)}, u32[]{:S(2)}, u32[]{:S(2)}) %collective-permute-start) | collective-permute-done | bytes 16416 | tf_op jit(solution)/shard_map/ppermute | solution.py:529
  30.0 6.5 %all-to-all-done.1 = bf16[16,24,384]{2,1,0:T(8,128)(2,1)S(1)} async-done(((bf16[16,24,384]{2,1,0:T(8,128)(2,1)}), bf16[16,24,384]{2,1,0:T(8,128)(2,1)S(1)}, u32[]{:S(2)}, u32[]{:S(2)}) %all-to-all-start.1) | async-done | bytes 294944 | tf_op jit(solution)/shard_map/all_to_all | solution.py:522
  36.5 2.1 %mix.1 = bf16[128,640]{1,0:T(8,128)(2,1)} custom-call(f32[64,64]{1,0:T(8,128)S(1)} %get-tuple-element.14.refs_0_, f32[64,64]{1,0:T(8,128)S(1)} %collective-permute-done.refs_1_, bf16[384,384]{1,0:T(8,128)(2,1)S(1)} %bitcast.14, bf16[7680,128]{1,0:T(8,128)(2,1)S(1)} %bitcast.13, bf16[9216,128]{1,0:T(8,128)(2,1)} %bitcast.20), custom_call_target="tpu_custom_call" | custom-call | flops 18874368 | bytes 4816896 | tf_op jit(solution)/shard_map/mix/pallas_call | solution.py:507
  38.6 3.5 %all-to-all-start.2 = ((bf16[16,8,640]{2,1,0:T(8,128)(2,1)}), bf16[16,8,640]{2,1,0:T(8,128)(2,1)S(1)}, u32[]{:S(2)}, u32[]{:S(2)}) async-start(bf16[16,8,640]{2,1,0:T(8,128)(2,1)} %bitcast.7), calls=%async_computation.2 | async-start | bytes 327680 | tf_op jit(solution)/shard_map/all_to_all | solution.py:522
  42.1 1.6 %collective-permute-start.1 = (bf16[384,384]{1,0:T(8,128)(2,1)S(1)}, bf16[384,384]{1,0:T(8,128)(2,1)S(1)}, u32[]{:S(2)}, u32[]{:S(2)}) collective-permute-start(bf16[384,384]{1,0:T(8,128)(2,1)S(1)} %bitcast.15), channel_id=1, source_target_pairs={{0,16},{16,0},{1,17},{17,1},{2,18},{18,2},{3,19},{19,3},{4,20},{20... | collective-permute-start | bytes 884744 | tf_op jit(solution)/shard_map/ppermute | solution.py:529
  43.7 0.0 copy-done.8
  43.7 0.0 copy-done.10
  43.7 1.8 %fusion.5.turn_ref = bf16[256,384]{1,0:T(8,128)(2,1)S(1)} fusion(s32[256]{0:T(256)S(1)} %copy-done.10, s32[384]{0:T(512)S(1)} %copy-done.7, s32[256]{0:T(256)S(1)} %mul.70, s32[384]{0:T(512)S(1)} %copy-done.8, s32[384]{0:T(512)S(1)} %copy-done.6, s32[256]{0:T(256)S(1)} %copy-done.11), kind=kLoop, calls=%fused_computation.11 | loop fusion | flops 1966080 | bytes 204288 | tf_op jit(solution)/shard_map/convert_element_type | solution.py:81
  45.5 5.0 %all-to-all-done.2 = bf16[16,8,640]{2,1,0:T(8,128)(2,1)S(1)} async-done(((bf16[16,8,640]{2,1,0:T(8,128)(2,1)}), bf16[16,8,640]{2,1,0:T(8,128)(2,1)S(1)}, u32[]{:S(2)}, u32[]{:S(2)}) %all-to-all-start.2) | async-done | bytes 163872 | tf_op jit(solution)/shard_map/all_to_all | solution.py:522
  50.5 1.0 %adjoint.1 = bf16[128,512]{1,0:T(8,128)(2,1)} custom-call(bf16[256,384]{1,0:T(8,128)(2,1)S(1)} %fusion.5.turn_ref, bf16[128,640]{1,0:T(8,128)(2,1)S(1)} %bitcast.18), custom_call_target="tpu_custom_call" | custom-call | flops 37748736 | bytes 491520 | tf_op jit(solution)/shard_map/adjoint/pallas_call | solution.py:507
  51.5 3.5 %all-to-all-start.3 = ((bf16[16,8,512]{2,1,0:T(8,128)(2,1)}), bf16[16,8,512]{2,1,0:T(8,128)(2,1)S(1)}, u32[]{:S(2)}, u32[]{:S(2)}) async-start(bf16[16,8,512]{2,1,0:T(8,128)(2,1)} %bitcast.9), calls=%async_computation.3 | async-start | bytes 262144 | tf_op jit(solution)/shard_map/all_to_all | solution.py:522
  55.1 0.0 copy-start
  55.1 0.0 copy-start.1
  55.1 0.0 copy-start.3
  55.1 0.0 copy-start.4
  55.1 0.0 collective-permute-done.1.refs_1_
  55.1 5.3 %outer.1 = f32[3,48,64,128]{3,2,1,0:T(8,128)} custom-call(bf16[384,384]{1,0:T(8,128)(2,1)S(1)} %bitcast.16, bf16[384,384]{1,0:T(8,128)(2,1)S(1)} %collective-permute-done.1.refs_1_), custom_call_target="tpu_custom_call" | custom-call | flops 37748736 | bytes 5308416 | tf_op jit(solution)/shard_map/outer/pallas_call | solution.py:507
  60.5 2.5 %all-to-all-done.3 = bf16[16,8,512]{2,1,0:T(8,128)(2,1)S(1)} async-done(((bf16[16,8,512]{2,1,0:T(8,128)(2,1)}), bf16[16,8,512]{2,1,0:T(8,128)(2,1)S(1)}, u32[]{:S(2)}, u32[]{:S(2)}) %all-to-all-start.3) | async-done | bytes 131104 | tf_op jit(solution)/shard_map/all_to_all | solution.py:522
  63.0 1.8 %spatial.1 = (bf16[1,4,64,2048]{3,2,1,0:T(8,128)(2,1)}, f32[64,64]{1,0:T(8,128)}) custom-call(s32[1,32]{1,0:T(1,128)S(1)} %copy-done.4, bf16[128,512]{1,0:T(8,128)(2,1)S(1)} %bitcast.19, bf16[128,128]{1,0:T(8,128)(2,1)S(1)} %copy-done.1, bf16[64,128]{1,0:T(8,128)(2,1)S(1)} %copy-done.3, bf16[192,2048]{1,0:T(8,128)(2,1)S(1)} %copy-done, ...), custom_call_target="tpu_custom_call" | custom-call | flops 201326592 | bytes 3080320 | tf_op jit(solution)/shard_map/spatial/pallas_call | solution.py:507
  (9 shorter events, 0.0 us)
Async XLA Ops:
  0.6 11.9 %copy-start.5 = (s32[32,2]{1,0:T(8,128)S(1)}, s32[32,2]{1,0:T(8,128)}, u32[]{:S(2)}) copy-start(s32[32,2]{1,0:T(8,128)} %constant.73) | copy-start | bytes 772
  0.6 15.4 %copy-start.6 = (s32[384]{0:T(512)S(1)}, s32[384]{0:T(512)}, u32[]{:S(2)}) copy-start(s32[384]{0:T(512)} %constant.60.clone) | copy-start | bytes 4612
  0.7 15.4 %copy-start.7 = (s32[384]{0:T(512)S(1)}, s32[384]{0:T(512)}, u32[]{:S(2)}) copy-start(s32[384]{0:T(512)} %constant.58.clone) | copy-start | bytes 4612
  0.7 15.4 %copy-start.9 = (s32[384]{0:T(512)S(1)}, s32[384]{0:T(512)}, u32[]{:S(2)}) copy-start(s32[384]{0:T(512)} %constant.57.clone) | copy-start | bytes 4612
  0.7 15.4 %copy-start.12 = (s32[256]{0:T(256)S(1)}, s32[256]{0:T(256)}, u32[]{:S(2)}) copy-start(s32[256]{0:T(256)} %constant.72) | copy-start | bytes 3076
  0.7 15.4 %copy-start.13 = (s32[256]{0:T(256)S(1)}, s32[256]{0:T(256)}, u32[]{:S(2)}) copy-start(s32[256]{0:T(256)} %constant.61.clone) | copy-start | bytes 3076
  0.7 11.8 %copy-start.14 = (s32[1,32]{1,0:T(1,128)S(1)}, s32[1,32]{1,0:T(1,128)}, u32[]{:S(2)}) copy-start(s32[1,32]{1,0:T(1,128)} %param.27) | copy-start | bytes 388
  0.7 12.3 %copy-start.2 = (bf16[64,64]{1,0:T(8,128)(2,1)S(1)}, bf16[64,64]{1,0:T(8,128)(2,1)}, u32[]{:S(2)}) copy-start(bf16[64,64]{1,0:T(8,128)(2,1)} %w_ref.1) | copy-start | bytes 24580
  5.1 16.4 %all-to-all-start = ((bf16[16,8,768]{2,1,0:T(8,128)(2,1)}), bf16[16,8,768]{2,1,0:T(8,128)(2,1)S(1)}, u32[]{:S(2)}, u32[]{:S(2)}) async-start(bf16[16,8,768]{2,1,0:T(8,128)(2,1)} %bitcast.22), calls=%async_computation | async-start | bytes 393216 | tf_op jit(solution)/shard_map/all_to_all | solution.py:522
  22.5 14.1 %all-to-all-start.1 = ((bf16[16,24,384]{2,1,0:T(8,128)(2,1)}), bf16[16,24,384]{2,1,0:T(8,128)(2,1)S(1)}, u32[]{:S(2)}, u32[]{:S(2)}) async-start(bf16[16,24,384]{2,1,0:T(8,128)(2,1)} %bitcast.3), calls=%async_computation.1 | async-start | bytes 589824 | tf_op jit(solution)/shard_map/all_to_all | solution.py:522
  26.0 4.0 %collective-permute-start = (f32[64,64]{1,0:T(8,128)S(1)}, f32[64,64]{1,0:T(8,128)S(1)}, u32[]{:S(2)}, u32[]{:S(2)}) collective-permute-start(f32[64,64]{1,0:T(8,128)S(1)} %get-tuple-element.14.refs_0_), channel_id=1, source_target_pairs={{0,16},{16,0},{1,17},{17,1},{2,18},{18,2},{3,19},{19,3},{4,20},{20... | collective-permute-start | bytes 49160 | tf_op jit(solution)/shard_map/ppermute | solution.py:529
  36.5 7.2 %copy-start.8 = (s32[384]{0:T(512)S(1)}, s32[384]{0:T(512)}, u32[]{:S(2)}) copy-start(s32[384]{0:T(512)} %constant.62.clone) | copy-start | bytes 4612
  36.5 7.2 %copy-start.10 = (s32[256]{0:T(256)S(1)}, s32[256]{0:T(256)}, u32[]{:S(2)}) copy-start(s32[256]{0:T(256)} %constant.71) | copy-start | bytes 3076
  36.5 7.2 %copy-start.11 = (s32[256]{0:T(256)S(1)}, s32[256]{0:T(256)}, u32[]{:S(2)}) copy-start(s32[256]{0:T(256)} %constant.59.clone) | copy-start | bytes 3076
  38.6 11.9 %all-to-all-start.2 = ((bf16[16,8,640]{2,1,0:T(8,128)(2,1)}), bf16[16,8,640]{2,1,0:T(8,128)(2,1)S(1)}, u32[]{:S(2)}, u32[]{:S(2)}) async-start(bf16[16,8,640]{2,1,0:T(8,128)(2,1)} %bitcast.7), calls=%async_computation.2 | async-start | bytes 327680 | tf_op jit(solution)/shard_map/all_to_all | solution.py:522
  42.1 13.0 %collective-permute-start.1 = (bf16[384,384]{1,0:T(8,128)(2,1)S(1)}, bf16[384,384]{1,0:T(8,128)(2,1)S(1)}, u32[]{:S(2)}, u32[]{:S(2)}) collective-permute-start(bf16[384,384]{1,0:T(8,128)(2,1)S(1)} %bitcast.15), channel_id=1, source_target_pairs={{0,16},{16,0},{1,17},{17,1},{2,18},{18,2},{3,19},{19,3},{4,20},{20... | collective-permute-start | bytes 884744 | tf_op jit(solution)/shard_map/ppermute | solution.py:529
  51.5 11.4 %all-to-all-start.3 = ((bf16[16,8,512]{2,1,0:T(8,128)(2,1)}), bf16[16,8,512]{2,1,0:T(8,128)(2,1)S(1)}, u32[]{:S(2)}, u32[]{:S(2)}) async-start(bf16[16,8,512]{2,1,0:T(8,128)(2,1)} %bitcast.9), calls=%async_computation.3 | async-start | bytes 262144 | tf_op jit(solution)/shard_map/all_to_all | solution.py:522
  55.1 7.9 %copy-start = (bf16[192,2048]{1,0:T(8,128)(2,1)S(1)}, bf16[192,2048]{1,0:T(8,128)(2,1)}, u32[]{:S(2)}) copy-start(bf16[192,2048]{1,0:T(8,128)(2,1)} %constant.55.clone.tab_hbm.tab_ref) | copy-start | bytes 2359300
  55.1 7.9 %copy-start.1 = (bf16[128,128]{1,0:T(8,128)(2,1)S(1)}, bf16[128,128]{1,0:T(8,128)(2,1)}, u32[]{:S(2)}) copy-start(bf16[128,128]{1,0:T(8,128)(2,1)} %constant.64.clone.back_ref) | copy-start | bytes 98308
  55.1 7.9 %copy-start.3 = (bf16[64,128]{1,0:T(8,128)(2,1)S(1)}, bf16[64,128]{1,0:T(8,128)(2,1)}, u32[]{:S(2)}) copy-start(bf16[64,128]{1,0:T(8,128)(2,1)} %constant.65.clone.share_ref) | copy-start | bytes 49156
  55.1 7.8 %copy-start.4 = (s32[1,32]{1,0:T(1,128)S(1)}, s32[1,32]{1,0:T(1,128)}, u32[]{:S(2)}) copy-start(s32[1,32]{1,0:T(1,128)} %ext_hbm.3) | copy-start | bytes 388

commit v7 on v5

--- a/solution.py
+++ b/solution.py
@@ -116,9 +116,9 @@
 
 
 def column_kernel(
-    plan, ext_hbm, x_hbm, pre_hbm, cot_hbm, tab_hbm, spread_hbm, gp_hbm, out_ref,
-    ext_ref, x_ref, pre_ref, cot_ref, lines_ref, tab_ref, spread_ref, stage_ref, in_sems,
-    out_sems, misc_sems,
+    plan, ext_hbm, x_hbm, pre_hbm, cot_hbm, tab_hbm, spread_hbm, gp_hbm, out_hbm,
+    ext_ref, x_ref, pre_ref, cot_ref, lines_ref, tab_ref, spread_ref, stage_ref, out_ref, in_sems,
+    out_sems, misc_sems, sent_sems,
 ):
     chans, ranks = plan.channels, plan.ranks
     slots = plan.local_rows // SLAB
@@ -217,7 +217,17 @@
                             base : base + ranks
                         ]
     small.wait()
-    out_ref[...] = jnp.dot(spread_ref[...], stage_ref[...], preferred_element_type=F32).astype(BF16)
+    parts = sent_sems.shape[0]
+    each = stage_ref.shape[1] // parts
+    for n in range(parts):
+        cols = slice(n * each, (n + 1) * each)
+        out_ref[:, cols] = jnp.dot(
+            spread_ref[...], stage_ref[:, cols], preferred_element_type=F32
+        ).astype(BF16)
+        span = pl.ds(n * each, each)
+        copy = pltpu.make_async_copy(out_ref.at[:, span], out_hbm.at[:, span], sent_sems.at[n])
+        copy.start()
+        saves.append([copy])
     for copies in saves:
         for copy in copies:
             copy.wait()
@@ -240,11 +250,23 @@
     return high, (total - high).astype(BF16).astype(F32)
 
 
-def row_kernel(plan, turn_ref, in_ref, out_ref):
+def row_kernel(plan, turn_ref, in_ref, out_hbm, out_ref, sems):
     half = plan.half
     stacked = jnp.concatenate([in_ref[:, :half], in_ref[:, half:]], axis=0)
-    sums = jnp.dot(turn_ref[...], stacked, preferred_element_type=F32)
-    out_ref[...] = (sums * plan.scale).astype(BF16)
+    parts = sems.shape[0]
+    each = out_ref.shape[0] // parts
+    copies = []
+    for n in range(parts):
+        sums = jnp.dot(
+            turn_ref[n * each : (n + 1) * each], stacked, preferred_element_type=F32
+        )
+        out_ref[n * each : (n + 1) * each] = (sums * plan.scale).astype(BF16)
+        span = pl.ds(n * each, each)
+        copy = pltpu.make_async_copy(out_ref.at[span], out_hbm.at[span], sems.at[n])
+        copy.start()
+        copies.append(copy)
+    for copy in copies:
+        copy.wait()
 
 
 def out_pair(tile, chans):
@@ -426,7 +448,7 @@
     lax.fori_loop(0, owners, body, 0)
 
 
-def adjoint_kernel(plan, turn_ref, in_ref, out_ref):
+def adjoint_kernel(plan, turn_ref, in_ref, out_hbm, out_ref, sem):
     chans = plan.channels
     order = slot_order(plan)
     parts = []
@@ -453,6 +475,9 @@
     block = jnp.concatenate(pieces, axis=0)
     block = jnp.concatenate([block, jnp.zeros((8, plan.both - chans), F32)], axis=1)
     out_ref[:, plan.half :] = jnp.concatenate([block] * plan.ranks, axis=0).astype(BF16)
+    copy = pltpu.make_async_copy(out_ref, out_hbm, sem)
+    copy.start()
+    copy.wait()
 
 
 def spatial_kernel(
@@ -554,7 +579,7 @@
         2 * local_rows * 2 * chans * columns * 2 * MODES,
         62,
         in_specs=[hbm] * 6,
-        out_specs=(hbm, vmem),
+        out_specs=(hbm, hbm),
         scratch_shapes=[
             pltpu.SMEM(extents.shape, jnp.int32),
             pltpu.VMEM(stored, BF16),
@@ -564,9 +589,11 @@
             pltpu.VMEM(table.shape, BF16),
             pltpu.VMEM(spread.shape, BF16),
             pltpu.VMEM((plan.group * ranks, 2 * plan.half), BF16),
+            pltpu.VMEM((lines, wide), BF16),
             pltpu.SemaphoreType.DMA((slots, COLUMN_PARTS, 3)),
             pltpu.SemaphoreType.DMA((slots, SLAB)),
             pltpu.SemaphoreType.DMA((3,)),
+            pltpu.SemaphoreType.DMA((2 if plan.half % 128 == 0 else 1,)),
         ],
     )
     received = exchange(sent)
@@ -597,6 +624,12 @@
         "rows",
         2 * forward_turn.size * plan.half,
         16,
+        in_specs=[vmem] * 2,
+        out_specs=(hbm,),
+        scratch_shapes=[
+            pltpu.VMEM((mode_lines, plan.half), BF16),
+            pltpu.SemaphoreType.DMA((2,)),
+        ],
     )[0]
     modes = exchange(sent)
 
@@ -655,6 +688,12 @@
         "adjoint",
         2 * backward_turn.size * plan.pairs * chans,
         16,
+        in_specs=[vmem] * 2,
+        out_specs=(hbm,),
+        scratch_shapes=[
+            pltpu.VMEM((lines, plan.half + plan.both), BF16),
+            pltpu.SemaphoreType.DMA,
+        ],
     )[0]
     local_back = exchange(sent)
 

time: 65.6 us -> 65.1 us (level)
  no operation moved by 1% of the time
where the time goes in v7:
time: 65.1 us; the launch traced here: 64.6 us
  starting transfers between devices  21.1 us (32%)
  waiting for transfers between devices  18.5 us (28%)
  Pallas kernels  18.1 us (28%)
  other arithmetic  3.78 us (6%)
  local copies, waits for them, and re-layouts  2.12 us (3%)
  between operations  0.94 us (1%)
    pallas_call x7, Pallas kernels, call(): pl.pallas_call(body, out_shape=outs, name=name, cost_estimate=pl.CostEsti...  18.1 us
    all_to_all x4, starting transfers between devices, exchange(): lax.all_to_all(value, 'rows', split_axis=0, concat_axis=0, tiled=True)  18 us
    all_to_all x4, waiting for transfers between devices, exchange(): lax.all_to_all(value, 'rows', split_axis=0, concat_axis=0, tiled=True)  17.8 us
    convert_element_type x2, other arithmetic, turn_table(): return jnp.where(mo == ro, value, 0.0).astype(BF16)  3.71 us
    ppermute x2, starting transfers between devices, every_sample(): return [value, lax.ppermute(value, 'batch', [(0, 1), (1, 0)])]  3.11 us
    slice x1, local copies, waits for them, and re-layouts, shards(): flat[:head]  1.7 us
  transfers between devices with their start and end apart: 6, of which 5 were waited for; matrix products, arithmetic and copies ran while one was open for 9% of the time, Pallas kernels for 14%

profile of v7, /device:TPU:0, one launch (start us, length us, event | category | flops | bytes accessed | tf_op | source)
XLA Modules:
  0.0 64.6 jit_solution(13131794720942756189)
XLA Ops:
  0.6 0.0 copy-start.6
  0.6 0.0 copy-start.7
  0.7 0.0 copy-start.8
  0.7 0.0 copy-start.10
  0.7 0.0 copy-start.13
  0.7 0.0 copy-start.14
  0.7 0.0 copy-start.15
  0.7 3.9 %columns.1 = (bf16[256,2048]{1,0:T(8,128)(2,1)}, bf16[128,768]{1,0:T(8,128)(2,1)}) custom-call(s32[1,32]{1,0:T(1,128)} %ext_hbm.3, bf16[1,4,64,2048]{3,2,1,0:T(8,128)(2,1)} %x_ref.1, bf16[1,4,64,2048]{3,2,1,0:T(8,128)(2,1)} %pre_hbm.1, bf16[1,4,64,2048]{3,2,1,0:T(8,128)(2,1)} %cot_hbm.1, bf16[192,2048]{1,0:T(8,128)(2,1)} %constant.55.clone.tab_hbm.tab_ref, ...), custom_call_target="tpu_custom_call" | custom-call | flops 402653184 | bytes 5210240 | tf_op jit(solution)/shard_map/columns/pallas_call | solution.py:531
  4.7 7.4 %all-to-all-start = ((bf16[16,8,768]{2,1,0:T(8,128)(2,1)}), bf16[16,8,768]{2,1,0:T(8,128)(2,1)S(1)}, u32[]{:S(2)}, u32[]{:S(2)}) async-start(bf16[16,8,768]{2,1,0:T(8,128)(2,1)} %bitcast.22), calls=%async_computation | async-start | bytes 393216 | tf_op jit(solution)/shard_map/all_to_all | solution.py:546
  12.1 0.0 copy-done.15
  12.1 0.0 copy-done.6
  12.1 0.1 broadcast_add_fusion
  12.2 0.1 reshape.42
  12.3 0.1 transpose.16
  12.4 0.1 mul.70
  12.5 2.8 %weights.1.refs_0_ = f32[64,64]{1,0:T(8,128)S(1)} custom-call(bf16[1,4,64,2048]{3,2,1,0:T(8,128)(2,1)} %x_ref.1, bf16[256,2048]{1,0:T(8,128)(2,1)} %get-tuple-element.10.gp_ref), custom_call_target="tpu_custom_call" | custom-call | flops 67108864 | bytes 2113536 | tf_op jit(solution)/shard_map/weights/pallas_call | solution.py:531
  15.3 0.0 copy-done.7
  15.3 0.0 copy-done.8
  15.4 0.0 copy-done.10
  15.4 1.9 %fusion.11.turn_ref = bf16[384,256]{1,0:T(8,128)(2,1)S(1)} fusion(s32[256]{0:T(256)S(1)} %copy-done.13, s32[384]{0:T(512)S(1)} %copy-done.8, s32[256]{0:T(256)S(1)} %mul.70, s32[384]{0:T(512)S(1)} %copy-done.10, s32[256]{0:T(256)S(1)} %copy-done.14, s32[384]{0:T(512)S(1)} %copy-done.7), kind=kLoop, calls=%fused_computation.17 | loop fusion | flops 1966080 | bytes 204288 | tf_op jit(solution)/shard_map/convert_element_type | solution.py:81
  17.3 3.8 %all-to-all-done = bf16[16,8,768]{2,1,0:T(8,128)(2,1)S(1)} async-done(((bf16[16,8,768]{2,1,0:T(8,128)(2,1)}), bf16[16,8,768]{2,1,0:T(8,128)(2,1)S(1)}, u32[]{:S(2)}, u32[]{:S(2)}) %all-to-all-start) | async-done | bytes 196640 | tf_op jit(solution)/shard_map/all_to_all | solution.py:546
  21.0 0.9 %rows.1 = bf16[384,384]{1,0:T(8,128)(2,1)} custom-call(bf16[384,256]{1,0:T(8,128)(2,1)S(1)} %fusion.11.turn_ref, bf16[128,768]{1,0:T(8,128)(2,1)S(1)} %bitcast.17), custom_call_target="tpu_custom_call" | custom-call | flops 75497472 | bytes 688128 | tf_op jit(solution)/shard_map/rows/pallas_call | solution.py:531
  22.0 3.5 %all-to-all-start.1 = ((bf16[16,24,384]{2,1,0:T(8,128)(2,1)}), bf16[16,24,384]{2,1,0:T(8,128)(2,1)S(1)}, u32[]{:S(2)}, u32[]{:S(2)}) async-start(bf16[16,24,384]{2,1,0:T(8,128)(2,1)} %bitcast.3), calls=%async_computation.1 | async-start | bytes 589824 | tf_op jit(solution)/shard_map/all_to_all | solution.py:546
  25.6 1.6 %collective-permute-start = (f32[64,64]{1,0:T(8,128)S(1)}, f32[64,64]{1,0:T(8,128)S(1)}, u32[]{:S(2)}, u32[]{:S(2)}) collective-permute-start(f32[64,64]{1,0:T(8,128)S(1)} %weights.1.refs_0_), channel_id=1, source_target_pairs={{0,16},{16,0},{1,17},{17,1},{2,18},{18,2},{3,19},{19,3},{4,20},{20... | collective-permute-start | bytes 49160 | tf_op jit(solution)/shard_map/ppermute | solution.py:553
  27.1 1.7 %slice.6 = bf16[120,64,128]{2,1,0:T(8,128)(2,1)S(1)} slice(bf16[144,64,128]{2,1,0:T(8,128)(2,1)} %param.26), slice={[0:120], [0:64], [0:128]} | slice | bytes 3932160 | tf_op jit(solution)/shard_map/slice | solution.py:653
  28.8 0.7 %collective-permute-done.refs_1_ = f32[64,64]{1,0:T(8,128)S(1)} collective-permute-done((f32[64,64]{1,0:T(8,128)S(1)}, f32[64,64]{1,0:T(8,128)S(1)}, u32[]{:S(2)}, u32[]{:S(2)}) %collective-permute-start) | collective-permute-done | bytes 16416 | tf_op jit(solution)/shard_map/ppermute | solution.py:553
  29.5 6.5 %all-to-all-done.1 = bf16[16,24,384]{2,1,0:T(8,128)(2,1)S(1)} async-done(((bf16[16,24,384]{2,1,0:T(8,128)(2,1)}), bf16[16,24,384]{2,1,0:T(8,128)(2,1)S(1)}, u32[]{:S(2)}, u32[]{:S(2)}) %all-to-all-start.1) | async-done | bytes 294944 | tf_op jit(solution)/shard_map/all_to_all | solution.py:546
  36.1 2.1 %mix.1 = bf16[128,640]{1,0:T(8,128)(2,1)} custom-call(f32[64,64]{1,0:T(8,128)S(1)} %weights.1.refs_0_, f32[64,64]{1,0:T(8,128)S(1)} %collective-permute-done.refs_1_, bf16[384,384]{1,0:T(8,128)(2,1)S(1)} %bitcast.14, bf16[7680,128]{1,0:T(8,128)(2,1)S(1)} %bitcast.13, bf16[9216,128]{1,0:T(8,128)(2,1)} %bitcast.20), custom_call_target="tpu_custom_call" | custom-call | flops 18874368 | bytes 4816896 | tf_op jit(solution)/shard_map/mix/pallas_call | solution.py:531
  38.1 3.5 %all-to-all-start.2 = ((bf16[16,8,640]{2,1,0:T(8,128)(2,1)}), bf16[16,8,640]{2,1,0:T(8,128)(2,1)S(1)}, u32[]{:S(2)}, u32[]{:S(2)}) async-start(bf16[16,8,640]{2,1,0:T(8,128)(2,1)} %bitcast.7), calls=%async_computation.2 | async-start | bytes 327680 | tf_op jit(solution)/shard_map/all_to_all | solution.py:546
  41.7 1.6 %collective-permute-start.1 = (bf16[384,384]{1,0:T(8,128)(2,1)S(1)}, bf16[384,384]{1,0:T(8,128)(2,1)S(1)}, u32[]{:S(2)}, u32[]{:S(2)}) collective-permute-start(bf16[384,384]{1,0:T(8,128)(2,1)S(1)} %bitcast.15), channel_id=1, source_target_pairs={{0,16},{16,0},{1,17},{17,1},{2,18},{18,2},{3,19},{19,3},{4,20},{20... | collective-permute-start | bytes 884744 | tf_op jit(solution)/shard_map/ppermute | solution.py:553
  43.2 0.0 copy-done.9
  43.2 1.8 %fusion.5.turn_ref = bf16[256,384]{1,0:T(8,128)(2,1)S(1)} fusion(s32[256]{0:T(256)S(1)} %copy-done.11, s32[384]{0:T(512)S(1)} %copy-done.8, s32[256]{0:T(256)S(1)} %mul.70, s32[384]{0:T(512)S(1)} %copy-done.9, s32[384]{0:T(512)S(1)} %copy-done.7, s32[256]{0:T(256)S(1)} %copy-done.12), kind=kLoop, calls=%fused_computation.11 | loop fusion | flops 1966080 | bytes 204288 | tf_op jit(solution)/shard_map/convert_element_type | solution.py:81
  45.1 5.0 %all-to-all-done.2 = bf16[16,8,640]{2,1,0:T(8,128)(2,1)S(1)} async-done(((bf16[16,8,640]{2,1,0:T(8,128)(2,1)}), bf16[16,8,640]{2,1,0:T(8,128)(2,1)S(1)}, u32[]{:S(2)}, u32[]{:S(2)}) %all-to-all-start.2) | async-done | bytes 163872 | tf_op jit(solution)/shard_map/all_to_all | solution.py:546
  50.1 1.0 %adjoint.1 = bf16[128,512]{1,0:T(8,128)(2,1)} custom-call(bf16[256,384]{1,0:T(8,128)(2,1)S(1)} %fusion.5.turn_ref, bf16[128,640]{1,0:T(8,128)(2,1)S(1)} %bitcast.18), custom_call_target="tpu_custom_call" | custom-call | flops 37748736 | bytes 491520 | tf_op jit(solution)/shard_map/adjoint/pallas_call | solution.py:531
  51.1 3.5 %all-to-all-start.3 = ((bf16[16,8,512]{2,1,0:T(8,128)(2,1)}), bf16[16,8,512]{2,1,0:T(8,128)(2,1)S(1)}, u32[]{:S(2)}, u32[]{:S(2)}) async-start(bf16[16,8,512]{2,1,0:T(8,128)(2,1)} %bitcast.9), calls=%async_computation.3 | async-start | bytes 262144 | tf_op jit(solution)/shard_map/all_to_all | solution.py:546
  54.6 0.0 copy-start
  54.6 0.0 copy-start.1
  54.6 0.0 copy-start.2
  54.7 0.0 copy-start.3
  54.7 0.0 copy-start.4
  54.7 0.0 copy-start.5
  54.7 0.0 collective-permute-done.1.refs_1_
  54.7 5.3 %outer.1 = f32[3,48,64,128]{3,2,1,0:T(8,128)} custom-call(bf16[384,384]{1,0:T(8,128)(2,1)S(1)} %bitcast.16, bf16[384,384]{1,0:T(8,128)(2,1)S(1)} %collective-permute-done.1.refs_1_), custom_call_target="tpu_custom_call" | custom-call | flops 37748736 | bytes 5308416 | tf_op jit(solution)/shard_map/outer/pallas_call | solution.py:531
  60.0 2.5 %all-to-all-done.3 = bf16[16,8,512]{2,1,0:T(8,128)(2,1)S(1)} async-done(((bf16[16,8,512]{2,1,0:T(8,128)(2,1)}), bf16[16,8,512]{2,1,0:T(8,128)(2,1)S(1)}, u32[]{:S(2)}, u32[]{:S(2)}) %all-to-all-start.3) | async-done | bytes 131104 | tf_op jit(solution)/shard_map/all_to_all | solution.py:546
  62.5 0.0 copy-done.3
  62.5 0.0 copy-done.4
  62.5 0.0 copy-done.5
  62.5 2.0 %spatial.1 = (bf16[1,4,64,2048]{3,2,1,0:T(8,128)(2,1)}, f32[64,64]{1,0:T(8,128)}) custom-call(s32[1,32]{1,0:T(1,128)S(1)} %copy-done.5, bf16[128,512]{1,0:T(8,128)(2,1)S(1)} %bitcast.19, bf16[128,128]{1,0:T(8,128)(2,1)S(1)} %copy-done.2, bf16[64,128]{1,0:T(8,128)(2,1)S(1)} %copy-done.4, bf16[64,64]{1,0:T(8,128)(2,1)S(1)} %copy-done.3, ...), custom_call_target="tpu_custom_call" | custom-call | flops 268435456 | bytes 3088512 | tf_op jit(solution)/shard_map/spatial/pallas_call | solution.py:531
  (11 shorter events, 0.0 us)
Async XLA Ops:
  0.6 11.5 %copy-start.6 = (s32[32,2]{1,0:T(8,128)S(1)}, s32[32,2]{1,0:T(8,128)}, u32[]{:S(2)}) copy-start(s32[32,2]{1,0:T(8,128)} %constant.73) | copy-start | bytes 772
  0.6 14.7 %copy-start.7 = (s32[384]{0:T(512)S(1)}, s32[384]{0:T(512)}, u32[]{:S(2)}) copy-start(s32[384]{0:T(512)} %constant.60.clone) | copy-start | bytes 4612
  0.7 14.7 %copy-start.8 = (s32[384]{0:T(512)S(1)}, s32[384]{0:T(512)}, u32[]{:S(2)}) copy-start(s32[384]{0:T(512)} %constant.58.clone) | copy-start | bytes 4612
  0.7 14.7 %copy-start.10 = (s32[384]{0:T(512)S(1)}, s32[384]{0:T(512)}, u32[]{:S(2)}) copy-start(s32[384]{0:T(512)} %constant.57.clone) | copy-start | bytes 4612
  0.7 14.7 %copy-start.13 = (s32[256]{0:T(256)S(1)}, s32[256]{0:T(256)}, u32[]{:S(2)}) copy-start(s32[256]{0:T(256)} %constant.72) | copy-start | bytes 3076
  0.7 14.7 %copy-start.14 = (s32[256]{0:T(256)S(1)}, s32[256]{0:T(256)}, u32[]{:S(2)}) copy-start(s32[256]{0:T(256)} %constant.61.clone) | copy-start | bytes 3076
  0.7 11.4 %copy-start.15 = (s32[1,32]{1,0:T(1,128)S(1)}, s32[1,32]{1,0:T(1,128)}, u32[]{:S(2)}) copy-start(s32[1,32]{1,0:T(1,128)} %param.27) | copy-start | bytes 388
  4.7 16.4 %all-to-all-start = ((bf16[16,8,768]{2,1,0:T(8,128)(2,1)}), bf16[16,8,768]{2,1,0:T(8,128)(2,1)S(1)}, u32[]{:S(2)}, u32[]{:S(2)}) async-start(bf16[16,8,768]{2,1,0:T(8,128)(2,1)} %bitcast.22), calls=%async_computation | async-start | bytes 393216 | tf_op jit(solution)/shard_map/all_to_all | solution.py:546
  22.0 14.1 %all-to-all-start.1 = ((bf16[16,24,384]{2,1,0:T(8,128)(2,1)}), bf16[16,24,384]{2,1,0:T(8,128)(2,1)S(1)}, u32[]{:S(2)}, u32[]{:S(2)}) async-start(bf16[16,24,384]{2,1,0:T(8,128)(2,1)} %bitcast.3), calls=%async_computation.1 | async-start | bytes 589824 | tf_op jit(solution)/shard_map/all_to_all | solution.py:546
  25.6 4.0 %collective-permute-start = (f32[64,64]{1,0:T(8,128)S(1)}, f32[64,64]{1,0:T(8,128)S(1)}, u32[]{:S(2)}, u32[]{:S(2)}) collective-permute-start(f32[64,64]{1,0:T(8,128)S(1)} %weights.1.refs_0_), channel_id=1, source_target_pairs={{0,16},{16,0},{1,17},{17,1},{2,18},{18,2},{3,19},{19,3},{4,20},{20... | collective-permute-start | bytes 49160 | tf_op jit(solution)/shard_map/ppermute | solution.py:553
  36.1 7.2 %copy-start.9 = (s32[384]{0:T(512)S(1)}, s32[384]{0:T(512)}, u32[]{:S(2)}) copy-start(s32[384]{0:T(512)} %constant.62.clone) | copy-start | bytes 4612
  36.1 7.2 %copy-start.11 = (s32[256]{0:T(256)S(1)}, s32[256]{0:T(256)}, u32[]{:S(2)}) copy-start(s32[256]{0:T(256)} %constant.71) | copy-start | bytes 3076
  36.1 7.2 %copy-start.12 = (s32[256]{0:T(256)S(1)}, s32[256]{0:T(256)}, u32[]{:S(2)}) copy-start(s32[256]{0:T(256)} %constant.59.clone) | copy-start | bytes 3076
  38.1 11.9 %all-to-all-start.2 = ((bf16[16,8,640]{2,1,0:T(8,128)(2,1)}), bf16[16,8,640]{2,1,0:T(8,128)(2,1)S(1)}, u32[]{:S(2)}, u32[]{:S(2)}) async-start(bf16[16,8,640]{2,1,0:T(8,128)(2,1)} %bitcast.7), calls=%async_computation.2 | async-start | bytes 327680 | tf_op jit(solution)/shard_map/all_to_all | solution.py:546
  41.7 13.0 %collective-permute-start.1 = (bf16[384,384]{1,0:T(8,128)(2,1)S(1)}, bf16[384,384]{1,0:T(8,128)(2,1)S(1)}, u32[]{:S(2)}, u32[]{:S(2)}) collective-permute-start(bf16[384,384]{1,0:T(8,128)(2,1)S(1)} %bitcast.15), channel_id=1, source_target_pairs={{0,16},{16,0},{1,17},{17,1},{2,18},{18,2},{3,19},{19,3},{4,20},{20... | collective-permute-start | bytes 884744 | tf_op jit(solution)/shard_map/ppermute | solution.py:553
  51.1 11.4 %all-to-all-start.3 = ((bf16[16,8,512]{2,1,0:T(8,128)(2,1)}), bf16[16,8,512]{2,1,0:T(8,128)(2,1)S(1)}, u32[]{:S(2)}, u32[]{:S(2)}) async-start(bf16[16,8,512]{2,1,0:T(8,128)(2,1)} %bitcast.9), calls=%async_computation.3 | async-start | bytes 262144 | tf_op jit(solution)/shard_map/all_to_all | solution.py:546
  54.6 7.9 %copy-start = (bf16[256,2048]{1,0:T(8,128)(2,1)S(1)}, bf16[256,2048]{1,0:T(8,128)(2,1)}, u32[]{:S(2)}) copy-start(bf16[256,2048]{1,0:T(8,128)(2,1)} %get-tuple-element.10.gp_ref) | copy-start | bytes 3145732
  54.6 7.9 %copy-start.1 = (bf16[192,2048]{1,0:T(8,128)(2,1)S(1)}, bf16[192,2048]{1,0:T(8,128)(2,1)}, u32[]{:S(2)}) copy-start(bf16[192,2048]{1,0:T(8,128)(2,1)} %constant.55.clone.tab_hbm.tab_ref) | copy-start | bytes 2359300
  54.6 7.9 %copy-start.2 = (bf16[128,128]{1,0:T(8,128)(2,1)S(1)}, bf16[128,128]{1,0:T(8,128)(2,1)}, u32[]{:S(2)}) copy-start(bf16[128,128]{1,0:T(8,128)(2,1)} %constant.64.clone.back_ref) | copy-start | bytes 98308
  54.7 7.8 %copy-start.3 = (bf16[64,64]{1,0:T(8,128)(2,1)S(1)}, bf16[64,64]{1,0:T(8,128)(2,1)}, u32[]{:S(2)}) copy-start(bf16[64,64]{1,0:T(8,128)(2,1)} %w_ref.1) | copy-start | bytes 24580
  54.7 7.8 %copy-start.4 = (bf16[64,128]{1,0:T(8,128)(2,1)S(1)}, bf16[64,128]{1,0:T(8,128)(2,1)}, u32[]{:S(2)}) copy-start(bf16[64,128]{1,0:T(8,128)(2,1)} %constant.65.clone.share_ref) | copy-start | bytes 49156
  54.7 7.8 %copy-start.5 = (s32[1,32]{1,0:T(1,128)S(1)}, s32[1,32]{1,0:T(1,128)}, u32[]{:S(2)}) copy-start(s32[1,32]{1,0:T(1,128)} %ext_hbm.3) | copy-start | bytes 388

commit v8 on v7

--- a/solution.py
+++ b/solution.py
@@ -233,8 +233,9 @@
             copy.wait()
 
 
-def weight_kernel(x_ref, gp_ref, out_ref):
+def weight_kernel(w_ref, x_ref, gp_ref, out_ref, direct_ref):
     part = lax.dot_general(x_ref[0, 0], gp_ref[...], NT, preferred_element_type=F32)
+    direct_ref[...] = jnp.dot(w_ref[...], gp_ref[...], preferred_element_type=F32).astype(BF16)
 
     @pl.when(pl.program_id(0) == 0)
     def _():
@@ -481,7 +482,7 @@
 
 
 def spatial_kernel(
-    plan, step, weight_scale, ext_hbm, in_ref, back_ref, share_ref, w_ref, tab_ref, gp_ref,
+    plan, step, weight_scale, ext_hbm, in_ref, back_ref, share_ref, tab_ref, direct_ref,
     out_hbm, gw_hbm, ext_ref, left_ref, out_ref, gw_ref, sems, ext_sem, gw_sem,
 ):
     chans, rows = plan.channels, plan.local_rows
@@ -509,8 +510,8 @@
             live = mask_rows(ext_ref[0, first + slot], n * step, step, chans)
             for row in range(slot * SLAB, (slot + 1) * SLAB):
                 lines = slice(row * chans, (row + 1) * chans)
-                direct = jnp.dot(w_ref[...], gp_ref[lines, cols], preferred_element_type=F32)
-                out_ref[row, :, cols] = (spatial[lines] + direct).astype(BF16) * live
+                value = spatial[lines] + direct_ref[lines, cols].astype(F32)
+                out_ref[row, :, cols] = value.astype(BF16) * live
         copy = pltpu.make_async_copy(
             out_ref.at[:, :, pl.ds(n * step, step)],
             out_hbm.at[0, :, :, pl.ds(n * step, step)],
@@ -597,20 +598,24 @@
         ],
     )
     received = exchange(sent)
-    local_weight = call(
+    local_weight, direct = call(
         weight_kernel,
-        (stay(layer_input), stay(grad_pre)),
-        (sds((chans, chans), F32),),
+        (weight, stay(layer_input), stay(grad_pre)),
+        (sds((chans, chans), F32), sds(grad_pre.shape, BF16)),
         "weights",
-        2 * layer_input.size * chans,
+        4 * layer_input.size * chans,
         16,
         grid=(local_rows,),
         in_specs=[
+            pl.BlockSpec((chans, chans), lambda r: (0, 0)),
             pl.BlockSpec((1, 1, chans, columns), lambda r: (0, r, 0, 0)),
             pl.BlockSpec((chans, columns), lambda r: (r, 0)),
         ],
-        out_specs=(pl.BlockSpec((chans, chans), lambda r: (0, 0)),),
-    )[0]
+        out_specs=(
+            pl.BlockSpec((chans, chans), lambda r: (0, 0)),
+            pl.BlockSpec((chans, columns), lambda r: (r, 0)),
+        ),
+    )
     received, local_weight = lax.optimization_barrier((received, local_weight))
     shares = every_sample(local_weight, samples)
     if samples > 2:
@@ -701,12 +706,12 @@
     gather_back, share_in = jnp.asarray(plan.gather_back()), jnp.asarray(plan.share_in())
     grad_input, grad_weight = call(
         functools.partial(spatial_kernel, plan, step, weight_scale),
-        (extents, local_back, gather_back, share_in, weight, table, grad_pre),
+        (extents, local_back, gather_back, share_in, table, direct),
         (sds(layer_input.shape, BF16), sds((chans, chans), F32)),
         "spatial",
-        2 * local_rows * chans * columns * (table.shape[0] + chans),
+        2 * local_rows * chans * columns * table.shape[0],
         16,
-        in_specs=[hbm] + [vmem] * 6,
+        in_specs=[hbm] + [vmem] * 5,
         out_specs=(hbm, hbm),
         scratch_shapes=[
             pltpu.SMEM(extents.shape, jnp.int32),

time: 65.1 us -> 64.9 us (level)
  transfers between devices with their start and end apart: 6 -> 6, of which waited for: 5 -> 5; matrix products, arithmetic and copies ran while one was open for 9% -> 9% of each run, Pallas kernels for 14% -> 15%
where the time goes in v8:
time: 64.9 us; the launch traced here: 64.3 us
  starting transfers between devices  21.1 us (33%)
  waiting for transfers between devices  18.3 us (28%)
  Pallas kernels  18.1 us (28%)
  other arithmetic  3.78 us (6%)
  local copies, waits for them, and re-layouts  2.12 us (3%)
  between operations  0.92 us (1%)
    pallas_call x7, Pallas kernels, call(): pl.pallas_call(body, out_shape=outs, name=name, cost_estimate=pl.CostEsti...  18.1 us
    all_to_all x4, starting transfers between devices, exchange(): lax.all_to_all(value, 'rows', split_axis=0, concat_axis=0, tiled=True)  18 us
    all_to_all x4, waiting for transfers between devices, exchange(): lax.all_to_all(value, 'rows', split_axis=0, concat_axis=0, tiled=True)  17.6 us
    convert_element_type x2, other arithmetic, turn_table(): return jnp.where(mo == ro, value, 0.0).astype(BF16)  3.71 us
    ppermute x2, starting transfers between devices, every_sample(): return [value, lax.ppermute(value, 'batch', [(0, 1), (1, 0)])]  3.11 us
    slice x1, local copies, waits for them, and re-layouts, shards(): flat[:head]  1.7 us
  transfers between devices with their start and end apart: 6, of which 5 were waited for; matrix products, arithmetic and copies ran while one was open for 9% of the time, Pallas kernels for 15%

profile of v8, /device:TPU:0, one launch (start us, length us, event | category | flops | bytes accessed | tf_op | source)
XLA Modules:
  0.0 64.3 jit_solution(16831756407539867877)
XLA Ops:
  0.6 0.0 copy-start.5
  0.6 0.0 copy-start.6
  0.7 0.0 copy-start.7
  0.7 0.0 copy-start.9
  0.7 0.0 copy-start.12
  0.7 0.0 copy-start.13
  0.7 0.0 copy-start.14
  0.7 0.0 copy-start.2
  0.7 3.9 %columns.1 = (bf16[256,2048]{1,0:T(8,128)(2,1)}, bf16[128,768]{1,0:T(8,128)(2,1)}) custom-call(s32[1,32]{1,0:T(1,128)} %ext_hbm.3, bf16[1,4,64,2048]{3,2,1,0:T(8,128)(2,1)} %x_ref.1, bf16[1,4,64,2048]{3,2,1,0:T(8,128)(2,1)} %pre_hbm.1, bf16[1,4,64,2048]{3,2,1,0:T(8,128)(2,1)} %cot_hbm.1, bf16[192,2048]{1,0:T(8,128)(2,1)} %constant.55.clone.tab_hbm.tab_ref, ...), custom_call_target="tpu_custom_call" | custom-call | flops 402653184 | bytes 5210240 | tf_op jit(solution)/shard_map/columns/pallas_call | solution.py:532
  4.7 7.4 %all-to-all-start = ((bf16[16,8,768]{2,1,0:T(8,128)(2,1)}), bf16[16,8,768]{2,1,0:T(8,128)(2,1)S(1)}, u32[]{:S(2)}, u32[]{:S(2)}) async-start(bf16[16,8,768]{2,1,0:T(8,128)(2,1)} %bitcast.22), calls=%async_computation | async-start | bytes 393216 | tf_op jit(solution)/shard_map/all_to_all | solution.py:547
  12.1 0.0 copy-done.14
  12.1 0.0 copy-done.5
  12.1 0.1 broadcast_add_fusion
  12.2 0.1 reshape.42
  12.3 0.1 transpose.16
  12.4 0.1 mul.70
  12.5 0.0 copy-done.2
  12.6 3.0 %weights.1 = (f32[64,64]{1,0:T(8,128)S(1)}, bf16[256,2048]{1,0:T(8,128)(2,1)S(1)}) custom-call(bf16[64,64]{1,0:T(8,128)(2,1)S(1)} %copy-done.2, bf16[1,4,64,2048]{3,2,1,0:T(8,128)(2,1)} %x_ref.1, bf16[256,2048]{1,0:T(8,128)(2,1)} %get-tuple-element.12.gp_ref), custom_call_target="tpu_custom_call" | custom-call | flops 134217728 | bytes 3170304 | tf_op jit(solution)/shard_map/weights/pallas_call | solution.py:532
  15.6 0.0 copy-done.6
  15.6 0.0 copy-done.7
  15.6 0.0 copy-done.9
  15.6 0.0 copy-done.12
  15.6 1.9 %fusion.11.turn_ref = bf16[384,256]{1,0:T(8,128)(2,1)S(1)} fusion(s32[256]{0:T(256)S(1)} %copy-done.12, s32[384]{0:T(512)S(1)} %copy-done.7, s32[256]{0:T(256)S(1)} %mul.70, s32[384]{0:T(512)S(1)} %copy-done.9, s32[256]{0:T(256)S(1)} %copy-done.13, s32[384]{0:T(512)S(1)} %copy-done.6), kind=kLoop, calls=%fused_computation.17 | loop fusion | flops 1966080 | bytes 204288 | tf_op jit(solution)/shard_map/convert_element_type | solution.py:81
  17.5 3.5 %all-to-all-done = bf16[16,8,768]{2,1,0:T(8,128)(2,1)S(1)} async-done(((bf16[16,8,768]{2,1,0:T(8,128)(2,1)}), bf16[16,8,768]{2,1,0:T(8,128)(2,1)S(1)}, u32[]{:S(2)}, u32[]{:S(2)}) %all-to-all-start) | async-done | bytes 196640 | tf_op jit(solution)/shard_map/all_to_all | solution.py:547
  21.1 0.9 %rows.1 = bf16[384,384]{1,0:T(8,128)(2,1)} custom-call(bf16[384,256]{1,0:T(8,128)(2,1)S(1)} %fusion.11.turn_ref, bf16[128,768]{1,0:T(8,128)(2,1)S(1)} %bitcast.17), custom_call_target="tpu_custom_call" | custom-call | flops 75497472 | bytes 688128 | tf_op jit(solution)/shard_map/rows/pallas_call | solution.py:532
  22.0 3.5 %all-to-all-start.1 = ((bf16[16,24,384]{2,1,0:T(8,128)(2,1)}), bf16[16,24,384]{2,1,0:T(8,128)(2,1)S(1)}, u32[]{:S(2)}, u32[]{:S(2)}) async-start(bf16[16,24,384]{2,1,0:T(8,128)(2,1)} %bitcast.3), calls=%async_computation.1 | async-start | bytes 589824 | tf_op jit(solution)/shard_map/all_to_all | solution.py:547
  25.6 1.6 %collective-permute-start = (f32[64,64]{1,0:T(8,128)S(1)}, f32[64,64]{1,0:T(8,128)S(1)}, u32[]{:S(2)}, u32[]{:S(2)}) collective-permute-start(f32[64,64]{1,0:T(8,128)S(1)} %get-tuple-element.14.refs_0_), channel_id=1, source_target_pairs={{0,16},{16,0},{1,17},{17,1},{2,18},{18,2},{3,19},{19,3},{4,20},{20... | collective-permute-start | bytes 49160 | tf_op jit(solution)/shard_map/ppermute | solution.py:554
  27.1 1.7 %slice.6 = bf16[120,64,128]{2,1,0:T(8,128)(2,1)S(1)} slice(bf16[144,64,128]{2,1,0:T(8,128)(2,1)} %param.26), slice={[0:120], [0:64], [0:128]} | slice | bytes 3932160 | tf_op jit(solution)/shard_map/slice | solution.py:658
  28.8 0.7 %collective-permute-done.refs_1_ = f32[64,64]{1,0:T(8,128)S(1)} collective-permute-done((f32[64,64]{1,0:T(8,128)S(1)}, f32[64,64]{1,0:T(8,128)S(1)}, u32[]{:S(2)}, u32[]{:S(2)}) %collective-permute-start) | collective-permute-done | bytes 16416 | tf_op jit(solution)/shard_map/ppermute | solution.py:554
  29.5 6.5 %all-to-all-done.1 = bf16[16,24,384]{2,1,0:T(8,128)(2,1)S(1)} async-done(((bf16[16,24,384]{2,1,0:T(8,128)(2,1)}), bf16[16,24,384]{2,1,0:T(8,128)(2,1)S(1)}, u32[]{:S(2)}, u32[]{:S(2)}) %all-to-all-start.1) | async-done | bytes 294944 | tf_op jit(solution)/shard_map/all_to_all | solution.py:547
  36.1 2.1 %mix.1 = bf16[128,640]{1,0:T(8,128)(2,1)} custom-call(f32[64,64]{1,0:T(8,128)S(1)} %get-tuple-element.14.refs_0_, f32[64,64]{1,0:T(8,128)S(1)} %collective-permute-done.refs_1_, bf16[384,384]{1,0:T(8,128)(2,1)S(1)} %bitcast.14, bf16[7680,128]{1,0:T(8,128)(2,1)S(1)} %bitcast.13, bf16[9216,128]{1,0:T(8,128)(2,1)} %bitcast.20), custom_call_target="tpu_custom_call" | custom-call | flops 18874368 | bytes 4816896 | tf_op jit(solution)/shard_map/mix/pallas_call | solution.py:532
  38.2 3.5 %all-to-all-start.2 = ((bf16[16,8,640]{2,1,0:T(8,128)(2,1)}), bf16[16,8,640]{2,1,0:T(8,128)(2,1)S(1)}, u32[]{:S(2)}, u32[]{:S(2)}) async-start(bf16[16,8,640]{2,1,0:T(8,128)(2,1)} %bitcast.7), calls=%async_computation.2 | async-start | bytes 327680 | tf_op jit(solution)/shard_map/all_to_all | solution.py:547
  41.7 1.6 %collective-permute-start.1 = (bf16[384,384]{1,0:T(8,128)(2,1)S(1)}, bf16[384,384]{1,0:T(8,128)(2,1)S(1)}, u32[]{:S(2)}, u32[]{:S(2)}) collective-permute-start(bf16[384,384]{1,0:T(8,128)(2,1)S(1)} %bitcast.15), channel_id=1, source_target_pairs={{0,16},{16,0},{1,17},{17,1},{2,18},{18,2},{3,19},{19,3},{4,20},{20... | collective-permute-start | bytes 884744 | tf_op jit(solution)/shard_map/ppermute | solution.py:554
  43.3 0.0 copy-done.8
  43.3 1.8 %fusion.5.turn_ref = bf16[256,384]{1,0:T(8,128)(2,1)S(1)} fusion(s32[256]{0:T(256)S(1)} %copy-done.10, s32[384]{0:T(512)S(1)} %copy-done.7, s32[256]{0:T(256)S(1)} %mul.70, s32[384]{0:T(512)S(1)} %copy-done.8, s32[384]{0:T(512)S(1)} %copy-done.6, s32[256]{0:T(256)S(1)} %copy-done.11), kind=kLoop, calls=%fused_computation.11 | loop fusion | flops 1966080 | bytes 204288 | tf_op jit(solution)/shard_map/convert_element_type | solution.py:81
  45.1 5.0 %all-to-all-done.2 = bf16[16,8,640]{2,1,0:T(8,128)(2,1)S(1)} async-done(((bf16[16,8,640]{2,1,0:T(8,128)(2,1)}), bf16[16,8,640]{2,1,0:T(8,128)(2,1)S(1)}, u32[]{:S(2)}, u32[]{:S(2)}) %all-to-all-start.2) | async-done | bytes 163872 | tf_op jit(solution)/shard_map/all_to_all | solution.py:547
  50.1 1.0 %adjoint.1 = bf16[128,512]{1,0:T(8,128)(2,1)} custom-call(bf16[256,384]{1,0:T(8,128)(2,1)S(1)} %fusion.5.turn_ref, bf16[128,640]{1,0:T(8,128)(2,1)S(1)} %bitcast.18), custom_call_target="tpu_custom_call" | custom-call | flops 37748736 | bytes 491520 | tf_op jit(solution)/shard_map/adjoint/pallas_call | solution.py:532
  51.1 3.5 %all-to-all-start.3 = ((bf16[16,8,512]{2,1,0:T(8,128)(2,1)}), bf16[16,8,512]{2,1,0:T(8,128)(2,1)S(1)}, u32[]{:S(2)}, u32[]{:S(2)}) async-start(bf16[16,8,512]{2,1,0:T(8,128)(2,1)} %bitcast.9), calls=%async_computation.3 | async-start | bytes 262144 | tf_op jit(solution)/shard_map/all_to_all | solution.py:547
  54.6 0.0 copy-start
  54.7 0.0 copy-start.1
  54.7 0.0 copy-start.3
  54.7 0.0 copy-start.4
  54.7 0.0 collective-permute-done.1.refs_1_
  54.7 5.3 %outer.1 = f32[3,48,64,128]{3,2,1,0:T(8,128)} custom-call(bf16[384,384]{1,0:T(8,128)(2,1)S(1)} %bitcast.16, bf16[384,384]{1,0:T(8,128)(2,1)S(1)} %collective-permute-done.1.refs_1_), custom_call_target="tpu_custom_call" | custom-call | flops 37748736 | bytes 5308416 | tf_op jit(solution)/shard_map/outer/pallas_call | solution.py:532
  60.0 2.5 %all-to-all-done.3 = bf16[16,8,512]{2,1,0:T(8,128)(2,1)S(1)} async-done(((bf16[16,8,512]{2,1,0:T(8,128)(2,1)}), bf16[16,8,512]{2,1,0:T(8,128)(2,1)S(1)}, u32[]{:S(2)}, u32[]{:S(2)}) %all-to-all-start.3) | async-done | bytes 131104 | tf_op jit(solution)/shard_map/all_to_all | solution.py:547
  62.5 0.0 copy-done.3
  62.5 0.0 copy-done.4
  62.5 1.8 %spatial.1 = (bf16[1,4,64,2048]{3,2,1,0:T(8,128)(2,1)}, f32[64,64]{1,0:T(8,128)}) custom-call(s32[1,32]{1,0:T(1,128)S(1)} %copy-done.4, bf16[128,512]{1,0:T(8,128)(2,1)S(1)} %bitcast.19, bf16[128,128]{1,0:T(8,128)(2,1)S(1)} %copy-done.1, bf16[64,128]{1,0:T(8,128)(2,1)S(1)} %copy-done.3, bf16[192,2048]{1,0:T(8,128)(2,1)S(1)} %copy-done, ...), custom_call_target="tpu_custom_call" | custom-call | flops 201326592 | bytes 3080320 | tf_op jit(solution)/shard_map/spatial/pallas_call | solution.py:532
  (9 shorter events, 0.0 us)
Async XLA Ops:
  0.6 11.5 %copy-start.5 = (s32[32,2]{1,0:T(8,128)S(1)}, s32[32,2]{1,0:T(8,128)}, u32[]{:S(2)}) copy-start(s32[32,2]{1,0:T(8,128)} %constant.73) | copy-start | bytes 772
  0.6 14.9 %copy-start.6 = (s32[384]{0:T(512)S(1)}, s32[384]{0:T(512)}, u32[]{:S(2)}) copy-start(s32[384]{0:T(512)} %constant.60.clone) | copy-start | bytes 4612
  0.7 14.9 %copy-start.7 = (s32[384]{0:T(512)S(1)}, s32[384]{0:T(512)}, u32[]{:S(2)}) copy-start(s32[384]{0:T(512)} %constant.58.clone) | copy-start | bytes 4612
  0.7 14.9 %copy-start.9 = (s32[384]{0:T(512)S(1)}, s32[384]{0:T(512)}, u32[]{:S(2)}) copy-start(s32[384]{0:T(512)} %constant.57.clone) | copy-start | bytes 4612
  0.7 14.9 %copy-start.12 = (s32[256]{0:T(256)S(1)}, s32[256]{0:T(256)}, u32[]{:S(2)}) copy-start(s32[256]{0:T(256)} %constant.72) | copy-start | bytes 3076
  0.7 14.9 %copy-start.13 = (s32[256]{0:T(256)S(1)}, s32[256]{0:T(256)}, u32[]{:S(2)}) copy-start(s32[256]{0:T(256)} %constant.61.clone) | copy-start | bytes 3076
  0.7 11.4 %copy-start.14 = (s32[1,32]{1,0:T(1,128)S(1)}, s32[1,32]{1,0:T(1,128)}, u32[]{:S(2)}) copy-start(s32[1,32]{1,0:T(1,128)} %param.27) | copy-start | bytes 388
  0.7 11.8 %copy-start.2 = (bf16[64,64]{1,0:T(8,128)(2,1)S(1)}, bf16[64,64]{1,0:T(8,128)(2,1)}, u32[]{:S(2)}) copy-start(bf16[64,64]{1,0:T(8,128)(2,1)} %w_ref.1) | copy-start | bytes 24580
  4.7 16.4 %all-to-all-start = ((bf16[16,8,768]{2,1,0:T(8,128)(2,1)}), bf16[16,8,768]{2,1,0:T(8,128)(2,1)S(1)}, u32[]{:S(2)}, u32[]{:S(2)}) async-start(bf16[16,8,768]{2,1,0:T(8,128)(2,1)} %bitcast.22), calls=%async_computation | async-start | bytes 393216 | tf_op jit(solution)/shard_map/all_to_all | solution.py:547
  22.0 14.1 %all-to-all-start.1 = ((bf16[16,24,384]{2,1,0:T(8,128)(2,1)}), bf16[16,24,384]{2,1,0:T(8,128)(2,1)S(1)}, u32[]{:S(2)}, u32[]{:S(2)}) async-start(bf16[16,24,384]{2,1,0:T(8,128)(2,1)} %bitcast.3), calls=%async_computation.1 | async-start | bytes 589824 | tf_op jit(solution)/shard_map/all_to_all | solution.py:547
  25.6 4.0 %collective-permute-start = (f32[64,64]{1,0:T(8,128)S(1)}, f32[64,64]{1,0:T(8,128)S(1)}, u32[]{:S(2)}, u32[]{:S(2)}) collective-permute-start(f32[64,64]{1,0:T(8,128)S(1)} %get-tuple-element.14.refs_0_), channel_id=1, source_target_pairs={{0,16},{16,0},{1,17},{17,1},{2,18},{18,2},{3,19},{19,3},{4,20},{20... | collective-permute-start | bytes 49160 | tf_op jit(solution)/shard_map/ppermute | solution.py:554
  36.1 7.2 %copy-start.8 = (s32[384]{0:T(512)S(1)}, s32[384]{0:T(512)}, u32[]{:S(2)}) copy-start(s32[384]{0:T(512)} %constant.62.clone) | copy-start | bytes 4612
  36.1 7.2 %copy-start.10 = (s32[256]{0:T(256)S(1)}, s32[256]{0:T(256)}, u32[]{:S(2)}) copy-start(s32[256]{0:T(256)} %constant.71) | copy-start | bytes 3076
  36.1 7.2 %copy-start.11 = (s32[256]{0:T(256)S(1)}, s32[256]{0:T(256)}, u32[]{:S(2)}) copy-start(s32[256]{0:T(256)} %constant.59.clone) | copy-start | bytes 3076
  38.2 11.9 %all-to-all-start.2 = ((bf16[16,8,640]{2,1,0:T(8,128)(2,1)}), bf16[16,8,640]{2,1,0:T(8,128)(2,1)S(1)}, u32[]{:S(2)}, u32[]{:S(2)}) async-start(bf16[16,8,640]{2,1,0:T(8,128)(2,1)} %bitcast.7), calls=%async_computation.2 | async-start | bytes 327680 | tf_op jit(solution)/shard_map/all_to_all | solution.py:547
  41.7 13.0 %collective-permute-start.1 = (bf16[384,384]{1,0:T(8,128)(2,1)S(1)}, bf16[384,384]{1,0:T(8,128)(2,1)S(1)}, u32[]{:S(2)}, u32[]{:S(2)}) collective-permute-start(bf16[384,384]{1,0:T(8,128)(2,1)S(1)} %bitcast.15), channel_id=1, source_target_pairs={{0,16},{16,0},{1,17},{17,1},{2,18},{18,2},{3,19},{19,3},{4,20},{20... | collective-permute-start | bytes 884744 | tf_op jit(solution)/shard_map/ppermute | solution.py:554
  51.1 11.4 %all-to-all-start.3 = ((bf16[16,8,512]{2,1,0:T(8,128)(2,1)}), bf16[16,8,512]{2,1,0:T(8,128)(2,1)S(1)}, u32[]{:S(2)}, u32[]{:S(2)}) async-start(bf16[16,8,512]{2,1,0:T(8,128)(2,1)} %bitcast.9), calls=%async_computation.3 | async-start | bytes 262144 | tf_op jit(solution)/shard_map/all_to_all | solution.py:547
  54.6 7.9 %copy-start = (bf16[192,2048]{1,0:T(8,128)(2,1)S(1)}, bf16[192,2048]{1,0:T(8,128)(2,1)}, u32[]{:S(2)}) copy-start(bf16[192,2048]{1,0:T(8,128)(2,1)} %constant.55.clone.tab_hbm.tab_ref) | copy-start | bytes 2359300
  54.7 7.9 %copy-start.1 = (bf16[128,128]{1,0:T(8,128)(2,1)S(1)}, bf16[128,128]{1,0:T(8,128)(2,1)}, u32[]{:S(2)}) copy-start(bf16[128,128]{1,0:T(8,128)(2,1)} %constant.64.clone.back_ref) | copy-start | bytes 98308
  54.7 7.9 %copy-start.3 = (bf16[64,128]{1,0:T(8,128)(2,1)S(1)}, bf16[64,128]{1,0:T(8,128)(2,1)}, u32[]{:S(2)}) copy-start(bf16[64,128]{1,0:T(8,128)(2,1)} %constant.65.clone.share_ref) | copy-start | bytes 49156
  54.7 7.8 %copy-start.4 = (s32[1,32]{1,0:T(1,128)S(1)}, s32[1,32]{1,0:T(1,128)}, u32[]{:S(2)}) copy-start(s32[1,32]{1,0:T(1,128)} %ext_hbm.3) | copy-start | bytes 388
